TPU v7x, 32 devices: a whole 2x2x4 slice. The times are simulated.
32 devices in a mesh: gx: 8 (over z, x), gy: 4 (over y, core).
Axes of the slice: x: 2, y: 2, z: 4, core: 2. Of those that a mesh axis runs over, the one named last changes fastest.
Arguments:
- velocity: float32 [3, 64, 256, 128], P(None, 'gx', 'gy'), may hold values from -2 to 3, as said below
- counts: int32 [8, 4, 9], P('gx', 'gy'), may hold values from 1 to 1024, as said below
- src_cell: int32 [8, 4, 9, 1024], P('gx', 'gy'), may hold values from 0 to 65535
- weights: float32 [8, 4, 9, 1024], P('gx', 'gy'), may hold values from 0.05 to 0.35
- dst_cell: int32 [8, 4, 9, 1024], P('gx', 'gy'), may hold values from 0 to 65535
- blade_tile: int32 [20, 192], replicated, may hold values from 0 to 31, as said below
- blade_cell: int32 [20, 192], replicated, may hold values from 0 to 65535
- blade_coef: float32 [20, 192], replicated, may hold values from 0.5 to 2
Outputs:
- updated: float32 [3, 64, 256, 128], P(None, 'gx', 'gy')
- forcing: float32 [3, 64, 256, 128], P(None, 'gx', 'gy')
Inputs may be any that keep to these rules, and one draw needn't show every extreme that they name: The velocity components, streamwise with a mean near 1. `counts`: some list is full, with 1024 used slots. `blade_tile`: turbines stand near one spanwise row of tiles; a turbine's points lie in at most three tiles.
All inputs are finite; a program needn't handle non-finite values.
Results may differ from a plain program's by a relative error of at most 0.00002.
Values sent between devices are 32-bit elements; how exact they have to be, the bound alone decides.
No kernel may reach another device: no remote copies, remote signals or barrier semaphores. Data moves between devices by JAX's collectives and lax.ppermute only.
A program may use at most 256 MiB of HBM per device.

v0:
```python
import jax
import jax.numpy as jnp
from jax import lax
from jax.sharding import PartitionSpec as P


def padded_2(cells, sides, width):
    for axis, dim in sides:
        count = lax.axis_size(axis)
        head = lax.slice_in_dim(cells, 0, width, axis=dim)
        tail = lax.slice_in_dim(cells, cells.shape[dim] - width, cells.shape[dim], axis=dim)
        cells = jnp.concatenate(
            [
                lax.ppermute(tail, axis, [(i, (i + 1) % count) for i in range(count)]),
                cells,
                lax.ppermute(head, axis, [((i + 1) % count, i) for i in range(count)]),
            ],
            axis=dim,
        )
    return cells


def body(velocity, counts, src_cell, weights, dst_cell, blade_tile, blade_cell, blade_coef):
    components = velocity.shape[0]
    cells_x = velocity.shape[1]
    cells_y = velocity.shape[2]
    levels = velocity.shape[3]
    total_cells = cells_x * cells_y * levels
    flat_vel = velocity.reshape(components, total_cells)
    count_y = lax.axis_size("gy")
    index_x = lax.axis_index("gx")
    index_y = lax.axis_index("gy")
    my_tile = index_x * count_y + index_y
    sampled = jnp.take(flat_vel, blade_cell, axis=1)
    owned = (blade_tile == my_tile)[None]
    sampled = jnp.where(owned, sampled, jnp.zeros_like(sampled))
    points = blade_cell.shape[1]
    points_x = lax.psum(sampled[0], ("gx", "gy"))
    rotor_mean = jnp.sum(points_x, axis=1) / points
    forces = -blade_coef[None] * rotor_mean[None, :, None] * sampled
    forcing = (
        jnp.zeros((components, total_cells), jnp.float32)
        .at[:, blade_cell.reshape(-1)]
        .add(forces.reshape(components, -1))
    )
    capacity = src_cell.shape[-1]
    active = lax.broadcasted_iota(jnp.int32, (9, capacity), 1) < counts[0, 0][:, None]
    masked_w = jnp.where(active, weights[0, 0], jnp.zeros_like(weights[0, 0]))
    picked = jnp.take(flat_vel, src_cell[0, 0].reshape(-1), axis=1).reshape(components, 9, capacity)
    blocks = jnp.concatenate([picked * masked_w[None], masked_w[None]], axis=0)
    grid_blocks = blocks.reshape(4, 3, 3, capacity)
    bordered = padded_2(grid_blocks, (("gx", 1), ("gy", 2)), 1)
    arrived = bordered[:, ::-2, ::-2].reshape(4, 9, capacity)
    targets = dst_cell[0, 0].reshape(-1)
    totals = jnp.zeros((4, total_cells), jnp.float32).at[:, targets].add(arrived.reshape(4, -1))
    corrected = (1.0 - totals[3]) * flat_vel - totals[:3]
    field_now = corrected.reshape(components, cells_x, cells_y, levels)
    padded = padded_2(field_now, (("gx", 1), ("gy", 2)), 1)
    padded = jnp.pad(padded, ((0, 0), (0, 0), (0, 0), (1, 1)))
    center = padded[:, 1:-1, 1:-1, 1:-1]
    east_side = padded[:, 2:, 1:-1, 1:-1]
    west_side = padded[:, :-2, 1:-1, 1:-1]
    north_side = padded[:, 1:-1, 2:, 1:-1]
    south_side = padded[:, 1:-1, :-2, 1:-1]
    upper_side = padded[:, 1:-1, 1:-1, 2:]
    lower_side = padded[:, 1:-1, 1:-1, :-2]
    laplace = (
        east_side + west_side + north_side + south_side + upper_side + lower_side - 6.0 * center
    )
    advection = (
        center[0:1] * (east_side - west_side) * 0.5
        + center[1:2] * (north_side - south_side) * 0.5
        + center[2:3] * (upper_side - lower_side) * 0.5
    )
    forcing_field = forcing.reshape(components, cells_x, cells_y, levels)
    updated = center + 0.2 * (0.15 * laplace - advection + forcing_field)
    return (updated, forcing_field)


def solution(mesh):
    placed = (
        P(None, "gx", "gy", None),
        P("gx", "gy", None),
        P("gx", "gy", None, None),
        P("gx", "gy", None, None),
        P("gx", "gy", None, None),
        P(),
        P(),
        P(),
    )
    return jax.shard_map(
        body,
        mesh=mesh,
        in_specs=placed,
        out_specs=(P(None, "gx", "gy", None), P(None, "gx", "gy", None)),
        check_vma=False,
    )
```

profile of v0, /device:TPU:0, one launch (start us, length us, event | category | flops | bytes accessed | tf_op | source)
XLA Modules:
  0.0 388.8 jit_solution(10842976870287354699)
XLA Ops:
  0.6 0.0 copy-start.2
  0.6 17.6 %copy.47 = f32[3,8,64,128]{0,3,2,1:T(8,128)} copy(f32[3,8,64,128]{3,2,1,0:T(8,128)} %param.8) | data formatting | bytes 1572864 | tf_op args[0]
  18.2 0.0 copy-start.7
  18.2 0.0 copy-start.3
  18.2 0.0 copy-start.4
  18.2 0.0 copy-start.1
  18.2 0.0 copy-done.2
  18.3 41.5 %gather_fusion = f32[9216,3]{1,0:T(8,128)} fusion(f32[3,65536]{0,1:T(8,128)} %bitcast.38, s32[9216]{0:T(1024)S(1)} %broadcast_clamp_fusion), kind=kCustom, calls=%fused_computation | custom fusion | bytes 258048 | tf_op jit(solution)/shard_map/jit(_take)/gather | solution.py:49
  59.8 0.0 copy-start.6
  59.8 3.1 copy.48
  62.9 0.1 reduce
  63.0 0.5 broadcast.151
  63.5 0.0 copy-done.7
  63.5 0.7 reduce.15
  64.2 0.1 lt.84
  64.2 0.0 copy-done.3
  64.2 0.1 reduce.2
  64.4 0.1 fusion.15
  64.5 0.1 compare_select_fusion.2
  64.6 0.1 select_multiply_fusion
  64.7 3.0 collective-permute-start
  67.7 3.1 collective-permute-start.1
  70.8 0.0 copy-done.4
  70.9 0.0 copy-done.1
  70.9 0.1 reshape.205
  71.0 16.8 %gather_fusion.1 = f32[3840,3]{1,0:T(8,128)S(1)} fusion(f32[3,65536]{0,1:T(8,128)} %bitcast.39, s32[4096]{0:T(1024)S(1)} %pad_clamp_fusion), kind=kCustom, calls=%fused_computation.1 | custom fusion | bytes 107520 | tf_op jit(solution)/shard_map/jit(_take)/gather | solution.py:34
  87.8 0.9 copy.56
  88.7 0.0 copy-done.6
  88.7 38.2 %psum.7 = f32[20,192]{1,0:T(8,128)S(1)} all-reduce(f32[20,192]{1,0:T(8,128)S(1)} %fusion.17), channel_id=1, replica_groups=mesh['gx'=8,'gy'=4] {'gx','gy'}, use_global_device_ids=true, to_apply=%region_1.2 | all-reduce | flops 3840 | bytes 30720 | tf_op jit(solution)/shard_map/psum | solution.py:38
  126.9 0.1 reduce_sum.9
  127.1 0.0 collective-permute-done
  127.1 0.0 collective-permute-done.1
  127.1 0.1 pad_maximum_fusion.12
  127.2 0.1 collective-permute-start.2
  127.2 1.7 collective-permute-start.3
  129.0 0.0 copy-done.5
  129.0 0.1 negate_multiply_fusion
  129.0 0.1 broadcast_in_dim.75
  129.1 0.1 broadcast_in_dim.77
  129.2 0.1 reshape.193
  129.3 0.1 mul.117
  129.4 1.7 collective-permute-done.2
  131.1 0.7 collective-permute-done.3
  131.8 0.1 pad_maximum_fusion.8
  132.0 3.0 copy.49
  134.9 62.9 %scatter_custom_fusion = f32[4,65536]{0,1:T(8,128)} fusion(s32[9216]{0:T(1024)S(1)} %bitcast.52, f32[9216,4]{1,0:T(8,128)} %copy.49, f32[]{:T(128)} %constant.18.clone.1), kind=kCustom, calls=%fused_computation.12 | custom fusion | flops 36864 | bytes 1049088 | tf_op jit(solution)/shard_map/scatter-add | solution.py:55
  197.8 20.3 %fusion = f32[65536]{0:T(1024)S(1)} fusion(f32[4,65536]{0,1:T(8,128)} %scatter_custom_fusion), kind=kLoop, calls=%fused_computation.9 | loop fusion | flops 65536 | bytes 524288 | tf_op jit(solution)/shard_map/sub | solution.py:56
  218.1 34.2 %slice_subtract_fusion = f32[3,65536]{0,1:T(8,128)} fusion(f32[4,65536]{0,1:T(8,128)} %scatter_custom_fusion, f32[65536]{0:T(1024)S(1)} %fusion, f32[3,8,64,128]{0,3,2,1:T(8,128)} %copy.47), kind=kLoop, calls=%fused_computation.7 | loop fusion | flops 393216 | bytes 2621440 | tf_op jit(solution)/shard_map/sub | solution.py:56
  252.4 19.5 %copy.59 = f32[3,8,64,128]{3,2,1,0:T(8,128)S(1)} copy(f32[3,8,64,128]{0,3,2,1:T(8,128)} %bitcast.37) | data formatting | bytes 1572864 | tf_op jit(solution)/shard_map/reshape | solution.py:57
  271.9 3.3 collective-permute-start.4
  275.1 0.0 collective-permute-start.5
  275.2 37.5 %scatter_custom_fusion.1 = f32[3,65536]{0,1:T(8,128)} fusion(s32[3840]{0:T(1024)S(1)} %fusion.18, f32[]{:T(128)} %constant.18.clone.1, f32[3840,3]{1,0:T(8,128)S(1)} %gather_fusion.1, f32[]{:T(128)} %constant.22.clone.1, f32[3840]{0:T(1024)S(1)} %mul.117, pred[3840]{0:T(1024)(128)(4,1)S(1)} %broadcast_in_dim.77, pred[3840]{0:T(1024)(128)(4,1)S(1)} %broadcast_in_dim.75), kind=kCustom, calls=%fused_computation.10 | custom fusion | flops 46080 | bytes 2778624 | tf_op jit(solution)/shard_map/scatter-add | solution.py:44
  312.6 19.5 %copy.58 = f32[3,8,64,128]{3,2,1,0:T(8,128)S(1)} copy(f32[3,8,64,128]{0,3,2,1:T(8,128)} %bitcast.40) | data formatting | bytes 1572864 | tf_op jit(solution)/shard_map/reshape | solution.py:75
  332.1 0.0 copy-start
  332.1 0.0 collective-permute-done.4
  332.1 0.0 collective-permute-done.5
  332.2 1.5 collective-permute-start.6
  333.7 0.0 collective-permute-start.7
  333.7 52.5 %slice_reduce_fusion.2 = (f32[65536]{0:T(1024)S(1)}, f32[65536]{0:T(1024)S(1)}, f32[65536]{0:T(1024)S(1)}) fusion(f32[3,65536]{0,1:T(8,128)} %slice_subtract_fusion), kind=kLoop, calls=%fused_computation.6 | loop fusion | bytes 1572864 | tf_op jit(solution)/shard_map/slice | solution.py:71
  386.2 0.0 collective-permute-done.6
  386.2 0.0 collective-permute-done.7
  386.2 0.8 select_maximum_fusion
  387.0 0.0 copy-done
  387.0 1.8 multiply_add_fusion
  (18 shorter events, 0.4 us)
Async XLA Ops:
  0.6 17.6 %copy-start.2 = (s32[1,1,9,1024]{3,1,2,0:T(1,128)S(1)}, s32[1,1,9,1024]{3,1,2,0:T(1,128)}, u32[]{:S(2)}) copy-start(s32[1,1,9,1024]{3,1,2,0:T(1,128)} %param.10) | copy-start | bytes 110596
  18.2 45.3 %copy-start.7 = (s32[1,1,9]{2,1,0:T(1,128)S(1)}, s32[1,1,9]{2,1,0:T(1,128)}, u32[]{:S(2)}) copy-start(s32[1,1,9]{2,1,0:T(1,128)} %param.9) | copy-start | bytes 112
  18.2 46.0 %copy-start.3 = (f32[1,1,9,1024]{3,1,2,0:T(1,128)S(1)}, f32[1,1,9,1024]{3,1,2,0:T(1,128)}, u32[]{:S(2)}) copy-start(f32[1,1,9,1024]{3,1,2,0:T(1,128)} %param.11) | copy-start | bytes 110596
  18.2 52.6 %copy-start.4 = (s32[1,1,9,1024]{3,1,2,0:T(1,128)S(1)}, s32[1,1,9,1024]{3,1,2,0:T(1,128)}, u32[]{:S(2)}) copy-start(s32[1,1,9,1024]{3,1,2,0:T(1,128)} %param.12) | copy-start | bytes 110596
  18.2 52.7 %copy-start.1 = (s32[20,192]{1,0:T(8,128)S(1)}, s32[20,192]{1,0:T(8,128)}, u32[]{:S(2)}) copy-start(s32[20,192]{1,0:T(8,128)} %param.14) | copy-start | bytes 46084
  59.8 28.9 %copy-start.6 = (s32[20,192]{1,0:T(8,128)S(1)}, s32[20,192]{1,0:T(8,128)}, u32[]{:S(2)}) copy-start(s32[20,192]{1,0:T(8,128)} %param.13) | copy-start | bytes 46084
  59.8 69.2 %copy-start.5 = (f32[20,192]{1,0:T(8,128)S(1)}, f32[20,192]{1,0:T(8,128)}, u32[]{:S(2)}) copy-start(f32[20,192]{1,0:T(8,128)} %param.15) | copy-start | bytes 46084
  64.7 62.3 %collective-permute-start = (f32[4,1,3,1024]{3,0,2,1:T(4,128)S(1)}, f32[4,1,3,1024]{3,0,2,1:T(4,128)S(1)}, u32[]{:S(2)}, u32[]{:S(2)}) collective-permute-start(f32[4,1,3,1024]{3,0,2,1:T(4,128)S(1)} %get-tuple-element.19), channel_id=1, source_target_pairs={{0,4},{4,8},{8,12},{12,16},{16,20},{20,24},{24,28},{28,0},{1,5},{5... | collective-permute-start | bytes 147464 | tf_op jit(solution)/shard_map/ppermute | solution.py:14
  67.7 59.3 %collective-permute-start.1 = (f32[4,1,3,1024]{3,0,2,1:T(4,128)S(1)}, f32[4,1,3,1024]{3,0,2,1:T(4,128)S(1)}, u32[]{:S(2)}, u32[]{:S(2)}) collective-permute-start(f32[4,1,3,1024]{3,0,2,1:T(4,128)S(1)} %get-tuple-element.20), channel_id=1, source_target_pairs={{4,0},{8,4},{12,8},{16,12},{20,16},{24,20},{28,24},{0,28},{5,1},{9... | collective-permute-start | bytes 147464 | tf_op jit(solution)/shard_map/ppermute | solution.py:16
  127.2 3.9 %collective-permute-start.2 = (f32[4,5,1,1024]{3,0,2,1:T(4,128)S(1)}, f32[4,5,1,1024]{3,0,2,1:T(4,128)S(1)}, u32[]{:S(2)}, u32[]{:S(2)}) collective-permute-start(f32[4,5,1,1024]{3,0,2,1:T(4,128)S(1)} %get-tuple-element.17), channel_id=1, source_target_pairs={{0,1},{1,2},{2,3},{3,0},{4,5},{5,6},{6,7},{7,4},{8,9},{9,10},{10,1... | collective-permute-start | bytes 245768 | tf_op jit(solution)/shard_map/ppermute | solution.py:14
  127.2 4.6 %collective-permute-start.3 = (f32[4,5,1,1024]{3,0,2,1:T(4,128)S(1)}, f32[4,5,1,1024]{3,0,2,1:T(4,128)S(1)}, u32[]{:S(2)}, u32[]{:S(2)}) collective-permute-start(f32[4,5,1,1024]{3,0,2,1:T(4,128)S(1)} %get-tuple-element.18), channel_id=1, source_target_pairs={{1,0},{2,1},{3,2},{0,3},{5,4},{6,5},{7,6},{4,7},{9,8},{10,9},{11,1... | collective-permute-start | bytes 245768 | tf_op jit(solution)/shard_map/ppermute | solution.py:16
  271.9 60.2 %collective-permute-start.4 = (f32[3,1,64,128]{3,2,1,0:T(8,128)S(1)}, f32[3,1,64,128]{3,2,1,0:T(8,128)S(1)}, u32[]{:S(2)}, u32[]{:S(2)}) collective-permute-start(f32[3,1,64,128]{3,2,1,0:T(8,128)S(1)} %get-tuple-element.16), channel_id=1, source_target_pairs={{4,0},{8,4},{12,8},{16,12},{20,16},{24,20},{28,24},{0,28},{5,1},{9... | collective-permute-start | bytes 294920 | tf_op jit(solution)/shard_map/ppermute | solution.py:16
  275.1 57.0 %collective-permute-start.5 = (f32[3,1,64,128]{3,2,1,0:T(8,128)S(1)}, f32[3,1,64,128]{3,2,1,0:T(8,128)S(1)}, u32[]{:S(2)}, u32[]{:S(2)}) collective-permute-start(f32[3,1,64,128]{3,2,1,0:T(8,128)S(1)} %get-tuple-element.15), channel_id=1, source_target_pairs={{0,4},{4,8},{8,12},{12,16},{16,20},{20,24},{24,28},{28,0},{1,5},{5... | collective-permute-start | bytes 294920 | tf_op jit(solution)/shard_map/ppermute | solution.py:14
  332.1 54.9 %copy-start = (f32[3,8,64,128]{3,2,1,0:T(8,128)}, f32[3,8,64,128]{3,2,1,0:T(8,128)S(1)}, u32[]{:S(2)}) copy-start(f32[3,8,64,128]{3,2,1,0:T(8,128)S(1)} %copy.58) | copy-start | bytes 2359300
  332.2 54.0 %collective-permute-start.6 = (f32[3,10,1,128]{3,2,1,0:T(1,128)S(1)}, f32[3,10,1,128]{3,2,1,0:T(1,128)S(1)}, u32[]{:S(2)}, u32[]{:S(2)}) collective-permute-start(f32[3,10,1,128]{3,2,1,0:T(1,128)S(1)} %get-tuple-element.14), channel_id=1, source_target_pairs={{1,0},{2,1},{3,2},{0,3},{5,4},{6,5},{7,6},{4,7},{9,8},{10,9},{11,1... | collective-permute-start | bytes 46088 | tf_op jit(solution)/shard_map/ppermute | solution.py:16
  333.7 52.5 %collective-permute-start.7 = (f32[3,10,1,128]{3,2,1,0:T(1,128)S(1)}, f32[3,10,1,128]{3,2,1,0:T(1,128)S(1)}, u32[]{:S(2)}, u32[]{:S(2)}) collective-permute-start(f32[3,10,1,128]{3,2,1,0:T(1,128)S(1)} %get-tuple-element.13), channel_id=1, source_target_pairs={{0,1},{1,2},{2,3},{3,0},{4,5},{5,6},{6,7},{7,4},{8,9},{9,10},{10,1... | collective-permute-start | bytes 46088 | tf_op jit(solution)/shard_map/ppermute | solution.py:14
where the time goes:
time: 391 us; the launch traced here: 389 us
  local copies, waits for them, and re-layouts  175 us (45%)
  other arithmetic  159 us (41%)
  blocking collectives  38.2 us (10%)
  starting transfers between devices  12.7 us (3%)
    scatter-add x1, other arithmetic, body(): jnp.zeros((4, total_cells), jnp.float32).at[:, targets]  62.9 us
    sub x2, other arithmetic, body(): corrected = (1.0 - totals[3]) * flat_vel - totals[:3]  54.5 us
    slice x1, local copies, waits for them, and re-layouts, body(): center[0:1] * (east_side - west_side) * 0.5  52.5 us
    gather x2, local copies, waits for them, and re-layouts, body(): jnp.take(flat_vel, src_cell[0, 0].reshape(-1), axis=1)  44.6 us
    psum x1, blocking collectives, body(): points_x = lax.psum(sampled[0], ('gx', 'gy'))  38.2 us
    scatter-add x1, other arithmetic, body(): forcing = jnp.zeros((components, total_cells), jnp.float32).at[:, blade_c...  37.5 us
    reshape x1, local copies, waits for them, and re-layouts, body(): field_now = corrected.reshape(components, cells_x, cells_y, levels)  19.5 us
    reshape x1, local copies, waits for them, and re-layouts, body(): forcing_field = forcing.reshape(components, cells_x, cells_y, levels)  19.5 us
  transfers between devices with their start and end apart: 8, of which 2 were waited for; matrix products, arithmetic and copies ran while one was open for 33% of the time, Pallas kernels for 0%

commit v1 on v0

v1 whole, which is shorter than its diff:
```python
import functools

import jax
import jax.numpy as jnp
from jax import lax
from jax.experimental import pallas as pl
from jax.experimental.pallas import tpu as pltpu
from jax.sharding import PartitionSpec as P

F32 = jnp.float32
BF16 = jnp.bfloat16
VMEM_SPEC = pl.BlockSpec(memory_space=pltpu.VMEM)
SMEM_SPEC = pl.BlockSpec(memory_space=pltpu.SMEM)
PARAMS = pltpu.CompilerParams(vmem_limit_bytes=48 << 20)


def halves(value):
    high = value.astype(BF16)
    low = (value - high.astype(F32)).astype(BF16)
    return high, low


def one_hot(extent, index):
    rows = lax.broadcasted_iota(jnp.int32, (extent, index.shape[1]), 0)
    return jnp.where(rows == index, 1.0, 0.0).astype(BF16)


def build_table(vel_ref, table):
    half = vel_ref.shape[1] // 2
    for c in range(3):
        for piece in range(2):
            high, low = halves(vel_ref[c, piece * half : (piece + 1) * half, :])
            table[c, :, piece * 128 : (piece + 1) * 128] = high
            table[c, :, 256 + piece * 128 : 256 + (piece + 1) * 128] = low


def pick(table, cell):
    key = (cell & 127) | (((cell >> 15) & 1) << 7)
    place = (cell >> 7) & 255
    hot = one_hot(256, key)
    hot = jnp.concatenate([hot, hot], axis=0)
    here = lax.broadcasted_iota(jnp.int32, (256, cell.shape[1]), 0) == place
    out = []
    for c in range(3):
        found = jnp.dot(table[c], hot, preferred_element_type=F32)
        out.append(jnp.sum(jnp.where(here, found, 0.0), axis=0, keepdims=True))
    return out


def spread(cell, values):
    row = (cell >> 7) & 511
    level = cell & 127
    hot = one_hot(512, row)
    at_level = lax.broadcasted_iota(jnp.int32, (128, cell.shape[1]), 0) == level
    high, low = [], []
    for value in values:
        vh = value.astype(BF16).astype(F32)
        vl = value - vh
        high.append(jnp.where(at_level, vh, 0.0).astype(BF16))
        low.append(jnp.where(at_level, vl, 0.0).astype(BF16))
    left = jnp.concatenate([hot, hot], axis=1)
    right = jnp.concatenate([jnp.concatenate(high, axis=0), jnp.concatenate(low, axis=0)], axis=1)
    return lax.dot_general(left, right, (((1,), (1,)), ((), ())), preferred_element_type=F32)


def active_turbines(tile_ref, mine, listed):
    turbines = tile_ref.shape[0]
    owned = jnp.where(tile_ref[...] == mine, 1.0, 0.0)
    found = jnp.max(owned, axis=1, keepdims=True)
    total = jnp.int32(0)
    for t in range(turbines):
        listed[total] = t
        total = total + jnp.where(found[t, 0] > 0.5, 1, 0)
    return total


def gather_kernel(mine_ref, cnt_ref, vel_ref, src_ref, w_ref, tile_ref, cell_ref, out_ref, pts_ref, rot_ref, table, listed, tlist):
    build_table(vel_ref, table)
    out_ref[...] = jnp.zeros_like(out_ref)
    pts_ref[...] = jnp.zeros_like(pts_ref)
    mine = mine_ref[0]
    n_turb = active_turbines(tile_ref, mine, tlist)
    points = tile_ref.shape[1]

    def turbine(i, carry):
        t = tlist[i]
        owned = tile_ref[pl.ds(t, 1), :] == mine
        rows = pick(table, cell_ref[pl.ds(t, 1), :])
        for c in range(3):
            pts_ref[c, pl.ds(t, 1), :] = jnp.where(owned, rows[c], 0.0)
        return carry

    lax.fori_loop(0, n_turb, turbine, 0)
    sums = jnp.sum(pts_ref[0], axis=1, keepdims=True)
    rot_ref[...] = jnp.broadcast_to(sums, rot_ref.shape)

    total = jnp.int32(0)
    for d in range(9):
        blocks = (cnt_ref[0, 0, d] + 127) >> 7

        def put(j, n, d=d):
            listed[n] = d * 8 + j
            return n + 1

        total = lax.fori_loop(0, blocks, put, total)
    listed[total] = listed[total - 1]

    def pair(i, carry):
        b0, b1 = listed[2 * i], listed[2 * i + 1]
        cell = jnp.concatenate([src_ref[pl.ds(b0, 1), :], src_ref[pl.ds(b1, 1), :]], axis=1)
        rows = pick(table, cell)
        lane = lax.broadcasted_iota(jnp.int32, (1, 128), 1)
        for s, b in enumerate((b0, b1)):
            d, j = b >> 3, b & 7
            weight = jnp.where(lane + j * 128 < cnt_ref[0, 0, d], w_ref[pl.ds(b, 1), :], 0.0)
            for c in range(3):
                out_ref[d, c, pl.ds(j, 1), :] = rows[c][:, s * 128 : (s + 1) * 128] * weight
            out_ref[d, 3, pl.ds(j, 1), :] = weight
        return carry

    lax.fori_loop(0, (total + 1) >> 1, pair, 0)


def scatter_kernel(val_ref, dst_ref, vel_ref, cor_ref, xlo_ref, xhi_ref, ylo_ref, yhi_ref, acc, listed):
    acc[...] = jnp.zeros_like(acc)
    total = jnp.int32(0)
    for d in range(9):
        used = jnp.sum(jnp.where(val_ref[d, 3] != 0.0, 1.0, 0.0)).astype(jnp.int32)
        blocks = (used + 127) >> 7

        def put(j, n, d=d):
            listed[n] = d * 8 + j
            return n + 1

        total = lax.fori_loop(0, blocks, put, total)
    for k in range(4):
        listed[total + k] = 0

    def chunk(i, carry):
        cells, vals = [], [[], [], [], []]
        for k in range(4):
            at = 4 * i + k
            b = listed[at]
            d, j = b >> 3, b & 7
            keep = jnp.where(at < total, 1.0, 0.0)
            cells.append(dst_ref[pl.ds(b, 1), :])
            for c in range(4):
                vals[c].append(val_ref[d, c, pl.ds(j, 1), :] * keep)
        cell = jnp.concatenate(cells, axis=1)
        vals = [jnp.concatenate(v, axis=1) for v in vals]
        acc[...] += spread(cell, vals)
        return carry

    lax.fori_loop(0, (total + 3) >> 2, chunk, 0)
    for c in range(3):
        cor = (1.0 - acc[:, 384:512]) * vel_ref[c] - acc[:, c * 128 : (c + 1) * 128]
        cor_ref[c] = cor
        xlo_ref[c] = cor[0:64]
        xhi_ref[c] = cor[448:512]
        for x in range(8):
            ylo_ref[c, x : x + 1, :] = cor[x * 64 : x * 64 + 1]
            yhi_ref[c, x : x + 1, :] = cor[x * 64 + 63 : x * 64 + 64]


def forcing_kernel(mine_ref, tile_ref, cell_ref, coef_ref, pts_ref, rot_ref, out_ref, tlist):
    out_ref[...] = jnp.zeros_like(out_ref)
    n_turb = active_turbines(tile_ref, mine_ref[0], tlist)
    points = tile_ref.shape[1]

    def turbine(i, carry):
        t = tlist[i]
        rotor = rot_ref[pl.ds(t, 1), 0:1] * (1.0 / 192)
        scale = -coef_ref[pl.ds(t, 1), :] * rotor
        force = [scale * pts_ref[c, pl.ds(t, 1), :] for c in range(3)]
        got = spread(cell_ref[pl.ds(t, 1), :], force)
        for c in range(3):
            out_ref[c] += got[:, c * 128 : (c + 1) * 128]
        return carry

    lax.fori_loop(0, n_turb, turbine, 0)


def stencil_kernel(cor_ref, frc_ref, west_ref, east_ref, south_ref, north_ref, out_ref):
    lane = lax.broadcasted_iota(jnp.int32, (64, 128), 1)
    for x in range(8):
        rows = slice(x * 64, x * 64 + 64)
        now = [cor_ref[c, rows, :] for c in range(3)]
        for c in range(3):
            u = now[c]
            west = cor_ref[c, (x - 1) * 64 : x * 64, :] if x > 0 else west_ref[c]
            east = cor_ref[c, (x + 1) * 64 : (x + 2) * 64, :] if x < 7 else east_ref[c]
            south = jnp.concatenate([south_ref[c, x : x + 1, :], u[:-1]], axis=0)
            north = jnp.concatenate([u[1:], north_ref[c, x : x + 1, :]], axis=0)
            upper = jnp.where(lane == 127, 0.0, pltpu.roll(u, 127, 1))
            lower = jnp.where(lane == 0, 0.0, pltpu.roll(u, 1, 1))
            laplace = east + west + north + south + upper + lower - 6.0 * u
            advect = (
                now[0] * (east - west) * 0.5
                + now[1] * (north - south) * 0.5
                + now[2] * (upper - lower) * 0.5
            )
            out_ref[c, rows, :] = u + 0.2 * (0.15 * laplace - advect + frc_ref[c, rows, :])


def shift(value, axis, step):
    count = lax.axis_size(axis)
    return lax.ppermute(value, axis, [(i, (i + step) % count) for i in range(count)])


def total_over(value, axis):
    count = lax.axis_size(axis)
    step = 1
    while step < count:
        value = value + lax.ppermute(value, axis, [(i, i ^ step) for i in range(count)])
        step *= 2
    return value


def body(velocity, counts, src_cell, weights, dst_cell, blade_tile, blade_cell, blade_coef):
    vel = velocity.reshape(3, 512, 128)
    src = src_cell.reshape(72, 128)
    weight = weights.reshape(72, 128)
    dst = dst_cell.reshape(72, 128)
    turbines, points = blade_cell.shape
    mine = (lax.axis_index("gx") * lax.axis_size("gy") + lax.axis_index("gy")).reshape(1).astype(jnp.int32)
    rows_t, lanes_t = turbines + -turbines % 8, points + -points % 128
    pad = ((0, rows_t - turbines), (0, lanes_t - points))
    tile = jnp.pad(blade_tile, pad, constant_values=-1)
    cell = jnp.pad(blade_cell, pad)
    coef = jnp.pad(blade_coef, pad)

    sent, pts, partial = pl.pallas_call(
        gather_kernel,
        out_shape=(
            jax.ShapeDtypeStruct((9, 4, 8, 128), F32),
            jax.ShapeDtypeStruct((3, rows_t, lanes_t), F32),
            jax.ShapeDtypeStruct((rows_t, 128), F32),
        ),
        in_specs=[SMEM_SPEC, SMEM_SPEC] + [VMEM_SPEC] * 5,
        out_specs=(VMEM_SPEC,) * 3,
        scratch_shapes=[pltpu.VMEM((3, 256, 512), BF16), pltpu.SMEM((80,), jnp.int32), pltpu.SMEM((32,), jnp.int32)],
        compiler_params=PARAMS,
        name="gather",
    )(mine, counts, vel, src, weight, tile, cell)

    rotor = total_over(total_over(partial, "gy"), "gx")

    low = shift(sent[0:3], "gx", -1)
    high = shift(sent[6:9], "gx", 1)
    grid = jnp.concatenate([low, sent[3:6], high], axis=0).reshape(3, 3, 4, 8, 128)
    low = shift(grid[:, 0], "gy", -1)
    high = shift(grid[:, 2], "gy", 1)
    arrived = jnp.stack([low, grid[:, 1], high], axis=1).reshape(9, 4, 8, 128)

    cor, xlo, xhi, ylo, yhi = pl.pallas_call(
        scatter_kernel,
        out_shape=(
            jax.ShapeDtypeStruct((3, 512, 128), F32),
            jax.ShapeDtypeStruct((3, 64, 128), F32),
            jax.ShapeDtypeStruct((3, 64, 128), F32),
            jax.ShapeDtypeStruct((3, 8, 128), F32),
            jax.ShapeDtypeStruct((3, 8, 128), F32),
        ),
        in_specs=[VMEM_SPEC] * 3,
        out_specs=(VMEM_SPEC,) * 5,
        scratch_shapes=[pltpu.VMEM((512, 512), F32), pltpu.SMEM((80,), jnp.int32)],
        compiler_params=PARAMS,
        name="scatter",
    )(arrived, dst, vel)

    west = shift(xhi, "gx", 1)
    east = shift(xlo, "gx", -1)
    south = shift(yhi, "gy", 1)
    north = shift(ylo, "gy", -1)

    forcing = pl.pallas_call(
        forcing_kernel,
        out_shape=jax.ShapeDtypeStruct((3, 512, 128), F32),
        in_specs=[SMEM_SPEC] + [VMEM_SPEC] * 5,
        out_specs=VMEM_SPEC,
        scratch_shapes=[pltpu.SMEM((32,), jnp.int32)],
        compiler_params=PARAMS,
        name="forcing",
    )(mine, tile, cell, coef, pts, rotor)

    updated = pl.pallas_call(
        stencil_kernel,
        out_shape=jax.ShapeDtypeStruct((3, 512, 128), F32),
        in_specs=[VMEM_SPEC] * 6,
        out_specs=VMEM_SPEC,
        compiler_params=PARAMS,
        name="stencil",
    )(cor, forcing, west, east, south, north)
    return updated.reshape(velocity.shape), forcing.reshape(velocity.shape)


def solution(mesh):
    grid = P("gx", "gy", None)
    lists = P("gx", "gy", None, None)
    field = P(None, "gx", "gy", None)
    return jax.shard_map(
        body,
        mesh=mesh,
        in_specs=(field, grid, lists, lists, lists, P(), P(), P()),
        out_specs=(field, field),
        check_vma=False,
    )
```

time: 391 us -> 69.1 us (0.18)
  local copies, waits for them, and re-layouts: 175 us -> 4.55 us
  other arithmetic: 159 us -> 0.04 us
  blocking collectives: 38.2 us -> 0 us
  Pallas kernels: 0 us -> 24.5 us
  waiting for transfers between devices: 2.43 us -> 25.5 us
    scatter-add x2 -> x0, other arithmetic: 100 us -> none  [the longest x1 62.9 us: body(): jnp.zeros((4, total_cells), jnp.float32).at[:, targets]]
    gather x4 -> x0, local copies, waits for them, and re-layouts: 62.3 us -> none  [the longest x2 44.6 us: body(): jnp.take(flat_vel, src_cell[0, 0].reshape(-1), axis=1)]
    sub x2 -> x0, other arithmetic: 54.5 us -> none  [body(): corrected = (1.0 - totals[3]) * flat_vel - totals[:3]]
    slice x3 -> x1, local copies, waits for them, and re-layouts: 52.5 us -> 0.01 us  [body(): low = shift(sent[0:3], 'gx', -1)]
    reshape x3 -> x0, local copies, waits for them, and re-layouts: 39 us -> none  [the longest x1 19.5 us: body(): field_now = corrected.reshape(components, cells_x, cells_y, levels)]
    psum x1 -> x0, blocking collectives: 38.2 us -> none  [body(): points_x = lax.psum(sampled[0], ('gx', 'gy'))]
    pallas_call x0 -> x4, Pallas kernels: none -> 24.5 us  [the longest x1 11.3 us: body(): pl.pallas_call(gather_kernel, out_shape=(jax.ShapeDtypeStruct((9, 4, 8, 1...]
    ppermute x8 -> x13, waiting for transfers between devices: 2.43 us -> 25.5 us  [the longest x5 13.4 us: total_over(): lax.ppermute(value, axis, [(i, i ^ step) for i in range(count)])]
  transfers between devices with their start and end apart: 8 -> 13, of which waited for: 2 -> 9; matrix products, arithmetic and copies ran while one was open for 33% -> 0% of each run, Pallas kernels for 0% -> 5%
where the time goes in v1:
time: 69.1 us; the launch traced here: 69.3 us
  waiting for transfers between devices  25.5 us (37%)
  Pallas kernels  24.5 us (35%)
  starting transfers between devices  14 us (20%)
  local copies, waits for them, and re-layouts  4.55 us (7%)
  between operations  0.79 us (1%)
    ppermute x5, waiting for transfers between devices, total_over(): lax.ppermute(value, axis, [(i, i ^ step) for i in range(count)])  13.4 us
    ppermute x8, waiting for transfers between devices, shift(): lax.ppermute(value, axis, [(i, (i + step) % count) for i in range(count)])  12.1 us
    pallas_call x1, Pallas kernels, body(): pl.pallas_call(gather_kernel, out_shape=(jax.ShapeDtypeStruct((9, 4, 8, 1...  11.3 us
    ppermute x8, starting transfers between devices, shift(): lax.ppermute(value, axis, [(i, (i + step) % count) for i in range(count)])  10.7 us
    pallas_call x1, Pallas kernels, body(): pl.pallas_call(scatter_kernel, out_shape=(jax.ShapeDtypeStruct((3, 512, 1...  8.22 us
    unnamed x18, local copies, waits for them, and re-layouts  3.76 us
    ppermute x5, starting transfers between devices, total_over(): lax.ppermute(value, axis, [(i, i ^ step) for i in range(count)])  3.27 us
    pallas_call x1, Pallas kernels, body(): pl.pallas_call(forcing_kernel, out_shape=jax.ShapeDtypeStruct((3, 512, 12...  3.25 us
  transfers between devices with their start and end apart: 13, of which 9 were waited for; matrix products, arithmetic and copies ran while one was open for 0% of the time, Pallas kernels for 5%

profile of v1, /device:TPU:0, one launch (start us, length us, event | category | flops | bytes accessed | tf_op | source)
XLA Modules:
  0.0 69.3 jit_solution(16540757590115968400)
XLA Ops:
  0.6 0.0 copy-start.7
  0.6 0.0 copy-start.4
  0.7 0.8 %pad.11.tile_ref = s32[24,256]{1,0:T(8,128)S(1)} pad(s32[20,192]{1,0:T(8,128)} %param.13, s32[]{:T(128)} %constant.14.clone.1), padding=0_4x0_64 | pad | bytes 39940 | tf_op jit(solution)/shard_map/jit(_pad)/pad | solution.py:228
  1.4 0.0 copy-done.7
  1.4 0.0 copy-start.3
  1.4 0.0 copy-start.6
  1.4 0.0 copy-done.4
  1.5 0.7 %copy-done.3 = s32[1,1,9,1024]{3,1,2,0:T(1,128)S(1)} copy-done((s32[1,1,9,1024]{3,1,2,0:T(1,128)S(1)}, s32[1,1,9,1024]{3,1,2,0:T(1,128)}, u32[]{:S(2)}) %copy-start.3) | copy-done | bytes 36888
  2.2 0.0 copy-done.6
  2.2 0.0 copy-start.1
  2.2 1.1 %copy-done.1 = f32[3,8,64,128]{3,2,1,0:T(8,128)S(1)} copy-done((f32[3,8,64,128]{3,2,1,0:T(8,128)S(1)}, f32[3,8,64,128]{3,2,1,0:T(8,128)}, u32[]{:S(2)}) %copy-start.1) | copy-done | bytes 786456
  3.3 11.3 %gather.1 = (f32[9,4,8,128]{3,2,1,0:T(8,128)S(1)}, f32[3,24,256]{2,1,0:T(8,128)S(1)}, f32[24,128]{1,0:T(8,128)S(1)}) custom-call(s32[1]{0:T(128)} %bitcast.mine_ref, s32[1,1,9]{2,1,0:T(1,128)S(1)} %copy-done.6, f32[3,512,128]{2,1,0:T(8,128)S(1)} %bitcast.20, s32[72,128]{1,0:T(8,128)S(1)} %bitcast.23, f32[72,128]{1,0:T(8,128)S(1)} %bitcast.24, ...), custom_call_target="tpu_custom_call" | custom-call | tf_op jit(solution)/shard_map/gather/pallas_call | solution.py:232
  14.6 0.0 copy-start.2
  14.7 3.6 %collective-permute-start = (f32[3,4,8,128]{3,2,1,0:T(8,128)S(1)}, f32[3,4,8,128]{3,2,1,0:T(8,128)S(1)}, u32[]{:S(2)}, u32[]{:S(2)}) collective-permute-start(f32[3,4,8,128]{3,2,1,0:T(8,128)S(1)} %get-tuple-element.21), channel_id=1, source_target_pairs={{0,28},{4,0},{8,4},{12,8},{16,12},{20,16},{24,20},{28,24},{1,29},{... | collective-permute-start | bytes 147464 | tf_op jit(solution)/shard_map/ppermute | solution.py:207
  18.3 0.0 collective-permute-start.1
  18.3 1.7 %collective-permute-done = f32[3,4,8,128]{3,2,1,0:T(8,128)S(1)} collective-permute-done((f32[3,4,8,128]{3,2,1,0:T(8,128)S(1)}, f32[3,4,8,128]{3,2,1,0:T(8,128)S(1)}, u32[]{:S(2)}, u32[]{:S(2)}) %collective-permute-start) | collective-permute-done | bytes 49184 | tf_op jit(solution)/shard_map/ppermute | solution.py:207
  20.0 5.0 %collective-permute-done.1 = f32[3,4,8,128]{3,2,1,0:T(8,128)S(1)} collective-permute-done((f32[3,4,8,128]{3,2,1,0:T(8,128)S(1)}, f32[3,4,8,128]{3,2,1,0:T(8,128)S(1)}, u32[]{:S(2)}, u32[]{:S(2)}) %collective-permute-start.1) | collective-permute-done | bytes 49184 | tf_op jit(solution)/shard_map/ppermute | solution.py:207
  25.1 0.4 collective-permute-start.2
  25.5 0.1 collective-permute-start.3
  25.7 1.6 %collective-permute-done.2 = f32[3,4,8,128]{3,2,1,0:T(8,128)S(1)} collective-permute-done((f32[3,4,8,128]{3,2,1,0:T(8,128)S(1)}, f32[3,4,8,128]{3,2,1,0:T(8,128)S(1)}, u32[]{:S(2)}, u32[]{:S(2)}) %collective-permute-start.2) | collective-permute-done | bytes 49184 | tf_op jit(solution)/shard_map/ppermute | solution.py:207
  27.3 3.7 %collective-permute-done.3 = f32[3,4,8,128]{3,2,1,0:T(8,128)S(1)} collective-permute-done((f32[3,4,8,128]{3,2,1,0:T(8,128)S(1)}, f32[3,4,8,128]{3,2,1,0:T(8,128)S(1)}, u32[]{:S(2)}, u32[]{:S(2)}) %collective-permute-start.3) | collective-permute-done | bytes 49184 | tf_op jit(solution)/shard_map/ppermute | solution.py:207
  31.0 0.0 copy-start.5
  31.0 0.0 copy-done.2
  31.0 0.7 %copy-done.5 = s32[1,1,9,1024]{3,1,2,0:T(1,128)S(1)} copy-done((s32[1,1,9,1024]{3,1,2,0:T(1,128)S(1)}, s32[1,1,9,1024]{3,1,2,0:T(1,128)}, u32[]{:S(2)}) %copy-start.5) | copy-done | bytes 36888
  31.7 8.2 %scatter.1 = (f32[3,512,128]{2,1,0:T(8,128)S(1)}, f32[3,64,128]{2,1,0:T(8,128)S(1)}, f32[3,64,128]{2,1,0:T(8,128)S(1)}, f32[3,8,128]{2,1,0:T(8,128)S(1)}, f32[3,8,128]{2,1,0:T(8,128)S(1)}) custom-call(f32[9,4,8,128]{3,2,1,0:T(8,128)S(1)} %bitcast.22, s32[72,128]{1,0:T(8,128)S(1)} %bitcast.25, f32[3,512,128]{2,1,0:T(8,128)S(1)} %bitcast.21), custom_call_target="tpu_custom_call" | custom-call | tf_op jit(solution)/shard_map/scatter/pallas_call | solution.py:255
  40.0 0.1 collective-permute-start.9
  40.0 4.7 %collective-permute-start.10 = (f32[3,64,128]{2,1,0:T(8,128)S(1)}, f32[3,64,128]{2,1,0:T(8,128)S(1)}, u32[]{:S(2)}, u32[]{:S(2)}) collective-permute-start(f32[3,64,128]{2,1,0:T(8,128)S(1)} %get-tuple-element.15), channel_id=1, source_target_pairs={{0,28},{4,0},{8,4},{12,8},{16,12},{20,16},{24,20},{28,24},{1,29},{... | collective-permute-start | bytes 294920 | tf_op jit(solution)/shard_map/ppermute | solution.py:207
  44.7 1.9 %collective-permute-start.4 = (f32[24,128]{1,0:T(8,128)S(1)}, f32[24,128]{1,0:T(8,128)S(1)}, u32[]{:S(2)}, u32[]{:S(2)}) collective-permute-start(f32[24,128]{1,0:T(8,128)S(1)} %get-tuple-element.13), channel_id=1, source_target_pairs={{0,1},{1,0},{2,3},{3,2},{4,5},{5,4},{6,7},{7,6},{8,9},{9,8},{10,11... | collective-permute-start | bytes 36872 | tf_op jit(solution)/shard_map/ppermute | solution.py:214
  46.6 0.8 %collective-permute-done.4 = f32[24,128]{1,0:T(8,128)S(1)} collective-permute-done((f32[24,128]{1,0:T(8,128)S(1)}, f32[24,128]{1,0:T(8,128)S(1)}, u32[]{:S(2)}, u32[]{:S(2)}) %collective-permute-start.4) | collective-permute-done | bytes 12320 | tf_op jit(solution)/shard_map/ppermute | solution.py:214
  47.5 1.4 %collective-permute-start.5 = (f32[24,128]{1,0:T(8,128)S(1)}, f32[24,128]{1,0:T(8,128)S(1)}, u32[]{:S(2)}, u32[]{:S(2)}) collective-permute-start(f32[24,128]{1,0:T(8,128)S(1)} %add.25), channel_id=1, source_target_pairs={{0,2},{1,3},{2,0},{3,1},{4,6},{5,7},{6,4},{7,5},{8,10},{9,11},{10,... | collective-permute-start | bytes 36872 | tf_op jit(solution)/shard_map/ppermute | solution.py:214
  48.8 2.3 %collective-permute-done.5 = f32[24,128]{1,0:T(8,128)S(1)} collective-permute-done((f32[24,128]{1,0:T(8,128)S(1)}, f32[24,128]{1,0:T(8,128)S(1)}, u32[]{:S(2)}, u32[]{:S(2)}) %collective-permute-start.5) | collective-permute-done | bytes 12320 | tf_op jit(solution)/shard_map/ppermute | solution.py:214
  51.2 0.0 collective-permute-start.6
  51.2 3.7 %collective-permute-done.6 = f32[24,128]{1,0:T(8,128)S(1)} collective-permute-done((f32[24,128]{1,0:T(8,128)S(1)}, f32[24,128]{1,0:T(8,128)S(1)}, u32[]{:S(2)}, u32[]{:S(2)}) %collective-permute-start.6) | collective-permute-done | bytes 12320 | tf_op jit(solution)/shard_map/ppermute | solution.py:214
  54.9 0.0 copy-start.8
  54.9 0.0 collective-permute-start.7
  54.9 3.7 %collective-permute-done.7 = f32[24,128]{1,0:T(8,128)S(1)} collective-permute-done((f32[24,128]{1,0:T(8,128)S(1)}, f32[24,128]{1,0:T(8,128)S(1)}, u32[]{:S(2)}, u32[]{:S(2)}) %collective-permute-start.7) | collective-permute-done | bytes 12320 | tf_op jit(solution)/shard_map/ppermute | solution.py:214
  58.6 0.0 collective-permute-start.8
  58.6 0.0 collective-permute-start.11
  58.6 1.7 %collective-permute-start.12 = (f32[3,8,128]{2,1,0:T(8,128)S(1)}, f32[3,8,128]{2,1,0:T(8,128)S(1)}, u32[]{:S(2)}, u32[]{:S(2)}) collective-permute-start(f32[3,8,128]{2,1,0:T(8,128)S(1)} %get-tuple-element.17), channel_id=1, source_target_pairs={{0,3},{1,0},{2,1},{3,2},{4,7},{5,4},{6,5},{7,6},{8,11},{9,8},{10,9... | collective-permute-start | bytes 36872 | tf_op jit(solution)/shard_map/ppermute | solution.py:207
  60.3 0.0 copy-done.8
  60.3 2.8 %collective-permute-done.8 = f32[24,128]{1,0:T(8,128)S(1)} collective-permute-done((f32[24,128]{1,0:T(8,128)S(1)}, f32[24,128]{1,0:T(8,128)S(1)}, u32[]{:S(2)}, u32[]{:S(2)}) %collective-permute-start.8) | collective-permute-done | bytes 12320 | tf_op jit(solution)/shard_map/ppermute | solution.py:214
  63.2 3.3 %forcing.1.frc_ref = f32[3,512,128]{2,1,0:T(8,128)} custom-call(s32[1]{0:T(128)} %bitcast.mine_ref, s32[24,256]{1,0:T(8,128)S(1)} %pad.11.tile_ref, s32[24,256]{1,0:T(8,128)S(1)} %pad.12.cell_ref, f32[24,256]{1,0:T(8,128)S(1)} %pad.13.coef_ref, f32[3,24,256]{2,1,0:T(8,128)S(1)} %get-tuple-element.12.pts_ref, f32[24,128]{1,0:T(8,128)S(1)} %add.29.rot_ref), custom_call_target="tpu_custom_call" | custom-call | tf_op jit(solution)/shard_map/forcing/pallas_call | solution.py:276
  66.4 0.0 collective-permute-done.11.south_ref
  66.4 0.0 collective-permute-done.12.north_ref
  66.4 0.0 collective-permute-done.9.west_ref
  66.4 0.0 collective-permute-done.10.east_ref
  66.5 0.0 copy-start
  66.5 1.1 %copy-done = f32[3,512,128]{2,1,0:T(8,128)S(1)} copy-done((f32[3,512,128]{2,1,0:T(8,128)S(1)}, f32[3,512,128]{2,1,0:T(8,128)}, u32[]{:S(2)}) %copy-start) | copy-done | bytes 786456
  67.6 1.7 %stencil.1 = f32[3,512,128]{2,1,0:T(8,128)} custom-call(f32[3,512,128]{2,1,0:T(8,128)S(1)} %get-tuple-element.11.cor_ref, f32[3,512,128]{2,1,0:T(8,128)S(1)} %copy-done, f32[3,64,128]{2,1,0:T(8,128)S(1)} %collective-permute-done.9.west_ref, f32[3,64,128]{2,1,0:T(8,128)S(1)} %collective-permute-done.10.east_ref, ...), custom_call_target="tpu_custom_call" | custom-call | tf_op jit(solution)/shard_map/stencil/pallas_call | solution.py:286
  (11 shorter events, 0.1 us)
Async XLA Ops:
  0.6 0.8 %copy-start.7 = (s32[20,192]{1,0:T(8,128)S(1)}, s32[20,192]{1,0:T(8,128)}, u32[]{:S(2)}) copy-start(s32[20,192]{1,0:T(8,128)} %param.14) | copy-start | bytes 46084
  0.6 0.8 %copy-start.4 = (f32[1,1,9,1024]{3,1,2,0:T(1,128)S(1)}, f32[1,1,9,1024]{3,1,2,0:T(1,128)}, u32[]{:S(2)}) copy-start(f32[1,1,9,1024]{3,1,2,0:T(1,128)} %param.11) | copy-start | bytes 110596
  1.4 0.8 %copy-start.3 = (s32[1,1,9,1024]{3,1,2,0:T(1,128)S(1)}, s32[1,1,9,1024]{3,1,2,0:T(1,128)}, u32[]{:S(2)}) copy-start(s32[1,1,9,1024]{3,1,2,0:T(1,128)} %param.10) | copy-start | bytes 110596
  1.4 0.8 %copy-start.6 = (s32[1,1,9]{2,1,0:T(1,128)S(1)}, s32[1,1,9]{2,1,0:T(1,128)}, u32[]{:S(2)}) copy-start(s32[1,1,9]{2,1,0:T(1,128)} %cnt_ref.1) | copy-start | bytes 112
  2.2 1.1 %copy-start.1 = (f32[3,8,64,128]{3,2,1,0:T(8,128)S(1)}, f32[3,8,64,128]{3,2,1,0:T(8,128)}, u32[]{:S(2)}) copy-start(f32[3,8,64,128]{3,2,1,0:T(8,128)} %param.8) | copy-start | bytes 2359300
  14.6 16.4 %copy-start.2 = (f32[3,8,64,128]{3,2,1,0:T(8,128)S(1)}, f32[3,8,64,128]{3,2,1,0:T(8,128)}, u32[]{:S(2)}) copy-start(f32[3,8,64,128]{3,2,1,0:T(8,128)} %param.8) | copy-start | bytes 2359300
  14.7 5.4 %collective-permute-start = (f32[3,4,8,128]{3,2,1,0:T(8,128)S(1)}, f32[3,4,8,128]{3,2,1,0:T(8,128)S(1)}, u32[]{:S(2)}, u32[]{:S(2)}) collective-permute-start(f32[3,4,8,128]{3,2,1,0:T(8,128)S(1)} %get-tuple-element.21), channel_id=1, source_target_pairs={{0,28},{4,0},{8,4},{12,8},{16,12},{20,16},{24,20},{28,24},{1,29},{... | collective-permute-start | bytes 147464 | tf_op jit(solution)/shard_map/ppermute | solution.py:207
  18.3 6.8 %collective-permute-start.1 = (f32[3,4,8,128]{3,2,1,0:T(8,128)S(1)}, f32[3,4,8,128]{3,2,1,0:T(8,128)S(1)}, u32[]{:S(2)}, u32[]{:S(2)}) collective-permute-start(f32[3,4,8,128]{3,2,1,0:T(8,128)S(1)} %get-tuple-element.22), channel_id=1, source_target_pairs={{0,4},{4,8},{8,12},{12,16},{16,20},{20,24},{24,28},{28,0},{1,5},{5... | collective-permute-start | bytes 147464 | tf_op jit(solution)/shard_map/ppermute | solution.py:207
  25.1 2.2 %collective-permute-start.2 = (f32[3,4,8,128]{3,2,1,0:T(8,128)S(1)}, f32[3,4,8,128]{3,2,1,0:T(8,128)S(1)}, u32[]{:S(2)}, u32[]{:S(2)}) collective-permute-start(f32[3,4,8,128]{3,2,1,0:T(8,128)S(1)} %get-tuple-element.18), channel_id=1, source_target_pairs={{0,3},{1,0},{2,1},{3,2},{4,7},{5,4},{6,5},{7,6},{8,11},{9,8},{10,9... | collective-permute-start | bytes 147464 | tf_op jit(solution)/shard_map/ppermute | solution.py:207
  25.5 5.4 %collective-permute-start.3 = (f32[3,4,8,128]{3,2,1,0:T(8,128)S(1)}, f32[3,4,8,128]{3,2,1,0:T(8,128)S(1)}, u32[]{:S(2)}, u32[]{:S(2)}) collective-permute-start(f32[3,4,8,128]{3,2,1,0:T(8,128)S(1)} %get-tuple-element.19), channel_id=1, source_target_pairs={{0,1},{1,2},{2,3},{3,0},{4,5},{5,6},{6,7},{7,4},{8,9},{9,10},{10,1... | collective-permute-start | bytes 147464 | tf_op jit(solution)/shard_map/ppermute | solution.py:207
  31.0 0.8 %copy-start.5 = (s32[1,1,9,1024]{3,1,2,0:T(1,128)S(1)}, s32[1,1,9,1024]{3,1,2,0:T(1,128)}, u32[]{:S(2)}) copy-start(s32[1,1,9,1024]{3,1,2,0:T(1,128)} %param.12) | copy-start | bytes 110596
  40.0 26.5 %collective-permute-start.9 = (f32[3,64,128]{2,1,0:T(8,128)S(1)}, f32[3,64,128]{2,1,0:T(8,128)S(1)}, u32[]{:S(2)}, u32[]{:S(2)}) collective-permute-start(f32[3,64,128]{2,1,0:T(8,128)S(1)} %get-tuple-element.14), channel_id=1, source_target_pairs={{0,4},{4,8},{8,12},{12,16},{16,20},{20,24},{24,28},{28,0},{1,5},{5... | collective-permute-start | bytes 294920 | tf_op jit(solution)/shard_map/ppermute | solution.py:207
  40.0 26.4 %collective-permute-start.10 = (f32[3,64,128]{2,1,0:T(8,128)S(1)}, f32[3,64,128]{2,1,0:T(8,128)S(1)}, u32[]{:S(2)}, u32[]{:S(2)}) collective-permute-start(f32[3,64,128]{2,1,0:T(8,128)S(1)} %get-tuple-element.15), channel_id=1, source_target_pairs={{0,28},{4,0},{8,4},{12,8},{16,12},{20,16},{24,20},{28,24},{1,29},{... | collective-permute-start | bytes 294920 | tf_op jit(solution)/shard_map/ppermute | solution.py:207
  44.7 2.7 %collective-permute-start.4 = (f32[24,128]{1,0:T(8,128)S(1)}, f32[24,128]{1,0:T(8,128)S(1)}, u32[]{:S(2)}, u32[]{:S(2)}) collective-permute-start(f32[24,128]{1,0:T(8,128)S(1)} %get-tuple-element.13), channel_id=1, source_target_pairs={{0,1},{1,0},{2,3},{3,2},{4,5},{5,4},{6,7},{7,6},{8,9},{9,8},{10,11... | collective-permute-start | bytes 36872 | tf_op jit(solution)/shard_map/ppermute | solution.py:214
  47.5 3.7 %collective-permute-start.5 = (f32[24,128]{1,0:T(8,128)S(1)}, f32[24,128]{1,0:T(8,128)S(1)}, u32[]{:S(2)}, u32[]{:S(2)}) collective-permute-start(f32[24,128]{1,0:T(8,128)S(1)} %add.25), channel_id=1, source_target_pairs={{0,2},{1,3},{2,0},{3,1},{4,6},{5,7},{6,4},{7,5},{8,10},{9,11},{10,... | collective-permute-start | bytes 36872 | tf_op jit(solution)/shard_map/ppermute | solution.py:214
  51.2 3.7 %collective-permute-start.6 = (f32[24,128]{1,0:T(8,128)S(1)}, f32[24,128]{1,0:T(8,128)S(1)}, u32[]{:S(2)}, u32[]{:S(2)}) collective-permute-start(f32[24,128]{1,0:T(8,128)S(1)} %add.26), channel_id=1, source_target_pairs={{0,4},{4,0},{8,12},{12,8},{16,20},{20,16},{24,28},{28,24},{1,5},{5... | collective-permute-start | bytes 36872 | tf_op jit(solution)/shard_map/ppermute | solution.py:214
  54.9 5.5 %copy-start.8 = (f32[20,192]{1,0:T(8,128)S(1)}, f32[20,192]{1,0:T(8,128)}, u32[]{:S(2)}) copy-start(f32[20,192]{1,0:T(8,128)} %param.15) | copy-start | bytes 46084
  54.9 3.7 %collective-permute-start.7 = (f32[24,128]{1,0:T(8,128)S(1)}, f32[24,128]{1,0:T(8,128)S(1)}, u32[]{:S(2)}, u32[]{:S(2)}) collective-permute-start(f32[24,128]{1,0:T(8,128)S(1)} %add.27), channel_id=1, source_target_pairs={{0,8},{4,12},{8,0},{12,4},{16,24},{20,28},{24,16},{28,20},{1,9},{5... | collective-permute-start | bytes 36872 | tf_op jit(solution)/shard_map/ppermute | solution.py:214
  58.6 4.6 %collective-permute-start.8 = (f32[24,128]{1,0:T(8,128)S(1)}, f32[24,128]{1,0:T(8,128)S(1)}, u32[]{:S(2)}, u32[]{:S(2)}) collective-permute-start(f32[24,128]{1,0:T(8,128)S(1)} %add.28), channel_id=1, source_target_pairs={{0,16},{4,20},{8,24},{12,28},{16,0},{20,4},{24,8},{28,12},{1,17},{... | collective-permute-start | bytes 36872 | tf_op jit(solution)/shard_map/ppermute | solution.py:214
  58.6 7.9 %collective-permute-start.11 = (f32[3,8,128]{2,1,0:T(8,128)S(1)}, f32[3,8,128]{2,1,0:T(8,128)S(1)}, u32[]{:S(2)}, u32[]{:S(2)}) collective-permute-start(f32[3,8,128]{2,1,0:T(8,128)S(1)} %get-tuple-element.16), channel_id=1, source_target_pairs={{0,1},{1,2},{2,3},{3,0},{4,5},{5,6},{6,7},{7,4},{8,9},{9,10},{10,1... | collective-permute-start | bytes 36872 | tf_op jit(solution)/shard_map/ppermute | solution.py:207
  58.6 7.8 %collective-permute-start.12 = (f32[3,8,128]{2,1,0:T(8,128)S(1)}, f32[3,8,128]{2,1,0:T(8,128)S(1)}, u32[]{:S(2)}, u32[]{:S(2)}) collective-permute-start(f32[3,8,128]{2,1,0:T(8,128)S(1)} %get-tuple-element.17), channel_id=1, source_target_pairs={{0,3},{1,0},{2,1},{3,2},{4,7},{5,4},{6,5},{7,6},{8,11},{9,8},{10,9... | collective-permute-start | bytes 36872 | tf_op jit(solution)/shard_map/ppermute | solution.py:207
  66.5 1.1 %copy-start = (f32[3,512,128]{2,1,0:T(8,128)S(1)}, f32[3,512,128]{2,1,0:T(8,128)}, u32[]{:S(2)}) copy-start(f32[3,512,128]{2,1,0:T(8,128)} %forcing.1.frc_ref) | copy-start | bytes 2359300

commit v2 on v0

v2 whole, which is shorter than its diff:
```python
import jax
import jax.numpy as jnp
from jax import lax
from jax.experimental import pallas as pl
from jax.experimental.pallas import tpu as pltpu
from jax.sharding import PartitionSpec as P

F32 = jnp.float32
BF16 = jnp.bfloat16
VMEM = pl.BlockSpec(memory_space=pltpu.VMEM)
SMEM = pl.BlockSpec(memory_space=pltpu.SMEM)
HBM = pl.BlockSpec(memory_space=pl.ANY)


def halves(value):
    high = value.astype(BF16)
    low = (value - high.astype(F32)).astype(BF16)
    return high, low


def one_hot(extent, index):
    rows = lax.broadcasted_iota(jnp.int32, (extent, index.shape[1]), 0)
    return jnp.where(rows == index, 1.0, 0.0).astype(BF16)


def pick(table, cell):
    key = (cell & 127) | (((cell >> 15) & 1) << 7)
    place = (cell >> 7) & 255
    hot = one_hot(256, key)
    hot = jnp.concatenate([hot, hot], axis=0)
    here = lax.broadcasted_iota(jnp.int32, (256, cell.shape[1]), 0) == place
    out = []
    for c in range(3):
        found = jnp.dot(table[c], hot, preferred_element_type=F32)
        out.append(jnp.sum(jnp.where(here, found, 0.0), axis=0, keepdims=True))
    return out


def spread(extent, row, level, values):
    hot = one_hot(extent, row)
    at_level = lax.broadcasted_iota(jnp.int32, (128, level.shape[1]), 0) == level
    high, low = [], []
    for value in values:
        vh = value.astype(BF16).astype(F32)
        high.append(jnp.where(at_level, vh, 0.0).astype(BF16))
        low.append(jnp.where(at_level, value - vh, 0.0).astype(BF16))
    left = jnp.concatenate([hot, hot], axis=1)
    right = jnp.concatenate([jnp.concatenate(high, axis=0), jnp.concatenate(low, axis=0)], axis=1)
    return lax.dot_general(left, right, (((1,), (1,)), ((), ())), preferred_element_type=F32)


def sides(mine_ref, count_y):
    mine = mine_ref[0]
    return 1 - 2 * ((mine // count_y) & 1), 1 - 2 * (mine & 1)


def list_blocks(lists, listed):
    total = jnp.int32(0)
    for used, tag in lists:

        def put(j, n, tag=tag):
            listed[n] = tag * 8 + j
            return n + 1

        total = lax.fori_loop(0, (used + 127) >> 7, put, total)
    return total


def gather_lists(table, total, width, listed, direction, cnt_ref, src_ref, w_ref, out_ref):
    for k in range(width - 1):
        listed[total + k] = listed[total - 1]

    def step(i, carry):
        blocks = [listed[width * i + k] for k in range(width)]
        rows = [direction[b >> 3] * 8 + (b & 7) for b in blocks]
        cell = jnp.concatenate([src_ref[pl.ds(r, 1), :] for r in rows], axis=1)
        found = pick(table, cell)
        lane = lax.broadcasted_iota(jnp.int32, (1, 128), 1)
        for k, (b, r) in enumerate(zip(blocks, rows)):
            used = cnt_ref[0, 0, r >> 3]
            j = b & 7
            weight = jnp.where(lane + j * 128 < used, w_ref[pl.ds(r, 1), :], 0.0)
            for c in range(3):
                out_ref[b >> 3, c, pl.ds(j, 1), :] = found[c][:, k * 128 : (k + 1) * 128] * weight
            out_ref[b >> 3, 3, pl.ds(j, 1), :] = weight
        return carry

    lax.fori_loop(0, (total + width - 1) // width, step, 0)


def make_far_gather(count_y, width):
    def kernel(mine_ref, cnt_ref, vel_hbm, src_ref, w_ref, out_ref, table, vel_ref, sem, listed, direction):
        half = vel_ref.shape[1] // 2
        copies = []
        for c in range(3):
            copies.append(pltpu.make_async_copy(vel_hbm.at[c], vel_ref.at[c], sem.at[c]))
            copies[-1].start()
        out_ref[...] = jnp.zeros_like(out_ref)
        side_x, side_y = sides(mine_ref, count_y)
        lists = []
        for s in range(2):
            for t in range(3):
                d = 3 * (side_x * (1 - 2 * s) + 1) + side_y * (1 - t) + 1
                direction[3 * s + t] = d
                lists.append((cnt_ref[0, 0, d], 3 * s + t))
        total = list_blocks(lists, listed)
        for c in range(3):
            copies[c].wait()
            for piece in range(2):
                high, low = halves(vel_ref[c, piece * half : (piece + 1) * half, :])
                table[c, :, piece * 128 : (piece + 1) * 128] = high
                table[c, :, 256 + piece * 128 : 256 + (piece + 1) * 128] = low
        gather_lists(table, total, width, listed, direction, cnt_ref, src_ref, w_ref, out_ref)

    return kernel


def active_turbines(tile_ref, mine, listed):
    turbines = tile_ref.shape[0]
    owned = jnp.where(tile_ref[...] == mine, 1.0, 0.0)
    found = jnp.max(owned, axis=1, keepdims=True)
    total = jnp.int32(0)
    for t in range(turbines):
        listed[total] = t
        total = total + jnp.where(found[t, 0] > 0.5, 1, 0)
    listed[total] = 0
    return total


def make_near_gather(count_y, width):
    def kernel(mine_ref, cnt_ref, table, src_ref, w_ref, tile_ref, cell_ref, out_ref, pts_ref, rot_ref, listed, direction, tlist):
        turbines, points = tile_ref.shape
        out_ref[...] = jnp.zeros_like(out_ref)
        pts_ref[...] = jnp.zeros_like(pts_ref)
        mine = mine_ref[0]
        n_turb = active_turbines(tile_ref, mine, tlist)

        def turbine(i, carry):
            pair = [tlist[2 * i], tlist[2 * i + 1]]
            cell = jnp.concatenate([cell_ref[pl.ds(t, 1), :] for t in pair], axis=1)
            found = pick(table, cell)
            for k, t in enumerate(pair):
                owned = tile_ref[pl.ds(t, 1), :] == mine
                for c in range(3):
                    pts_ref[c, pl.ds(t, 1), :] = jnp.where(owned, found[c][:, k * points : (k + 1) * points], 0.0)
            return carry

        lax.fori_loop(0, (n_turb + 1) >> 1, turbine, 0)
        rot_ref[...] = jnp.zeros_like(rot_ref)
        sums = jnp.sum(pts_ref[0], axis=1, keepdims=True)
        rot_ref[0:turbines, :] = jnp.broadcast_to(sums, (turbines, 128))

        _, side_y = sides(mine_ref, count_y)
        lists = []
        for t in range(3):
            d = 3 + side_y * (1 - t) + 1
            direction[t] = d
            lists.append((cnt_ref[0, 0, d], t))
        total = list_blocks(lists, listed)
        gather_lists(table, total, width, listed, direction, cnt_ref, src_ref, w_ref, out_ref)

    return kernel


def scatter_lists(val, n_lists, direction, dst_ref, listed, acc, extent, place):
    lists = []
    for q in range(n_lists):
        used = jnp.sum(jnp.where(val[q, 3] != 0.0, 1.0, 0.0)).astype(jnp.int32)
        lists.append((used, q))
    total = list_blocks(lists, listed)
    for k in range(3):
        listed[total + k] = 0

    def chunk(i, carry):
        cells, vals = [], [[], [], [], []]
        for k in range(4):
            at = 4 * i + k
            b = listed[at]
            q, j = b >> 3, b & 7
            keep = jnp.where(at < total, 1.0, 0.0)
            cells.append(dst_ref[pl.ds(direction[q] * 8 + j, 1), :])
            for c in range(4):
                vals[c].append(val[q, c, pl.ds(j, 1), :] * keep)
        cell = jnp.concatenate(cells, axis=1)
        vals = [jnp.concatenate(v, axis=1) for v in vals]
        acc[...] += spread(extent, place((cell >> 7) & 511), cell & 127, vals)
        return carry

    lax.fori_loop(0, (total + 3) >> 2, chunk, 0)


def make_first_scatter(count_y):
    def kernel(mine_ref, low_ref, own_ref, high_ref, dst_ref, acc, val, listed, direction):
        side_x, _ = sides(mine_ref, count_y)
        for q, ref in enumerate((low_ref, own_ref, high_ref)):
            val[q] = ref[1]
            direction[q] = 3 * (side_x * (q - 1) + 1) + 1
        acc[...] = jnp.zeros_like(acc)
        scatter_lists(val, 3, direction, dst_ref, listed, acc, 512, lambda row: row)

    return kernel


def load_later_lists(mine_ref, count_y, first_ref, second_ref, val, direction):
    side_x, side_y = sides(mine_ref, count_y)
    for t, ref in enumerate((first_ref, second_ref)):
        for s in range(3):
            q = 3 * t + s
            for c in range(4):
                at = (s * 4 + c) * 8
                val[q, c] = ref[at : at + 8, :]
            direction[q] = 3 * (side_x * (s - 1) + 1) + side_y * (2 * t - 1) + 1


def corrected(acc, vel, c):
    return (1.0 - acc[:, 384:512]) * vel - acc[:, c * 128 : (c + 1) * 128]


def make_outer_scatter(count_y):
    def kernel(mine_ref, base_ref, first_ref, second_ref, dst_ref, vel_ref, cor_ref, fa_ref, fb_ref, acc, val, listed, direction):
        load_later_lists(mine_ref, count_y, first_ref, second_ref, val, direction)
        acc[0:128, :] = base_ref[0:128, :]
        acc[128:256, :] = base_ref[384:512, :]
        place = lambda row: jnp.where(row < 128, row, jnp.where(row >= 384, row - 256, 512))
        scatter_lists(val, 6, direction, dst_ref, listed, acc, 256, place)
        side_x, _ = sides(mine_ref, count_y)
        for c in range(3):
            vel = jnp.concatenate([vel_ref[c, 0:128, :], vel_ref[c, 384:512, :]], axis=0)
            cor = corrected(acc, vel, c)
            cor_ref[c] = cor
            fa_ref[c] = jnp.where(side_x > 0, cor[192:256], cor[0:64])
            fb_ref[c] = jnp.where(side_x > 0, cor[0:64], cor[192:256])

    return kernel


def make_inner_scatter(count_y):
    def kernel(mine_ref, base_ref, first_ref, second_ref, dst_ref, vel_ref, outer_ref, cor_ref, fa_ref, fb_ref, acc, val, listed, direction):
        load_later_lists(mine_ref, count_y, first_ref, second_ref, val, direction)
        acc[...] = base_ref[128:384, :]
        scatter_lists(val, 6, direction, dst_ref, listed, acc, 256, lambda row: row - 128)
        _, side_y = sides(mine_ref, count_y)
        for c in range(3):
            cor_ref[c] = corrected(acc, vel_ref[c, 128:384, :], c)
            for x in range(8):
                ref, at = (cor_ref, x - 2) if 2 <= x < 6 else (outer_ref, x if x < 2 else x - 4)
                low = ref[c, at * 64 : at * 64 + 1, :]
                high = ref[c, at * 64 + 63 : at * 64 + 64, :]
                fa_ref[c, x : x + 1, :] = jnp.where(side_y > 0, high, low)
                fb_ref[c, x : x + 1, :] = jnp.where(side_y > 0, low, high)

    return kernel


def forcing_kernel(mine_ref, tile_ref, cell_ref, coef_ref, pts_ref, rot_ref, out_ref, tlist):
    out_ref[...] = jnp.zeros_like(out_ref)
    n_turb = active_turbines(tile_ref, mine_ref[0], tlist)
    points = tile_ref.shape[1]

    def turbine(i, carry):
        pair = [tlist[2 * i], tlist[2 * i + 1]]
        cell = jnp.concatenate([cell_ref[pl.ds(t, 1), :] for t in pair], axis=1)
        force = [[], [], []]
        for k, t in enumerate(pair):
            keep = jnp.where(2 * i + k < n_turb, 1.0 / points, 0.0)
            scale = -coef_ref[pl.ds(t, 1), :] * (rot_ref[pl.ds(t, 1), 0:1] * keep)
            for c in range(3):
                force[c].append(scale * pts_ref[c, pl.ds(t, 1), :])
        force = [jnp.concatenate(f, axis=1) for f in force]
        got = spread(512, (cell >> 7) & 511, cell & 127, force)
        for c in range(3):
            out_ref[c] += got[:, c * 128 : (c + 1) * 128]
        return carry

    lax.fori_loop(0, (n_turb + 1) >> 1, turbine, 0)


def make_stencil(count_y):
    def kernel(mine_ref, outer_ref, inner_ref, frc_ref, xa_ref, xb_ref, ya_ref, yb_ref, out_hbm, frc_hbm, out_ref, sem):
        side_x, side_y = sides(mine_ref, count_y)
        given = pltpu.make_async_copy(frc_ref, frc_hbm, sem.at[8])
        given.start()
        lane = lax.broadcasted_iota(jnp.int32, (64, 128), 1)

        def slab(c, x):
            if x < 0:
                return jnp.where(side_x > 0, xb_ref[c * 64 : c * 64 + 64, :], xa_ref[c * 64 : c * 64 + 64, :])
            if x > 7:
                return jnp.where(side_x > 0, xa_ref[c * 64 : c * 64 + 64, :], xb_ref[c * 64 : c * 64 + 64, :])
            ref, at = (inner_ref, x - 2) if 2 <= x < 6 else (outer_ref, x if x < 2 else x - 4)
            return ref[c, at * 64 : at * 64 + 64, :]

        copies = []
        for x in range(8):
            now = [slab(c, x) for c in range(3)]
            for c in range(3):
                u = now[c]
                west, east = slab(c, x - 1), slab(c, x + 1)
                ya, yb = ya_ref[c, x : x + 1, :], yb_ref[c, x : x + 1, :]
                south = jnp.concatenate([jnp.where(side_y > 0, yb, ya), u[:-1]], axis=0)
                north = jnp.concatenate([u[1:], jnp.where(side_y > 0, ya, yb)], axis=0)
                upper = jnp.where(lane == 127, 0.0, pltpu.roll(u, 127, 1))
                lower = jnp.where(lane == 0, 0.0, pltpu.roll(u, 1, 1))
                laplace = east + west + north + south + upper + lower - 6.0 * u
                advect = (
                    now[0] * (east - west) * 0.5
                    + now[1] * (north - south) * 0.5
                    + now[2] * (upper - lower) * 0.5
                )
                out_ref[c, x] = u + 0.2 * (0.15 * laplace - advect + frc_ref[c, x * 64 : x * 64 + 64, :])
            copies.append(pltpu.make_async_copy(out_ref.at[:, x], out_hbm.at[:, x], sem.at[x]))
            copies[-1].start()
        for copy in copies:
            copy.wait()
        given.wait()

    return kernel


def swap(value, axis, step):
    count = lax.axis_size(axis)
    return lax.ppermute(value, axis, [(i, i ^ step) for i in range(count)])


def swap_next(value, axis):
    count = lax.axis_size(axis)
    return lax.ppermute(value, axis, [(i, (i - 1 if i % 2 == 0 else i + 1) % count) for i in range(count)])


def call(kernel, name, outs, ins, args, scratch=(), flops=10**9, limit=32):
    return pl.pallas_call(
        kernel,
        out_shape=tuple(jax.ShapeDtypeStruct(shape, dtype) for shape, dtype, _ in outs),
        in_specs=ins,
        out_specs=tuple(spec for _, _, spec in outs),
        scratch_shapes=list(scratch),
        compiler_params=pltpu.CompilerParams(vmem_limit_bytes=limit << 20),
        cost_estimate=pl.CostEstimate(flops=flops, bytes_accessed=10**5, transcendentals=0),
        name=name,
    )(*args)


def body(velocity, counts, src_cell, weights, dst_cell, blade_tile, blade_cell, blade_coef):
    vel = velocity.reshape(3, 512, 128)
    src = src_cell.reshape(72, 128)
    weight = weights.reshape(72, 128)
    dst = dst_cell.reshape(72, 128)
    turbines, points = blade_cell.shape
    count_x, count_y = lax.axis_size("gx"), lax.axis_size("gy")
    mine = (lax.axis_index("gx") * count_y + lax.axis_index("gy")).reshape(1).astype(jnp.int32)
    rows_t = turbines + -turbines % 8
    ints = lambda n: pltpu.SMEM((n,), jnp.int32)

    far, table = call(
        make_far_gather(count_y, 6),
        "far_gather",
        [((6, 4, 8, 128), F32, VMEM), ((3, 256, 512), BF16, VMEM)],
        [SMEM, SMEM, HBM, VMEM, VMEM],
        (mine, counts, vel, src, weight),
        [pltpu.VMEM((3, 512, 128), F32), pltpu.SemaphoreType.DMA((3,)), ints(64), ints(8)],
        flops=5 * 10**9,
    )
    low = swap(far[0:3], "gx", 1)
    high = swap_next(far[3:6], "gx")
    own, pts, rotor = call(
        make_near_gather(count_y, 4),
        "near_gather",
        [((3, 4, 8, 128), F32, VMEM), ((3, turbines, points), F32, VMEM), ((rows_t, 128), F32, VMEM)],
        [SMEM, SMEM] + [VMEM] * 5,
        (mine, counts, table, src, weight, blade_tile, blade_cell),
        [ints(40), ints(8), ints(32)],
        flops=4 * 10**9,
    )
    for axis, count in (("gx", count_x), ("gy", count_y)):
        step = 4
        while step < count:
            rotor = rotor + swap(rotor, axis, step)
            step *= 2

    def y_payload(t):
        parts = [part[t].reshape(32, 128) for part in (low, own, high)]
        return jnp.concatenate(parts + [rotor], axis=0)

    first = swap(y_payload(0), "gy", 1)
    rotor = rotor + first[96:]
    second = swap_next(y_payload(2), "gy")
    (acc,) = call(
        make_first_scatter(count_y),
        "first_scatter",
        [((512, 512), F32, VMEM)],
        [SMEM] + [VMEM] * 4,
        (mine, low, own, high, dst),
        [pltpu.VMEM((3, 4, 8, 128), F32), ints(40), ints(8)],
        flops=4 * 10**9,
    )
    rotor = rotor + second[96:]
    rotor = rotor + swap(rotor, "gx", 2)
    half_scratch = [pltpu.VMEM((256, 512), F32), pltpu.VMEM((6, 4, 8, 128), F32), ints(64), ints(8)]
    outer, fa, fb = call(
        make_outer_scatter(count_y),
        "outer_scatter",
        [((3, 256, 128), F32, VMEM), ((3, 64, 128), F32, VMEM), ((3, 64, 128), F32, VMEM)],
        [SMEM] + [VMEM] * 5,
        (mine, acc, first, second, dst, vel),
        half_scratch,
        flops=4 * 10**9,
    )
    xa = swap(jnp.concatenate([fa.reshape(192, 128), rotor], axis=0), "gx", 1)
    xb = swap_next(fb.reshape(192, 128), "gx")
    inner, fa, fb = call(
        make_inner_scatter(count_y),
        "inner_scatter",
        [((3, 256, 128), F32, VMEM), ((3, 8, 128), F32, VMEM), ((3, 8, 128), F32, VMEM)],
        [SMEM] + [VMEM] * 6,
        (mine, acc, first, second, dst, vel, outer),
        half_scratch,
        flops=4 * 10**9,
    )
    ya = swap(fa, "gy", 1)
    yb = swap_next(fb, "gy")
    rotor = rotor + xa[192:]
    (force,) = call(
        forcing_kernel,
        "forcing",
        [((3, 512, 128), F32, VMEM)],
        [SMEM] + [VMEM] * 5,
        (mine, blade_tile, blade_cell, blade_coef, pts, rotor),
        [ints(32)],
        flops=10**6,
    )
    updated, forcing = call(
        make_stencil(count_y),
        "stencil",
        [((3, 8, 64, 128), F32, HBM), ((3, 512, 128), F32, HBM)],
        [SMEM] + [VMEM] * 7,
        (mine, outer, inner, force, xa, xb, ya, yb),
        [pltpu.VMEM((3, 8, 64, 128), F32), pltpu.SemaphoreType.DMA((9,))],
    )
    return updated, forcing.reshape(velocity.shape)


def solution(mesh):
    grid = P("gx", "gy", None)
    lists = P("gx", "gy", None, None)
    field = P(None, "gx", "gy", None)
    return jax.shard_map(
        body,
        mesh=mesh,
        in_specs=(field, grid, lists, lists, lists, P(), P(), P()),
        out_specs=(field, field),
        check_vma=False,
    )
```

time: 391 us -> 52.2 us (0.13)
  local copies, waits for them, and re-layouts: 175 us -> 4.05 us
  other arithmetic: 159 us -> 0.04 us
  blocking collectives: 38.2 us -> 0 us
  Pallas kernels: 0 us -> 26.6 us
  waiting for transfers between devices: 2.43 us -> 8 us
    scatter-add x2 -> x0, other arithmetic: 100 us -> none  [the longest x1 62.9 us: body(): jnp.zeros((4, total_cells), jnp.float32).at[:, targets]]
    gather x4 -> x0, local copies, waits for them, and re-layouts: 62.3 us -> none  [the longest x2 44.6 us: body(): jnp.take(flat_vel, src_cell[0, 0].reshape(-1), axis=1)]
    sub x2 -> x0, other arithmetic: 54.5 us -> none  [body(): corrected = (1.0 - totals[3]) * flat_vel - totals[:3]]
    slice x3 -> x1, local copies, waits for them, and re-layouts: 52.5 us -> 0.01 us  [body(): high = swap_next(far[3:6], 'gx')]
    reshape x3 -> x0, local copies, waits for them, and re-layouts: 39 us -> none  [the longest x1 19.5 us: body(): field_now = corrected.reshape(components, cells_x, cells_y, levels)]
    psum x1 -> x0, blocking collectives: 38.2 us -> none  [body(): points_x = lax.psum(sampled[0], ('gx', 'gy'))]
    pallas_call x0 -> x7, Pallas kernels: none -> 26.6 us  [call(): pl.pallas_call(kernel, out_shape=tuple((jax.ShapeDtypeStruct(shape, dtype...]
    unnamed x18 -> x22, local copies, waits for them, and re-layouts: 18.1 us -> 4.03 us
  transfers between devices with their start and end apart: 8 -> 10, of which waited for: 2 -> 4; matrix products, arithmetic and copies ran while one was open for 33% -> 0% of each run, Pallas kernels for 0% -> 38%
where the time goes in v2:
time: 52.2 us; the launch traced here: 51.9 us
  Pallas kernels  26.6 us (51%)
  starting transfers between devices  12.4 us (24%)
  waiting for transfers between devices  8 us (15%)
  local copies, waits for them, and re-layouts  4.05 us (8%)
  between operations  0.87 us (2%)
    pallas_call x7, Pallas kernels, call(): pl.pallas_call(kernel, out_shape=tuple((jax.ShapeDtypeStruct(shape, dtype...  26.6 us
    ppermute x4, starting transfers between devices, swap_next(): lax.ppermute(value, axis, [(i, (i - 1 if i % 2 == 0 else i + 1) % count)...  10.4 us
    ppermute x6, waiting for transfers between devices, swap(): return lax.ppermute(value, axis, [(i, i ^ step) for i in range(count)])  5.09 us
    unnamed x22, local copies, waits for them, and re-layouts  4.03 us
    ppermute x4, waiting for transfers between devices, swap_next(): lax.ppermute(value, axis, [(i, (i - 1 if i % 2 == 0 else i + 1) % count)...  2.9 us
    ppermute x6, starting transfers between devices, swap(): return lax.ppermute(value, axis, [(i, i ^ step) for i in range(count)])  2.03 us
  transfers between devices with their start and end apart: 10, of which 4 were waited for; matrix products, arithmetic and copies ran while one was open for 0% of the time, Pallas kernels for 38%

profile of v2, /device:TPU:0, one launch (start us, length us, event | category | flops | bytes accessed | tf_op | source)
XLA Modules:
  0.0 51.9 jit_solution(18293632450730251650)
XLA Ops:
  0.6 0.0 copy-start.10
  0.6 0.6 %copy-done.10 = s32[1,1,9]{2,1,0:T(1,128)S(1)} copy-done((s32[1,1,9]{2,1,0:T(1,128)S(1)}, s32[1,1,9]{2,1,0:T(1,128)}, u32[]{:S(2)}) %copy-start.10) | copy-done | bytes 60
  1.3 0.0 copy-start.3
  1.3 1.1 %copy-done.3 = f32[3,8,64,128]{3,2,1,0:T(8,128)S(1)} copy-done((f32[3,8,64,128]{3,2,1,0:T(8,128)S(1)}, f32[3,8,64,128]{3,2,1,0:T(8,128)}, u32[]{:S(2)}) %copy-start.3) | copy-done | bytes 786456
  2.4 0.0 copy-start.5
  2.4 0.8 %copy-done.5 = s32[1,1,9,1024]{3,1,2,0:T(1,128)S(1)} copy-done((s32[1,1,9,1024]{3,1,2,0:T(1,128)S(1)}, s32[1,1,9,1024]{3,1,2,0:T(1,128)}, u32[]{:S(2)}) %copy-start.5) | copy-done | bytes 36888
  3.2 0.0 copy-start.7
  3.2 0.8 %copy-done.7 = f32[1,1,9,1024]{3,1,2,0:T(1,128)S(1)} copy-done((f32[1,1,9,1024]{3,1,2,0:T(1,128)S(1)}, f32[1,1,9,1024]{3,1,2,0:T(1,128)}, u32[]{:S(2)}) %copy-start.7) | copy-done | bytes 36888
  4.0 5.3 %far_gather.1 = (f32[6,4,8,128]{3,2,1,0:T(8,128)S(1)}, bf16[3,256,512]{2,1,0:T(8,128)(2,1)S(1)}) custom-call(s32[1]{0:T(128)} %bitcast.mine_ref, s32[1,1,9]{2,1,0:T(1,128)S(1)} %copy-done.10, f32[3,512,128]{2,1,0:T(8,128)S(1)} %bitcast.21, s32[72,128]{1,0:T(8,128)S(1)} %bitcast.25, f32[72,128]{1,0:T(8,128)S(1)} %bitcast.27), custom_call_target="tpu_custom_call" | custom-call | flops 5000000000 | bytes 100000 | tf_op jit(solution)/shard_map/far_gather/pallas_call | solution.py:331
  9.3 0.0 copy-start
  9.3 0.0 copy-start.1
  9.3 0.0 copy-start.6
  9.3 0.0 copy-start.8
  9.4 6.9 %collective-permute-start.1 = (f32[3,4,8,128]{3,2,1,0:T(8,128)S(1)}, f32[3,4,8,128]{3,2,1,0:T(8,128)S(1)}, u32[]{:S(2)}, u32[]{:S(2)}) collective-permute-start(f32[3,4,8,128]{3,2,1,0:T(8,128)S(1)} %get-tuple-element.28), channel_id=1, source_target_pairs={{0,28},{4,8},{8,4},{12,16},{16,12},{20,24},{24,20},{28,0},{1,29},{... | collective-permute-start | bytes 147464 | tf_op jit(solution)/shard_map/ppermute | solution.py:327
  16.3 0.0 collective-permute-start
  16.3 0.0 copy-done
  16.3 0.0 copy-done.1
  16.3 0.0 copy-done.6
  16.3 0.0 copy-done.8
  16.3 5.0 %near_gather.1 = (f32[3,4,8,128]{3,2,1,0:T(8,128)S(1)}, f32[3,20,192]{2,1,0:T(8,128)S(1)}, f32[24,128]{1,0:T(8,128)S(1)}) custom-call(s32[1]{0:T(128)} %bitcast.mine_ref, s32[1,1,9]{2,1,0:T(1,128)S(1)} %copy-done.10, bf16[3,256,512]{2,1,0:T(8,128)(2,1)S(1)} %get-tuple-element.16.table, s32[72,128]{1,0:T(8,128)S(1)} %bitcast.26, f32[72,128]{1,0:T(8,128)S(1)} %bitcast.28, ...), custom_call_target="tpu_custom_call" | custom-call | flops 4000000000 | bytes 100000 | tf_op jit(solution)/shard_map/near_gather/pallas_call | solution.py:331
  21.3 0.8 %collective-permute-start.2 = (f32[24,128]{1,0:T(8,128)S(1)}, f32[24,128]{1,0:T(8,128)S(1)}, u32[]{:S(2)}, u32[]{:S(2)}) collective-permute-start(f32[24,128]{1,0:T(8,128)S(1)} %get-tuple-element.18), channel_id=1, source_target_pairs={{0,16},{4,20},{8,24},{12,28},{16,0},{20,4},{24,8},{28,12},{1,17},{... | collective-permute-start | bytes 36872 | tf_op jit(solution)/shard_map/ppermute | solution.py:322
  22.1 3.8 %collective-permute-done.2 = f32[24,128]{1,0:T(8,128)S(1)} collective-permute-done((f32[24,128]{1,0:T(8,128)S(1)}, f32[24,128]{1,0:T(8,128)S(1)}, u32[]{:S(2)}, u32[]{:S(2)}) %collective-permute-start.2) | collective-permute-done | bytes 12320 | tf_op jit(solution)/shard_map/ppermute | solution.py:322
  26.0 0.0 collective-permute-done.1.high_ref
  26.0 0.0 collective-permute-done.low_ref
  26.0 0.1 collective-permute-start.3
  26.1 1.2 %collective-permute-done.3.first_ref = f32[120,128]{1,0:T(8,128)S(1)} collective-permute-done((f32[120,128]{1,0:T(8,128)S(1)}, f32[120,128]{1,0:T(8,128)S(1)}, u32[]{:S(2)}, u32[]{:S(2)}) %collective-permute-start.3) | collective-permute-done | bytes 61472 | tf_op jit(solution)/shard_map/ppermute | solution.py:322
  27.4 0.0 copy-start.9
  27.4 0.1 collective-permute-start.4
  27.5 0.7 %copy-done.9 = s32[1,1,9,1024]{3,1,2,0:T(1,128)S(1)} copy-done((s32[1,1,9,1024]{3,1,2,0:T(1,128)S(1)}, s32[1,1,9,1024]{3,1,2,0:T(1,128)}, u32[]{:S(2)}) %copy-start.9) | copy-done | bytes 36888
  28.1 0.0 copy-start.4
  28.1 2.4 %first_scatter.1.base_ref = f32[512,512]{1,0:T(8,128)S(1)} custom-call(s32[1]{0:T(128)} %bitcast.mine_ref, f32[3,4,8,128]{3,2,1,0:T(8,128)S(1)} %collective-permute-done.low_ref, f32[3,4,8,128]{3,2,1,0:T(8,128)S(1)} %get-tuple-element.17.own_ref, f32[3,4,8,128]{3,2,1,0:T(8,128)S(1)} %collective-permute-done.1.high_ref, s32[72,128]{1,0:T(8,128)S(1)} %bitcast.29), custom_call_target="tpu_custom_call" | custom-call | flops 4000000000 | bytes 100000 | tf_op jit(solution)/shard_map/first_scatter/pallas_call | solution.py:331
  30.6 0.8 %collective-permute-done.4.second_ref = f32[120,128]{1,0:T(8,128)S(1)} collective-permute-done((f32[120,128]{1,0:T(8,128)S(1)}, f32[120,128]{1,0:T(8,128)S(1)}, u32[]{:S(2)}, u32[]{:S(2)}) %collective-permute-start.4) | collective-permute-done | bytes 61472 | tf_op jit(solution)/shard_map/ppermute | solution.py:327
  31.4 0.0 collective-permute-start.5
  31.4 0.0 copy-done.4
  31.4 4.9 %outer_scatter.1 = (f32[3,256,128]{2,1,0:T(8,128)S(1)}, f32[3,64,128]{2,1,0:T(8,128)S(1)}, f32[3,64,128]{2,1,0:T(8,128)S(1)}) custom-call(s32[1]{0:T(128)} %bitcast.mine_ref, f32[512,512]{1,0:T(8,128)S(1)} %first_scatter.1.base_ref, f32[120,128]{1,0:T(8,128)S(1)} %collective-permute-done.3.first_ref, f32[120,128]{1,0:T(8,128)S(1)} %collective-permute-done.4.second_ref, ...), custom_call_target="tpu_custom_call" | custom-call | flops 4000000000 | bytes 100000 | tf_op jit(solution)/shard_map/outer_scatter/pallas_call | solution.py:331
  36.3 0.0 collective-permute-done.5
  36.4 1.1 %collective-permute-start.6 = (f32[216,128]{1,0:T(8,128)S(1)}, f32[216,128]{1,0:T(8,128)S(1)}, u32[]{:S(2)}, u32[]{:S(2)}) collective-permute-start(f32[216,128]{1,0:T(8,128)S(1)} %pad_maximum_fusion), channel_id=1, source_target_pairs={{0,4},{4,0},{8,12},{12,8},{16,20},{20,16},{24,28},{28,24},{1,5},{5... | collective-permute-start | bytes 331784 | tf_op jit(solution)/shard_map/ppermute | solution.py:322
  37.4 5.0 %inner_scatter.1 = (f32[3,256,128]{2,1,0:T(8,128)S(1)}, f32[3,8,128]{2,1,0:T(8,128)S(1)}, f32[3,8,128]{2,1,0:T(8,128)S(1)}) custom-call(s32[1]{0:T(128)} %bitcast.mine_ref, f32[512,512]{1,0:T(8,128)S(1)} %first_scatter.1.base_ref, f32[120,128]{1,0:T(8,128)S(1)} %collective-permute-done.3.first_ref, f32[120,128]{1,0:T(8,128)S(1)} %collective-permute-done.4.second_ref, ...), custom_call_target="tpu_custom_call" | custom-call | flops 4000000000 | bytes 100000 | tf_op jit(solution)/shard_map/inner_scatter/pallas_call | solution.py:331
  42.4 0.0 copy-start.2
  42.4 0.1 collective-permute-start.8
  42.5 0.1 collective-permute-start.9
  42.6 3.3 %collective-permute-start.7 = (f32[192,128]{1,0:T(8,128)S(1)}, f32[192,128]{1,0:T(8,128)S(1)}, u32[]{:S(2)}, u32[]{:S(2)}) collective-permute-start(f32[192,128]{1,0:T(8,128)S(1)} %bitcast.24), channel_id=1, source_target_pairs={{0,28},{4,8},{8,4},{12,16},{16,12},{20,24},{24,20},{28,0},{1,29},{... | collective-permute-start | bytes 294920 | tf_op jit(solution)/shard_map/ppermute | solution.py:327
  45.9 0.0 collective-permute-done.6.xa_ref
  45.9 0.0 copy-done.2
  45.9 2.4 %forcing.1.frc_ref = f32[3,512,128]{2,1,0:T(8,128)S(1)} custom-call(s32[1]{0:T(128)} %bitcast.mine_ref, s32[20,192]{1,0:T(8,128)S(1)} %copy-done, s32[20,192]{1,0:T(8,128)S(1)} %copy-done.1, f32[20,192]{1,0:T(8,128)S(1)} %copy-done.2, f32[3,20,192]{2,1,0:T(8,128)S(1)} %get-tuple-element.21.pts_ref, f32[24,128]{1,0:T(8,128)S(1)} %slice_add_fusion.rot_ref), custom_call_target="tpu_custom_call" | custom-call | flops 1000000 | bytes 100000 | tf_op jit(solution)/shard_map/forcing/pallas_call | solution.py:331
  48.3 0.0 collective-permute-done.8.ya_ref
  48.3 0.0 collective-permute-done.9.yb_ref
  48.3 2.1 %collective-permute-done.7.xb_ref = f32[192,128]{1,0:T(8,128)S(1)} collective-permute-done((f32[192,128]{1,0:T(8,128)S(1)}, f32[192,128]{1,0:T(8,128)S(1)}, u32[]{:S(2)}, u32[]{:S(2)}) %collective-permute-start.7) | collective-permute-done | bytes 98336 | tf_op jit(solution)/shard_map/ppermute | solution.py:327
  50.4 1.5 %stencil.1 = (f32[3,8,64,128]{3,2,1,0:T(8,128)}, f32[3,512,128]{2,1,0:T(8,128)}) custom-call(s32[1]{0:T(128)} %bitcast.mine_ref, f32[3,256,128]{2,1,0:T(8,128)S(1)} %get-tuple-element.19.outer_ref, f32[3,256,128]{2,1,0:T(8,128)S(1)} %get-tuple-element.20.inner_ref, f32[3,512,128]{2,1,0:T(8,128)S(1)} %forcing.1.frc_ref, ...), custom_call_target="tpu_custom_call" | custom-call | flops 1000000000 | bytes 100000 | tf_op jit(solution)/shard_map/stencil/pallas_call | solution.py:331
  (12 shorter events, 0.1 us)
Async XLA Ops:
  0.6 0.7 %copy-start.10 = (s32[1,1,9]{2,1,0:T(1,128)S(1)}, s32[1,1,9]{2,1,0:T(1,128)}, u32[]{:S(2)}) copy-start(s32[1,1,9]{2,1,0:T(1,128)} %cnt_ref.3) | copy-start | bytes 112
  1.3 1.1 %copy-start.3 = (f32[3,8,64,128]{3,2,1,0:T(8,128)S(1)}, f32[3,8,64,128]{3,2,1,0:T(8,128)}, u32[]{:S(2)}) copy-start(f32[3,8,64,128]{3,2,1,0:T(8,128)} %param.8) | copy-start | bytes 2359300
  2.4 0.8 %copy-start.5 = (s32[1,1,9,1024]{3,1,2,0:T(1,128)S(1)}, s32[1,1,9,1024]{3,1,2,0:T(1,128)}, u32[]{:S(2)}) copy-start(s32[1,1,9,1024]{3,1,2,0:T(1,128)} %param.10) | copy-start | bytes 110596
  3.2 0.8 %copy-start.7 = (f32[1,1,9,1024]{3,1,2,0:T(1,128)S(1)}, f32[1,1,9,1024]{3,1,2,0:T(1,128)}, u32[]{:S(2)}) copy-start(f32[1,1,9,1024]{3,1,2,0:T(1,128)} %param.11) | copy-start | bytes 110596
  9.3 7.0 %copy-start = (s32[20,192]{1,0:T(8,128)S(1)}, s32[20,192]{1,0:T(8,128)}, u32[]{:S(2)}) copy-start(s32[20,192]{1,0:T(8,128)} %tile_ref.3) | copy-start | bytes 46084
  9.3 7.0 %copy-start.1 = (s32[20,192]{1,0:T(8,128)S(1)}, s32[20,192]{1,0:T(8,128)}, u32[]{:S(2)}) copy-start(s32[20,192]{1,0:T(8,128)} %cell_ref.3) | copy-start | bytes 46084
  9.3 7.0 %copy-start.6 = (s32[1,1,9,1024]{3,1,2,0:T(1,128)S(1)}, s32[1,1,9,1024]{3,1,2,0:T(1,128)}, u32[]{:S(2)}) copy-start(s32[1,1,9,1024]{3,1,2,0:T(1,128)} %param.10) | copy-start | bytes 110596
  9.3 7.0 %copy-start.8 = (f32[1,1,9,1024]{3,1,2,0:T(1,128)S(1)}, f32[1,1,9,1024]{3,1,2,0:T(1,128)}, u32[]{:S(2)}) copy-start(f32[1,1,9,1024]{3,1,2,0:T(1,128)} %param.11) | copy-start | bytes 110596
  9.4 16.6 %collective-permute-start.1 = (f32[3,4,8,128]{3,2,1,0:T(8,128)S(1)}, f32[3,4,8,128]{3,2,1,0:T(8,128)S(1)}, u32[]{:S(2)}, u32[]{:S(2)}) collective-permute-start(f32[3,4,8,128]{3,2,1,0:T(8,128)S(1)} %get-tuple-element.28), channel_id=1, source_target_pairs={{0,28},{4,8},{8,4},{12,16},{16,12},{20,24},{24,20},{28,0},{1,29},{... | collective-permute-start | bytes 147464 | tf_op jit(solution)/shard_map/ppermute | solution.py:327
  16.3 9.7 %collective-permute-start = (f32[3,4,8,128]{3,2,1,0:T(8,128)S(1)}, f32[3,4,8,128]{3,2,1,0:T(8,128)S(1)}, u32[]{:S(2)}, u32[]{:S(2)}) collective-permute-start(f32[3,4,8,128]{3,2,1,0:T(8,128)S(1)} %get-tuple-element.29), channel_id=1, source_target_pairs={{0,4},{4,0},{8,12},{12,8},{16,20},{20,16},{24,28},{28,24},{1,5},{5... | collective-permute-start | bytes 147464 | tf_op jit(solution)/shard_map/ppermute | solution.py:322
  21.3 4.7 %collective-permute-start.2 = (f32[24,128]{1,0:T(8,128)S(1)}, f32[24,128]{1,0:T(8,128)S(1)}, u32[]{:S(2)}, u32[]{:S(2)}) collective-permute-start(f32[24,128]{1,0:T(8,128)S(1)} %get-tuple-element.18), channel_id=1, source_target_pairs={{0,16},{4,20},{8,24},{12,28},{16,0},{20,4},{24,8},{28,12},{1,17},{... | collective-permute-start | bytes 36872 | tf_op jit(solution)/shard_map/ppermute | solution.py:322
  26.0 1.3 %collective-permute-start.3 = (f32[120,128]{1,0:T(8,128)S(1)}, f32[120,128]{1,0:T(8,128)S(1)}, u32[]{:S(2)}, u32[]{:S(2)}) collective-permute-start(f32[120,128]{1,0:T(8,128)S(1)} %pad_maximum_fusion.1), channel_id=1, source_target_pairs={{0,1},{1,0},{2,3},{3,2},{4,5},{5,4},{6,7},{7,6},{8,9},{9,8},{10,11... | collective-permute-start | bytes 184328 | tf_op jit(solution)/shard_map/ppermute | solution.py:322
  27.4 0.8 %copy-start.9 = (s32[1,1,9,1024]{3,1,2,0:T(1,128)S(1)}, s32[1,1,9,1024]{3,1,2,0:T(1,128)}, u32[]{:S(2)}) copy-start(s32[1,1,9,1024]{3,1,2,0:T(1,128)} %param.12) | copy-start | bytes 110596
  27.4 4.0 %collective-permute-start.4 = (f32[120,128]{1,0:T(8,128)S(1)}, f32[120,128]{1,0:T(8,128)S(1)}, u32[]{:S(2)}, u32[]{:S(2)}) collective-permute-start(f32[120,128]{1,0:T(8,128)S(1)} %pad_maximum_fusion.2), channel_id=1, source_target_pairs={{0,3},{1,2},{2,1},{3,0},{4,7},{5,6},{6,5},{7,4},{8,11},{9,10},{10,... | collective-permute-start | bytes 184328 | tf_op jit(solution)/shard_map/ppermute | solution.py:327
  28.1 3.3 %copy-start.4 = (f32[3,8,64,128]{3,2,1,0:T(8,128)S(1)}, f32[3,8,64,128]{3,2,1,0:T(8,128)}, u32[]{:S(2)}) copy-start(f32[3,8,64,128]{3,2,1,0:T(8,128)} %param.8) | copy-start | bytes 2359300
  31.4 4.9 %collective-permute-start.5 = (f32[24,128]{1,0:T(8,128)S(1)}, f32[24,128]{1,0:T(8,128)S(1)}, u32[]{:S(2)}, u32[]{:S(2)}) collective-permute-start(f32[24,128]{1,0:T(8,128)S(1)} %slice_add_fusion.1), channel_id=1, source_target_pairs={{0,8},{4,12},{8,0},{12,4},{16,24},{20,28},{24,16},{28,20},{1,9},{5... | collective-permute-start | bytes 36872 | tf_op jit(solution)/shard_map/ppermute | solution.py:322
  36.4 9.5 %collective-permute-start.6 = (f32[216,128]{1,0:T(8,128)S(1)}, f32[216,128]{1,0:T(8,128)S(1)}, u32[]{:S(2)}, u32[]{:S(2)}) collective-permute-start(f32[216,128]{1,0:T(8,128)S(1)} %pad_maximum_fusion), channel_id=1, source_target_pairs={{0,4},{4,0},{8,12},{12,8},{16,20},{20,16},{24,28},{28,24},{1,5},{5... | collective-permute-start | bytes 331784 | tf_op jit(solution)/shard_map/ppermute | solution.py:322
  42.4 3.5 %copy-start.2 = (f32[20,192]{1,0:T(8,128)S(1)}, f32[20,192]{1,0:T(8,128)}, u32[]{:S(2)}) copy-start(f32[20,192]{1,0:T(8,128)} %coef_ref.1) | copy-start | bytes 46084
  42.4 5.9 %collective-permute-start.8 = (f32[3,8,128]{2,1,0:T(8,128)S(1)}, f32[3,8,128]{2,1,0:T(8,128)S(1)}, u32[]{:S(2)}, u32[]{:S(2)}) collective-permute-start(f32[3,8,128]{2,1,0:T(8,128)S(1)} %get-tuple-element.24), channel_id=1, source_target_pairs={{0,1},{1,0},{2,3},{3,2},{4,5},{5,4},{6,7},{7,6},{8,9},{9,8},{10,11... | collective-permute-start | bytes 36872 | tf_op jit(solution)/shard_map/ppermute | solution.py:322
  42.5 5.8 %collective-permute-start.9 = (f32[3,8,128]{2,1,0:T(8,128)S(1)}, f32[3,8,128]{2,1,0:T(8,128)S(1)}, u32[]{:S(2)}, u32[]{:S(2)}) collective-permute-start(f32[3,8,128]{2,1,0:T(8,128)S(1)} %get-tuple-element.25), channel_id=1, source_target_pairs={{0,3},{1,2},{2,1},{3,0},{4,7},{5,6},{6,5},{7,4},{8,11},{9,10},{10,... | collective-permute-start | bytes 36872 | tf_op jit(solution)/shard_map/ppermute | solution.py:327
  42.6 7.8 %collective-permute-start.7 = (f32[192,128]{1,0:T(8,128)S(1)}, f32[192,128]{1,0:T(8,128)S(1)}, u32[]{:S(2)}, u32[]{:S(2)}) collective-permute-start(f32[192,128]{1,0:T(8,128)S(1)} %bitcast.24), channel_id=1, source_target_pairs={{0,28},{4,8},{8,4},{12,16},{16,12},{20,24},{24,20},{28,0},{1,29},{... | collective-permute-start | bytes 294920 | tf_op jit(solution)/shard_map/ppermute | solution.py:327

commit v3 on v2

--- a/solution.py
+++ b/solution.py
@@ -9,7 +9,7 @@
 BF16 = jnp.bfloat16
 VMEM = pl.BlockSpec(memory_space=pltpu.VMEM)
 SMEM = pl.BlockSpec(memory_space=pltpu.SMEM)
-HBM = pl.BlockSpec(memory_space=pl.ANY)
+HBM = pl.BlockSpec(memory_space=pltpu.HBM)
 
 
 def halves(value):
@@ -89,13 +89,16 @@
 
 
 def make_far_gather(count_y, width):
-    def kernel(mine_ref, cnt_ref, vel_hbm, src_ref, w_ref, out_ref, table, vel_ref, sem, listed, direction):
+    def kernel(mine_ref, cnt_hbm, vel_hbm, src_hbm, w_hbm, dst_hbm, out_ref, table, vel_ref, src_ref, w_ref, dst_ref, sem, cnt_ref, listed, direction):
         half = vel_ref.shape[1] // 2
-        copies = []
-        for c in range(3):
-            copies.append(pltpu.make_async_copy(vel_hbm.at[c], vel_ref.at[c], sem.at[c]))
-            copies[-1].start()
+        pairs = [(cnt_hbm, cnt_ref), (src_hbm, src_ref)]
+        pairs += [(vel_hbm.at[c], vel_ref.at[c]) for c in range(3)]
+        pairs += [(w_hbm, w_ref), (dst_hbm, dst_ref)]
+        copies = [pltpu.make_async_copy(a, b, sem.at[k]) for k, (a, b) in enumerate(pairs)]
+        for copy in copies:
+            copy.start()
         out_ref[...] = jnp.zeros_like(out_ref)
+        copies[0].wait()
         side_x, side_y = sides(mine_ref, count_y)
         lists = []
         for s in range(2):
@@ -104,13 +107,16 @@
                 direction[3 * s + t] = d
                 lists.append((cnt_ref[0, 0, d], 3 * s + t))
         total = list_blocks(lists, listed)
+        copies[1].wait()
         for c in range(3):
-            copies[c].wait()
+            copies[2 + c].wait()
             for piece in range(2):
                 high, low = halves(vel_ref[c, piece * half : (piece + 1) * half, :])
                 table[c, :, piece * 128 : (piece + 1) * 128] = high
                 table[c, :, 256 + piece * 128 : 256 + (piece + 1) * 128] = low
+        copies[5].wait()
         gather_lists(table, total, width, listed, direction, cnt_ref, src_ref, w_ref, out_ref)
+        copies[6].wait()
 
     return kernel
 
@@ -127,29 +133,31 @@
     return total
 
 
+def points_kernel(mine_ref, table, tile_ref, cell_ref, pts_ref, rot_ref, tlist):
+    turbines, points = tile_ref.shape
+    pts_ref[...] = jnp.zeros_like(pts_ref)
+    mine = mine_ref[0]
+    n_turb = active_turbines(tile_ref, mine, tlist)
+
+    def turbine(i, carry):
+        pair = [tlist[2 * i], tlist[2 * i + 1]]
+        cell = jnp.concatenate([cell_ref[pl.ds(t, 1), :] for t in pair], axis=1)
+        found = pick(table, cell)
+        for k, t in enumerate(pair):
+            owned = tile_ref[pl.ds(t, 1), :] == mine
+            for c in range(3):
+                pts_ref[c, pl.ds(t, 1), :] = jnp.where(owned, found[c][:, k * points : (k + 1) * points], 0.0)
+        return carry
+
+    lax.fori_loop(0, (n_turb + 1) >> 1, turbine, 0)
+    rot_ref[...] = jnp.zeros_like(rot_ref)
+    sums = jnp.sum(pts_ref[0], axis=1, keepdims=True)
+    rot_ref[0:turbines, :] = jnp.broadcast_to(sums, (turbines, 128))
+
+
 def make_near_gather(count_y, width):
-    def kernel(mine_ref, cnt_ref, table, src_ref, w_ref, tile_ref, cell_ref, out_ref, pts_ref, rot_ref, listed, direction, tlist):
-        turbines, points = tile_ref.shape
+    def kernel(mine_ref, cnt_ref, table, src_ref, w_ref, out_ref, listed, direction):
         out_ref[...] = jnp.zeros_like(out_ref)
-        pts_ref[...] = jnp.zeros_like(pts_ref)
-        mine = mine_ref[0]
-        n_turb = active_turbines(tile_ref, mine, tlist)
-
-        def turbine(i, carry):
-            pair = [tlist[2 * i], tlist[2 * i + 1]]
-            cell = jnp.concatenate([cell_ref[pl.ds(t, 1), :] for t in pair], axis=1)
-            found = pick(table, cell)
-            for k, t in enumerate(pair):
-                owned = tile_ref[pl.ds(t, 1), :] == mine
-                for c in range(3):
-                    pts_ref[c, pl.ds(t, 1), :] = jnp.where(owned, found[c][:, k * points : (k + 1) * points], 0.0)
-            return carry
-
-        lax.fori_loop(0, (n_turb + 1) >> 1, turbine, 0)
-        rot_ref[...] = jnp.zeros_like(rot_ref)
-        sums = jnp.sum(pts_ref[0], axis=1, keepdims=True)
-        rot_ref[0:turbines, :] = jnp.broadcast_to(sums, (turbines, 128))
-
         _, side_y = sides(mine_ref, count_y)
         lists = []
         for t in range(3):
@@ -351,24 +359,34 @@
     rows_t = turbines + -turbines % 8
     ints = lambda n: pltpu.SMEM((n,), jnp.int32)
 
-    far, table = call(
+    whole = ((72, 128), jnp.int32, VMEM)
+    far, table, vel, src, weight, dst = call(
         make_far_gather(count_y, 6),
         "far_gather",
-        [((6, 4, 8, 128), F32, VMEM), ((3, 256, 512), BF16, VMEM)],
-        [SMEM, SMEM, HBM, VMEM, VMEM],
-        (mine, counts, vel, src, weight),
-        [pltpu.VMEM((3, 512, 128), F32), pltpu.SemaphoreType.DMA((3,)), ints(64), ints(8)],
+        [((6, 4, 8, 128), F32, VMEM), ((3, 256, 512), BF16, VMEM), ((3, 512, 128), F32, VMEM), whole, ((72, 128), F32, VMEM), whole],
+        [SMEM] + [HBM] * 5,
+        (mine, counts, vel, src, weight, dst),
+        [pltpu.SemaphoreType.DMA((7,)), pltpu.SMEM((1, 1, 9), jnp.int32), ints(64), ints(8)],
         flops=5 * 10**9,
     )
     low = swap(far[0:3], "gx", 1)
     high = swap_next(far[3:6], "gx")
-    own, pts, rotor = call(
+    pts, rotor = call(
+        points_kernel,
+        "points",
+        [((3, turbines, points), F32, VMEM), ((rows_t, 128), F32, VMEM)],
+        [SMEM] + [VMEM] * 3,
+        (mine, table, blade_tile, blade_cell),
+        [ints(32)],
+        flops=10**9,
+    )
+    (own,) = call(
         make_near_gather(count_y, 4),
         "near_gather",
-        [((3, 4, 8, 128), F32, VMEM), ((3, turbines, points), F32, VMEM), ((rows_t, 128), F32, VMEM)],
-        [SMEM, SMEM] + [VMEM] * 5,
-        (mine, counts, table, src, weight, blade_tile, blade_cell),
-        [ints(40), ints(8), ints(32)],
+        [((3, 4, 8, 128), F32, VMEM)],
+        [SMEM, SMEM] + [VMEM] * 3,
+        (mine, counts, table, src, weight),
+        [ints(40), ints(8)],
         flops=4 * 10**9,
     )
     for axis, count in (("gx", count_x), ("gy", count_y)):
@@ -416,9 +434,9 @@
         half_scratch,
         flops=4 * 10**9,
     )
+    rotor, xb, fa, fb = lax.optimization_barrier((rotor + xa[192:], xb, fa, fb))
     ya = swap(fa, "gy", 1)
     yb = swap_next(fb, "gy")
-    rotor = rotor + xa[192:]
     (force,) = call(
         forcing_kernel,
         "forcing",

time: 52.2 us -> 46.8 us (0.90)
  Pallas kernels: 26.6 us -> 20.5 us
  starting transfers between devices: 12.4 us -> 15 us
  waiting for transfers between devices: 8 us -> 6.23 us
    pallas_call x7 -> x8, Pallas kernels: 26.6 us -> 20.5 us  [call(): pl.pallas_call(kernel, out_shape=tuple((jax.ShapeDtypeStruct(shape, dtype...]
    ppermute x6, starting transfers between devices: 2.03 us -> 5.58 us  [swap(): return lax.ppermute(value, axis, [(i, i ^ step) for i in range(count)])]
    ppermute x6, waiting for transfers between devices: 5.09 us -> 2.8 us  [swap(): return lax.ppermute(value, axis, [(i, i ^ step) for i in range(count)])]
    ppermute x4, starting transfers between devices: 10.4 us -> 9.47 us  [swap_next(): lax.ppermute(value, axis, [(i, (i - 1 if i % 2 == 0 else i + 1) % count)...]
    ppermute x4, waiting for transfers between devices: 2.9 us -> 3.43 us  [swap_next(): lax.ppermute(value, axis, [(i, (i - 1 if i % 2 == 0 else i + 1) % count)...]
    unnamed x22 -> x16, local copies, waits for them, and re-layouts: 4.03 us -> 4.1 us
  transfers between devices with their start and end apart: 10 -> 10, of which waited for: 4 -> 4; matrix products, arithmetic and copies ran while one was open for 0% -> 0% of each run, Pallas kernels for 38% -> 29%
where the time goes in v3:
time: 46.8 us
  Pallas kernels  20.5 us (44%)
  starting transfers between devices  15 us (32%)
  waiting for transfers between devices  6.23 us (13%)
  local copies, waits for them, and re-layouts  4.12 us (9%)
  between operations  0.81 us (2%)
    pallas_call x8, Pallas kernels, call(): pl.pallas_call(kernel, out_shape=tuple((jax.ShapeDtypeStruct(shape, dtype...  20.5 us
    ppermute x4, starting transfers between devices, swap_next(): lax.ppermute(value, axis, [(i, (i - 1 if i % 2 == 0 else i + 1) % count)...  9.47 us
    ppermute x6, starting transfers between devices, swap(): return lax.ppermute(value, axis, [(i, i ^ step) for i in range(count)])  5.58 us
    unnamed x16, local copies, waits for them, and re-layouts  4.1 us
    ppermute x4, waiting for transfers between devices, swap_next(): lax.ppermute(value, axis, [(i, (i - 1 if i % 2 == 0 else i + 1) % count)...  3.43 us
    ppermute x6, waiting for transfers between devices, swap(): return lax.ppermute(value, axis, [(i, i ^ step) for i in range(count)])  2.8 us
  transfers between devices with their start and end apart: 10, of which 4 were waited for; matrix products, arithmetic and copies ran while one was open for 0% of the time, Pallas kernels for 29%

profile of v3, /device:TPU:0, one launch (start us, length us, event | category | flops | bytes accessed | tf_op | source)
XLA Modules:
  0.0 46.8 jit_solution(2117314946158878235)
XLA Ops:
  0.6 0.0 copy-start.7
  0.6 0.6 %copy-done.7 = s32[1,1,9]{2,1,0:T(1,128)S(1)} copy-done((s32[1,1,9]{2,1,0:T(1,128)S(1)}, s32[1,1,9]{2,1,0:T(1,128)}, u32[]{:S(2)}) %copy-start.7) | copy-done | bytes 60
  1.3 0.0 copy-start.3
  1.3 1.1 %copy-done.3 = f32[3,8,64,128]{3,2,1,0:T(8,128)S(1)} copy-done((f32[3,8,64,128]{3,2,1,0:T(8,128)S(1)}, f32[3,8,64,128]{3,2,1,0:T(8,128)}, u32[]{:S(2)}) %copy-start.3) | copy-done | bytes 786456
  2.4 0.0 copy-start.4
  2.4 0.8 %copy-done.4 = s32[1,1,9,1024]{3,1,2,0:T(1,128)S(1)} copy-done((s32[1,1,9,1024]{3,1,2,0:T(1,128)S(1)}, s32[1,1,9,1024]{3,1,2,0:T(1,128)}, u32[]{:S(2)}) %copy-start.4) | copy-done | bytes 36888
  3.2 0.0 copy-start.5
  3.2 0.8 %copy-done.5 = f32[1,1,9,1024]{3,1,2,0:T(1,128)S(1)} copy-done((f32[1,1,9,1024]{3,1,2,0:T(1,128)S(1)}, f32[1,1,9,1024]{3,1,2,0:T(1,128)}, u32[]{:S(2)}) %copy-start.5) | copy-done | bytes 36888
  4.0 0.0 copy-start.6
  4.0 0.8 %copy-done.6 = s32[1,1,9,1024]{3,1,2,0:T(1,128)S(1)} copy-done((s32[1,1,9,1024]{3,1,2,0:T(1,128)S(1)}, s32[1,1,9,1024]{3,1,2,0:T(1,128)}, u32[]{:S(2)}) %copy-start.6) | copy-done | bytes 36888
  4.7 0.0 copy-start
  4.7 0.0 copy-start.1
  4.7 4.3 %far_gather.1 = (f32[6,4,8,128]{3,2,1,0:T(8,128)S(1)}, bf16[3,256,512]{2,1,0:T(8,128)(2,1)S(1)}, f32[3,512,128]{2,1,0:T(8,128)S(1)}, s32[72,128]{1,0:T(8,128)S(1...) custom-call(s32[1]{0:T(128)} %bitcast.mine_ref, s32[1,1,9]{2,1,0:T(1,128)S(1)} %copy-done.7, ...), custom_call_target="tpu_custom_call" | custom-call | flops 5000000000 | bytes 100000 | tf_op jit(solution)/shard_map/far_gather/pallas_call | solution.py:339
  9.1 0.0 copy-done
  9.1 0.0 copy-done.1
  9.1 1.0 %points.1 = (f32[3,20,192]{2,1,0:T(8,128)S(1)}, f32[24,128]{1,0:T(8,128)S(1)}) custom-call(s32[1]{0:T(128)} %bitcast.mine_ref, bf16[3,256,512]{2,1,0:T(8,128)(2,1)S(1)} %get-tuple-element.23.table, s32[20,192]{1,0:T(8,128)S(1)} %copy-done, s32[20,192]{1,0:T(8,128)S(1)} %copy-done.1), custom_call_target="tpu_custom_call" | custom-call | flops 1000000000 | bytes 100000 | tf_op jit(solution)/shard_map/points/pallas_call | solution.py:339
  10.1 5.1 %collective-permute-start.2 = (f32[24,128]{1,0:T(8,128)S(1)}, f32[24,128]{1,0:T(8,128)S(1)}, u32[]{:S(2)}, u32[]{:S(2)}) collective-permute-start(f32[24,128]{1,0:T(8,128)S(1)} %get-tuple-element.27), channel_id=1, source_target_pairs={{0,16},{4,20},{8,24},{12,28},{16,0},{20,4},{24,8},{28,12},{1,17},{... | collective-permute-start | bytes 36872 | tf_op jit(solution)/shard_map/ppermute | solution.py:330
  15.2 1.3 %collective-permute-start.1 = (f32[3,4,8,128]{3,2,1,0:T(8,128)S(1)}, f32[3,4,8,128]{3,2,1,0:T(8,128)S(1)}, u32[]{:S(2)}, u32[]{:S(2)}) collective-permute-start(f32[3,4,8,128]{3,2,1,0:T(8,128)S(1)} %get-tuple-element.42), channel_id=1, source_target_pairs={{0,28},{4,8},{8,4},{12,16},{16,12},{20,24},{24,20},{28,0},{1,29},{... | collective-permute-start | bytes 147464 | tf_op jit(solution)/shard_map/ppermute | solution.py:335
  16.5 0.0 collective-permute-start
  16.5 2.6 %near_gather.1.own_ref = f32[3,4,8,128]{3,2,1,0:T(8,128)S(1)} custom-call(s32[1]{0:T(128)} %bitcast.mine_ref, s32[1,1,9]{2,1,0:T(1,128)S(1)} %copy-done.7, bf16[3,256,512]{2,1,0:T(8,128)(2,1)S(1)} %get-tuple-element.23.table, s32[72,128]{1,0:T(8,128)S(1)} %get-tuple-element.24.src_ref, f32[72,128]{1,0:T(8,128)S(1)} %get-tuple-element.25.w_ref), custom_call_target="tpu_custom_call" | custom-call | flops 4000000000 | bytes 100000 | tf_op jit(solution)/shard_map/near_gather/pallas_call | solution.py:339
  19.1 0.0 collective-permute-done.2
  19.1 2.9 %collective-permute-done.1.high_ref = f32[3,4,8,128]{3,2,1,0:T(8,128)S(1)} collective-permute-done((f32[3,4,8,128]{3,2,1,0:T(8,128)S(1)}, f32[3,4,8,128]{3,2,1,0:T(8,128)S(1)}, u32[]{:S(2)}, u32[]{:S(2)}) %collective-permute-start.1) | collective-permute-done | bytes 49184 | tf_op jit(solution)/shard_map/ppermute | solution.py:335
  22.0 0.0 collective-permute-done.low_ref
  22.1 0.4 collective-permute-start.3
  22.4 1.0 %collective-permute-done.3.first_ref = f32[120,128]{1,0:T(8,128)S(1)} collective-permute-done((f32[120,128]{1,0:T(8,128)S(1)}, f32[120,128]{1,0:T(8,128)S(1)}, u32[]{:S(2)}, u32[]{:S(2)}) %collective-permute-start.3) | collective-permute-done | bytes 61472 | tf_op jit(solution)/shard_map/ppermute | solution.py:330
  23.4 2.1 %collective-permute-start.4 = (f32[120,128]{1,0:T(8,128)S(1)}, f32[120,128]{1,0:T(8,128)S(1)}, u32[]{:S(2)}, u32[]{:S(2)}) collective-permute-start(f32[120,128]{1,0:T(8,128)S(1)} %pad_maximum_fusion.2), channel_id=1, source_target_pairs={{0,3},{1,2},{2,1},{3,0},{4,7},{5,6},{6,5},{7,4},{8,11},{9,10},{10,... | collective-permute-start | bytes 184328 | tf_op jit(solution)/shard_map/ppermute | solution.py:335
  25.5 2.5 %first_scatter.1.base_ref = f32[512,512]{1,0:T(8,128)S(1)} custom-call(s32[1]{0:T(128)} %bitcast.mine_ref, f32[3,4,8,128]{3,2,1,0:T(8,128)S(1)} %collective-permute-done.low_ref, f32[3,4,8,128]{3,2,1,0:T(8,128)S(1)} %near_gather.1.own_ref, f32[3,4,8,128]{3,2,1,0:T(8,128)S(1)} %collective-permute-done.1.high_ref, s32[72,128]{1,0:T(8,128)S(1)} %get-tuple-element.26.dst_ref), custom_call_target="tpu_custom_call" | custom-call | flops 4000000000 | bytes 100000 | tf_op jit(solution)/shard_map/first_scatter/pallas_call | solution.py:339
  27.9 0.0 collective-permute-done.4.second_ref
  28.0 0.1 collective-permute-start.5
  28.0 3.8 %outer_scatter.1 = (f32[3,256,128]{2,1,0:T(8,128)S(1)}, f32[3,64,128]{2,1,0:T(8,128)S(1)}, f32[3,64,128]{2,1,0:T(8,128)S(1)}) custom-call(s32[1]{0:T(128)} %bitcast.mine_ref, f32[512,512]{1,0:T(8,128)S(1)} %first_scatter.1.base_ref, f32[120,128]{1,0:T(8,128)S(1)} %collective-permute-done.3.first_ref, f32[120,128]{1,0:T(8,128)S(1)} %collective-permute-done.4.second_ref, ...), custom_call_target="tpu_custom_call" | custom-call | flops 4000000000 | bytes 100000 | tf_op jit(solution)/shard_map/outer_scatter/pallas_call | solution.py:339
  31.9 4.0 %collective-permute-start.7 = (f32[192,128]{1,0:T(8,128)S(1)}, f32[192,128]{1,0:T(8,128)S(1)}, u32[]{:S(2)}, u32[]{:S(2)}) collective-permute-start(f32[192,128]{1,0:T(8,128)S(1)} %bitcast.22), channel_id=1, source_target_pairs={{0,28},{4,8},{8,4},{12,16},{16,12},{20,24},{24,20},{28,0},{1,29},{... | collective-permute-start | bytes 294920 | tf_op jit(solution)/shard_map/ppermute | solution.py:335
  35.9 0.0 collective-permute-done.5
  35.9 0.1 collective-permute-start.6
  36.0 3.9 %inner_scatter.1 = (f32[3,256,128]{2,1,0:T(8,128)S(1)}, f32[3,8,128]{2,1,0:T(8,128)S(1)}, f32[3,8,128]{2,1,0:T(8,128)S(1)}) custom-call(s32[1]{0:T(128)} %bitcast.mine_ref, f32[512,512]{1,0:T(8,128)S(1)} %first_scatter.1.base_ref, f32[120,128]{1,0:T(8,128)S(1)} %collective-permute-done.3.first_ref, f32[120,128]{1,0:T(8,128)S(1)} %collective-permute-done.4.second_ref, ...), custom_call_target="tpu_custom_call" | custom-call | flops 4000000000 | bytes 100000 | tf_op jit(solution)/shard_map/inner_scatter/pallas_call | solution.py:339
  39.9 0.0 copy-start.2
  39.9 1.8 %collective-permute-done.6.xa_ref = f32[216,128]{1,0:T(8,128)S(1)} collective-permute-done((f32[216,128]{1,0:T(8,128)S(1)}, f32[216,128]{1,0:T(8,128)S(1)}, u32[]{:S(2)}, u32[]{:S(2)}) %collective-permute-start.6) | collective-permute-done | bytes 110624 | tf_op jit(solution)/shard_map/ppermute | solution.py:330
  41.7 0.0 collective-permute-done.7.xb_ref
  41.7 0.0 collective-permute-start.8
  41.7 2.1 %collective-permute-start.9 = (f32[3,8,128]{2,1,0:T(8,128)S(1)}, f32[3,8,128]{2,1,0:T(8,128)S(1)}, u32[]{:S(2)}, u32[]{:S(2)}) collective-permute-start(f32[3,8,128]{2,1,0:T(8,128)S(1)} %get-tuple-element.39), channel_id=1, source_target_pairs={{0,3},{1,2},{2,1},{3,0},{4,7},{5,6},{6,5},{7,4},{8,11},{9,10},{10,... | collective-permute-start | bytes 36872 | tf_op jit(solution)/shard_map/ppermute | solution.py:335
  43.8 0.0 copy-done.2
  43.8 0.9 %forcing.1.frc_ref = f32[3,512,128]{2,1,0:T(8,128)S(1)} custom-call(s32[1]{0:T(128)} %bitcast.mine_ref, s32[20,192]{1,0:T(8,128)S(1)} %copy-done, s32[20,192]{1,0:T(8,128)S(1)} %copy-done.1, f32[20,192]{1,0:T(8,128)S(1)} %copy-done.2, f32[3,20,192]{2,1,0:T(8,128)S(1)} %get-tuple-element.31.pts_ref, f32[24,128]{1,0:T(8,128)S(1)} %slice_add_fusion.rot_ref), custom_call_target="tpu_custom_call" | custom-call | flops 1000000 | bytes 100000 | tf_op jit(solution)/shard_map/forcing/pallas_call | solution.py:339
  44.7 0.0 collective-permute-done.8.ya_ref
  44.7 0.5 %collective-permute-done.9.yb_ref = f32[3,8,128]{2,1,0:T(8,128)S(1)} collective-permute-done((f32[3,8,128]{2,1,0:T(8,128)S(1)}, f32[3,8,128]{2,1,0:T(8,128)S(1)}, u32[]{:S(2)}, u32[]{:S(2)}) %collective-permute-start.9) | collective-permute-done | bytes 12320 | tf_op jit(solution)/shard_map/ppermute | solution.py:335
  45.2 1.5 %stencil.1 = (f32[3,8,64,128]{3,2,1,0:T(8,128)}, f32[3,512,128]{2,1,0:T(8,128)}) custom-call(s32[1]{0:T(128)} %bitcast.mine_ref, f32[3,256,128]{2,1,0:T(8,128)S(1)} %get-tuple-element.29.outer_ref, f32[3,256,128]{2,1,0:T(8,128)S(1)} %get-tuple-element.30.inner_ref, f32[3,512,128]{2,1,0:T(8,128)S(1)} %forcing.1.frc_ref, ...), custom_call_target="tpu_custom_call" | custom-call | flops 1000000000 | bytes 100000 | tf_op jit(solution)/shard_map/stencil/pallas_call | solution.py:339
  (12 shorter events, 0.1 us)
Async XLA Ops:
  0.6 0.7 %copy-start.7 = (s32[1,1,9]{2,1,0:T(1,128)S(1)}, s32[1,1,9]{2,1,0:T(1,128)}, u32[]{:S(2)}) copy-start(s32[1,1,9]{2,1,0:T(1,128)} %cnt_ref.1) | copy-start | bytes 112
  1.3 1.1 %copy-start.3 = (f32[3,8,64,128]{3,2,1,0:T(8,128)S(1)}, f32[3,8,64,128]{3,2,1,0:T(8,128)}, u32[]{:S(2)}) copy-start(f32[3,8,64,128]{3,2,1,0:T(8,128)} %param.8) | copy-start | bytes 2359300
  2.4 0.8 %copy-start.4 = (s32[1,1,9,1024]{3,1,2,0:T(1,128)S(1)}, s32[1,1,9,1024]{3,1,2,0:T(1,128)}, u32[]{:S(2)}) copy-start(s32[1,1,9,1024]{3,1,2,0:T(1,128)} %param.10) | copy-start | bytes 110596
  3.2 0.8 %copy-start.5 = (f32[1,1,9,1024]{3,1,2,0:T(1,128)S(1)}, f32[1,1,9,1024]{3,1,2,0:T(1,128)}, u32[]{:S(2)}) copy-start(f32[1,1,9,1024]{3,1,2,0:T(1,128)} %param.11) | copy-start | bytes 110596
  4.0 0.8 %copy-start.6 = (s32[1,1,9,1024]{3,1,2,0:T(1,128)S(1)}, s32[1,1,9,1024]{3,1,2,0:T(1,128)}, u32[]{:S(2)}) copy-start(s32[1,1,9,1024]{3,1,2,0:T(1,128)} %param.12) | copy-start | bytes 110596
  4.7 4.3 %copy-start = (s32[20,192]{1,0:T(8,128)S(1)}, s32[20,192]{1,0:T(8,128)}, u32[]{:S(2)}) copy-start(s32[20,192]{1,0:T(8,128)} %tile_ref.3) | copy-start | bytes 46084
  4.7 4.4 %copy-start.1 = (s32[20,192]{1,0:T(8,128)S(1)}, s32[20,192]{1,0:T(8,128)}, u32[]{:S(2)}) copy-start(s32[20,192]{1,0:T(8,128)} %cell_ref.3) | copy-start | bytes 46084
  10.1 9.0 %collective-permute-start.2 = (f32[24,128]{1,0:T(8,128)S(1)}, f32[24,128]{1,0:T(8,128)S(1)}, u32[]{:S(2)}, u32[]{:S(2)}) collective-permute-start(f32[24,128]{1,0:T(8,128)S(1)} %get-tuple-element.27), channel_id=1, source_target_pairs={{0,16},{4,20},{8,24},{12,28},{16,0},{20,4},{24,8},{28,12},{1,17},{... | collective-permute-start | bytes 36872 | tf_op jit(solution)/shard_map/ppermute | solution.py:330
  15.2 6.9 %collective-permute-start.1 = (f32[3,4,8,128]{3,2,1,0:T(8,128)S(1)}, f32[3,4,8,128]{3,2,1,0:T(8,128)S(1)}, u32[]{:S(2)}, u32[]{:S(2)}) collective-permute-start(f32[3,4,8,128]{3,2,1,0:T(8,128)S(1)} %get-tuple-element.42), channel_id=1, source_target_pairs={{0,28},{4,8},{8,4},{12,16},{16,12},{20,24},{24,20},{28,0},{1,29},{... | collective-permute-start | bytes 147464 | tf_op jit(solution)/shard_map/ppermute | solution.py:335
  16.5 5.6 %collective-permute-start = (f32[3,4,8,128]{3,2,1,0:T(8,128)S(1)}, f32[3,4,8,128]{3,2,1,0:T(8,128)S(1)}, u32[]{:S(2)}, u32[]{:S(2)}) collective-permute-start(f32[3,4,8,128]{3,2,1,0:T(8,128)S(1)} %get-tuple-element.43), channel_id=1, source_target_pairs={{0,4},{4,0},{8,12},{12,8},{16,20},{20,16},{24,28},{28,24},{1,5},{5... | collective-permute-start | bytes 147464 | tf_op jit(solution)/shard_map/ppermute | solution.py:330
  22.1 1.3 %collective-permute-start.3 = (f32[120,128]{1,0:T(8,128)S(1)}, f32[120,128]{1,0:T(8,128)S(1)}, u32[]{:S(2)}, u32[]{:S(2)}) collective-permute-start(f32[120,128]{1,0:T(8,128)S(1)} %pad_maximum_fusion.1), channel_id=1, source_target_pairs={{0,1},{1,0},{2,3},{3,2},{4,5},{5,4},{6,7},{7,6},{8,9},{9,8},{10,11... | collective-permute-start | bytes 184328 | tf_op jit(solution)/shard_map/ppermute | solution.py:330
  23.4 4.5 %collective-permute-start.4 = (f32[120,128]{1,0:T(8,128)S(1)}, f32[120,128]{1,0:T(8,128)S(1)}, u32[]{:S(2)}, u32[]{:S(2)}) collective-permute-start(f32[120,128]{1,0:T(8,128)S(1)} %pad_maximum_fusion.2), channel_id=1, source_target_pairs={{0,3},{1,2},{2,1},{3,0},{4,7},{5,6},{6,5},{7,4},{8,11},{9,10},{10,... | collective-permute-start | bytes 184328 | tf_op jit(solution)/shard_map/ppermute | solution.py:335
  28.0 7.9 %collective-permute-start.5 = (f32[24,128]{1,0:T(8,128)S(1)}, f32[24,128]{1,0:T(8,128)S(1)}, u32[]{:S(2)}, u32[]{:S(2)}) collective-permute-start(f32[24,128]{1,0:T(8,128)S(1)} %slice_add_fusion.1), channel_id=1, source_target_pairs={{0,8},{4,12},{8,0},{12,4},{16,24},{20,28},{24,16},{28,20},{1,9},{5... | collective-permute-start | bytes 36872 | tf_op jit(solution)/shard_map/ppermute | solution.py:330
  31.9 9.8 %collective-permute-start.7 = (f32[192,128]{1,0:T(8,128)S(1)}, f32[192,128]{1,0:T(8,128)S(1)}, u32[]{:S(2)}, u32[]{:S(2)}) collective-permute-start(f32[192,128]{1,0:T(8,128)S(1)} %bitcast.22), channel_id=1, source_target_pairs={{0,28},{4,8},{8,4},{12,16},{16,12},{20,24},{24,20},{28,0},{1,29},{... | collective-permute-start | bytes 294920 | tf_op jit(solution)/shard_map/ppermute | solution.py:335
  35.9 5.8 %collective-permute-start.6 = (f32[216,128]{1,0:T(8,128)S(1)}, f32[216,128]{1,0:T(8,128)S(1)}, u32[]{:S(2)}, u32[]{:S(2)}) collective-permute-start(f32[216,128]{1,0:T(8,128)S(1)} %pad_maximum_fusion), channel_id=1, source_target_pairs={{0,4},{4,0},{8,12},{12,8},{16,20},{20,16},{24,28},{28,24},{1,5},{5... | collective-permute-start | bytes 331784 | tf_op jit(solution)/shard_map/ppermute | solution.py:330
  39.9 3.9 %copy-start.2 = (f32[20,192]{1,0:T(8,128)S(1)}, f32[20,192]{1,0:T(8,128)}, u32[]{:S(2)}) copy-start(f32[20,192]{1,0:T(8,128)} %coef_ref.1) | copy-start | bytes 46084
  41.7 3.0 %collective-permute-start.8 = (f32[3,8,128]{2,1,0:T(8,128)S(1)}, f32[3,8,128]{2,1,0:T(8,128)S(1)}, u32[]{:S(2)}, u32[]{:S(2)}) collective-permute-start(f32[3,8,128]{2,1,0:T(8,128)S(1)} %get-tuple-element.38), channel_id=1, source_target_pairs={{0,1},{1,0},{2,3},{3,2},{4,5},{5,4},{6,7},{7,6},{8,9},{9,8},{10,11... | collective-permute-start | bytes 36872 | tf_op jit(solution)/shard_map/ppermute | solution.py:330
  41.7 3.5 %collective-permute-start.9 = (f32[3,8,128]{2,1,0:T(8,128)S(1)}, f32[3,8,128]{2,1,0:T(8,128)S(1)}, u32[]{:S(2)}, u32[]{:S(2)}) collective-permute-start(f32[3,8,128]{2,1,0:T(8,128)S(1)} %get-tuple-element.39), channel_id=1, source_target_pairs={{0,3},{1,2},{2,1},{3,0},{4,7},{5,6},{6,5},{7,4},{8,11},{9,10},{10,... | collective-permute-start | bytes 36872 | tf_op jit(solution)/shard_map/ppermute | solution.py:335

commit v4 on v3

--- a/solution.py
+++ b/solution.py
@@ -170,19 +170,19 @@
     return kernel
 
 
-def scatter_lists(val, n_lists, direction, dst_ref, listed, acc, extent, place):
+def scatter_lists(val, n_lists, direction, dst_ref, listed, acc, extent, place, width=4):
     lists = []
     for q in range(n_lists):
         used = jnp.sum(jnp.where(val[q, 3] != 0.0, 1.0, 0.0)).astype(jnp.int32)
         lists.append((used, q))
     total = list_blocks(lists, listed)
-    for k in range(3):
+    for k in range(width - 1):
         listed[total + k] = 0
 
     def chunk(i, carry):
         cells, vals = [], [[], [], [], []]
-        for k in range(4):
-            at = 4 * i + k
+        for k in range(width):
+            at = width * i + k
             b = listed[at]
             q, j = b >> 3, b & 7
             keep = jnp.where(at < total, 1.0, 0.0)
@@ -194,7 +194,7 @@
         acc[...] += spread(extent, place((cell >> 7) & 511), cell & 127, vals)
         return carry
 
-    lax.fori_loop(0, (total + 3) >> 2, chunk, 0)
+    lax.fori_loop(0, (total + width - 1) // width, chunk, 0)
 
 
 def make_first_scatter(count_y):
@@ -230,7 +230,7 @@
         acc[0:128, :] = base_ref[0:128, :]
         acc[128:256, :] = base_ref[384:512, :]
         place = lambda row: jnp.where(row < 128, row, jnp.where(row >= 384, row - 256, 512))
-        scatter_lists(val, 6, direction, dst_ref, listed, acc, 256, place)
+        scatter_lists(val, 6, direction, dst_ref, listed, acc, 256, place, 6)
         side_x, _ = sides(mine_ref, count_y)
         for c in range(3):
             vel = jnp.concatenate([vel_ref[c, 0:128, :], vel_ref[c, 384:512, :]], axis=0)
@@ -246,7 +246,7 @@
     def kernel(mine_ref, base_ref, first_ref, second_ref, dst_ref, vel_ref, outer_ref, cor_ref, fa_ref, fb_ref, acc, val, listed, direction):
         load_later_lists(mine_ref, count_y, first_ref, second_ref, val, direction)
         acc[...] = base_ref[128:384, :]
-        scatter_lists(val, 6, direction, dst_ref, listed, acc, 256, lambda row: row - 128)
+        scatter_lists(val, 6, direction, dst_ref, listed, acc, 256, lambda row: row - 128, 6)
         _, side_y = sides(mine_ref, count_y)
         for c in range(3):
             cor_ref[c] = corrected(acc, vel_ref[c, 128:384, :], c)
@@ -365,7 +365,7 @@
         "far_gather",
         [((6, 4, 8, 128), F32, VMEM), ((3, 256, 512), BF16, VMEM), ((3, 512, 128), F32, VMEM), whole, ((72, 128), F32, VMEM), whole],
         [SMEM] + [HBM] * 5,
-        (mine, counts, vel, src, weight, dst),
+        (mine,) + tuple(pltpu.with_memory_space_constraint(v, pltpu.HBM) for v in (counts, vel, src, weight, dst)),
         [pltpu.SemaphoreType.DMA((7,)), pltpu.SMEM((1, 1, 9), jnp.int32), ints(64), ints(8)],
         flops=5 * 10**9,
     )

time: 46.8 us -> 43.9 us (0.938)
  Pallas kernels: 20.5 us -> 24.7 us
  local copies, waits for them, and re-layouts: 4.12 us -> 0.69 us
  waiting for transfers between devices: 6.23 us -> 3.08 us
    pallas_call x8, Pallas kernels: 20.5 us -> 24.7 us  [call(): pl.pallas_call(kernel, out_shape=tuple((jax.ShapeDtypeStruct(shape, dtype...]
    unnamed x16 -> x8, local copies, waits for them, and re-layouts: 4.1 us -> 0.67 us
    ppermute x4, waiting for transfers between devices: 3.43 us -> 0.49 us  [swap_next(): lax.ppermute(value, axis, [(i, (i - 1 if i % 2 == 0 else i + 1) % count)...]
  transfers between devices with their start and end apart: 10 -> 10, of which waited for: 4 -> 3; matrix products, arithmetic and copies ran while one was open for 0% -> 0% of each run, Pallas kernels for 29% -> 38%
where the time goes in v4:
time: 43.9 us; the launch traced here: 44.1 us
  Pallas kernels  24.7 us (56%)
  starting transfers between devices  14.7 us (33%)
  waiting for transfers between devices  3.08 us (7%)
  between operations  0.84 us (2%)
  local copies, waits for them, and re-layouts  0.69 us (2%)
    pallas_call x8, Pallas kernels, call(): pl.pallas_call(kernel, out_shape=tuple((jax.ShapeDtypeStruct(shape, dtype...  24.7 us
    ppermute x4, starting transfers between devices, swap_next(): lax.ppermute(value, axis, [(i, (i - 1 if i % 2 == 0 else i + 1) % count)...  9.23 us
    ppermute x6, starting transfers between devices, swap(): return lax.ppermute(value, axis, [(i, i ^ step) for i in range(count)])  5.45 us
    ppermute x6, waiting for transfers between devices, swap(): return lax.ppermute(value, axis, [(i, i ^ step) for i in range(count)])  2.59 us
  transfers between devices with their start and end apart: 10, of which 3 were waited for; matrix products, arithmetic and copies ran while one was open for 0% of the time, Pallas kernels for 38%

profile of v4, /device:TPU:0, one launch (start us, length us, event | category | flops | bytes accessed | tf_op | source)
XLA Modules:
  0.0 44.1 jit_solution(693233106109266170)
XLA Ops:
  0.6 0.0 copy-start
  0.6 0.0 copy-start.1
  0.7 5.5 %far_gather.1 = (f32[6,4,8,128]{3,2,1,0:T(8,128)S(1)}, bf16[3,256,512]{2,1,0:T(8,128)(2,1)S(1)}, f32[3,512,128]{2,1,0:T(8,128)S(1)}, s32[72,128]{1,0:T(8,128)S(1...) custom-call(s32[1]{0:T(128)} %bitcast.mine_ref, s32[1,1,9]{2,1,0:T(1,128)} %cnt_ref.1, f32[3,512,128]{2,1,0:T(8,128)} %bitcast.22, ...), custom_call_target="tpu_custom_call" | custom-call | flops 5000000000 | bytes 100000 | tf_op jit(solution)/shard_map/far_gather/pallas_call | solution.py:339
  6.2 0.0 copy-done
  6.2 0.0 copy-done.1
  6.2 1.0 %points.1 = (f32[3,20,192]{2,1,0:T(8,128)S(1)}, f32[24,128]{1,0:T(8,128)S(1)}) custom-call(s32[1]{0:T(128)} %bitcast.mine_ref, bf16[3,256,512]{2,1,0:T(8,128)(2,1)S(1)} %get-tuple-element.23.table, s32[20,192]{1,0:T(8,128)S(1)} %copy-done, s32[20,192]{1,0:T(8,128)S(1)} %copy-done.1), custom_call_target="tpu_custom_call" | custom-call | flops 1000000000 | bytes 100000 | tf_op jit(solution)/shard_map/points/pallas_call | solution.py:339
  7.2 4.9 %collective-permute-start.2 = (f32[24,128]{1,0:T(8,128)S(1)}, f32[24,128]{1,0:T(8,128)S(1)}, u32[]{:S(2)}, u32[]{:S(2)}) collective-permute-start(f32[24,128]{1,0:T(8,128)S(1)} %get-tuple-element.27), channel_id=1, source_target_pairs={{0,16},{4,20},{8,24},{12,28},{16,0},{20,4},{24,8},{28,12},{1,17},{... | collective-permute-start | bytes 36872 | tf_op jit(solution)/shard_map/ppermute | solution.py:330
  12.1 2.9 %collective-permute-start.1 = (f32[3,4,8,128]{3,2,1,0:T(8,128)S(1)}, f32[3,4,8,128]{3,2,1,0:T(8,128)S(1)}, u32[]{:S(2)}, u32[]{:S(2)}) collective-permute-start(f32[3,4,8,128]{3,2,1,0:T(8,128)S(1)} %get-tuple-element.42), channel_id=1, source_target_pairs={{0,28},{4,8},{8,4},{12,16},{16,12},{20,24},{24,20},{28,0},{1,29},{... | collective-permute-start | bytes 147464 | tf_op jit(solution)/shard_map/ppermute | solution.py:335
  15.0 0.0 collective-permute-start
  15.0 0.0 copy-start.3
  15.0 0.7 %copy-done.3 = s32[1,1,9]{2,1,0:T(1,128)S(1)} copy-done((s32[1,1,9]{2,1,0:T(1,128)S(1)}, s32[1,1,9]{2,1,0:T(1,128)}, u32[]{:S(2)}) %copy-start.3) | copy-done | bytes 60
  15.6 3.9 %near_gather.1.own_ref = f32[3,4,8,128]{3,2,1,0:T(8,128)S(1)} custom-call(s32[1]{0:T(128)} %bitcast.mine_ref, s32[1,1,9]{2,1,0:T(1,128)S(1)} %copy-done.3, bf16[3,256,512]{2,1,0:T(8,128)(2,1)S(1)} %get-tuple-element.23.table, s32[72,128]{1,0:T(8,128)S(1)} %get-tuple-element.24.src_ref, f32[72,128]{1,0:T(8,128)S(1)} %get-tuple-element.25.w_ref), custom_call_target="tpu_custom_call" | custom-call | flops 4000000000 | bytes 100000 | tf_op jit(solution)/shard_map/near_gather/pallas_call | solution.py:339
  19.5 0.0 collective-permute-done.2
  19.6 0.0 collective-permute-done.1.high_ref
  19.6 0.0 collective-permute-done.low_ref
  19.6 0.1 collective-permute-start.3
  19.7 1.2 %collective-permute-done.3.first_ref = f32[120,128]{1,0:T(8,128)S(1)} collective-permute-done((f32[120,128]{1,0:T(8,128)S(1)}, f32[120,128]{1,0:T(8,128)S(1)}, u32[]{:S(2)}, u32[]{:S(2)}) %collective-permute-start.3) | collective-permute-done | bytes 61472 | tf_op jit(solution)/shard_map/ppermute | solution.py:330
  21.0 0.7 %collective-permute-start.4 = (f32[120,128]{1,0:T(8,128)S(1)}, f32[120,128]{1,0:T(8,128)S(1)}, u32[]{:S(2)}, u32[]{:S(2)}) collective-permute-start(f32[120,128]{1,0:T(8,128)S(1)} %pad_maximum_fusion.2), channel_id=1, source_target_pairs={{0,3},{1,2},{2,1},{3,0},{4,7},{5,6},{6,5},{7,4},{8,11},{9,10},{10,... | collective-permute-start | bytes 184328 | tf_op jit(solution)/shard_map/ppermute | solution.py:335
  21.6 4.8 %first_scatter.1.base_ref = f32[512,512]{1,0:T(8,128)S(1)} custom-call(s32[1]{0:T(128)} %bitcast.mine_ref, f32[3,4,8,128]{3,2,1,0:T(8,128)S(1)} %collective-permute-done.low_ref, f32[3,4,8,128]{3,2,1,0:T(8,128)S(1)} %near_gather.1.own_ref, f32[3,4,8,128]{3,2,1,0:T(8,128)S(1)} %collective-permute-done.1.high_ref, s32[72,128]{1,0:T(8,128)S(1)} %get-tuple-element.26.dst_ref), custom_call_target="tpu_custom_call" | custom-call | flops 4000000000 | bytes 100000 | tf_op jit(solution)/shard_map/first_scatter/pallas_call | solution.py:339
  26.4 0.0 collective-permute-done.4.second_ref
  26.4 0.1 collective-permute-start.5
  26.5 3.6 %outer_scatter.1 = (f32[3,256,128]{2,1,0:T(8,128)S(1)}, f32[3,64,128]{2,1,0:T(8,128)S(1)}, f32[3,64,128]{2,1,0:T(8,128)S(1)}) custom-call(s32[1]{0:T(128)} %bitcast.mine_ref, f32[512,512]{1,0:T(8,128)S(1)} %first_scatter.1.base_ref, f32[120,128]{1,0:T(8,128)S(1)} %collective-permute-done.3.first_ref, f32[120,128]{1,0:T(8,128)S(1)} %collective-permute-done.4.second_ref, ...), custom_call_target="tpu_custom_call" | custom-call | flops 4000000000 | bytes 100000 | tf_op jit(solution)/shard_map/outer_scatter/pallas_call | solution.py:339
  30.1 3.2 %collective-permute-start.7 = (f32[192,128]{1,0:T(8,128)S(1)}, f32[192,128]{1,0:T(8,128)S(1)}, u32[]{:S(2)}, u32[]{:S(2)}) collective-permute-start(f32[192,128]{1,0:T(8,128)S(1)} %bitcast.21), channel_id=1, source_target_pairs={{0,28},{4,8},{8,4},{12,16},{16,12},{20,24},{24,20},{28,0},{1,29},{... | collective-permute-start | bytes 294920 | tf_op jit(solution)/shard_map/ppermute | solution.py:335
  33.3 0.0 collective-permute-done.5
  33.3 0.4 collective-permute-start.6
  33.7 3.6 %inner_scatter.1 = (f32[3,256,128]{2,1,0:T(8,128)S(1)}, f32[3,8,128]{2,1,0:T(8,128)S(1)}, f32[3,8,128]{2,1,0:T(8,128)S(1)}) custom-call(s32[1]{0:T(128)} %bitcast.mine_ref, f32[512,512]{1,0:T(8,128)S(1)} %first_scatter.1.base_ref, f32[120,128]{1,0:T(8,128)S(1)} %collective-permute-done.3.first_ref, f32[120,128]{1,0:T(8,128)S(1)} %collective-permute-done.4.second_ref, ...), custom_call_target="tpu_custom_call" | custom-call | flops 4000000000 | bytes 100000 | tf_op jit(solution)/shard_map/inner_scatter/pallas_call | solution.py:339
  37.3 0.0 copy-start.2
  37.3 1.3 %collective-permute-done.6.xa_ref = f32[216,128]{1,0:T(8,128)S(1)} collective-permute-done((f32[216,128]{1,0:T(8,128)S(1)}, f32[216,128]{1,0:T(8,128)S(1)}, u32[]{:S(2)}, u32[]{:S(2)}) %collective-permute-start.6) | collective-permute-done | bytes 110624 | tf_op jit(solution)/shard_map/ppermute | solution.py:330
  38.6 0.0 collective-permute-done.7.xb_ref
  38.6 0.0 collective-permute-start.8
  38.6 2.5 %collective-permute-start.9 = (f32[3,8,128]{2,1,0:T(8,128)S(1)}, f32[3,8,128]{2,1,0:T(8,128)S(1)}, u32[]{:S(2)}, u32[]{:S(2)}) collective-permute-start(f32[3,8,128]{2,1,0:T(8,128)S(1)} %get-tuple-element.39), channel_id=1, source_target_pairs={{0,3},{1,2},{2,1},{3,0},{4,7},{5,6},{6,5},{7,4},{8,11},{9,10},{10,... | collective-permute-start | bytes 36872 | tf_op jit(solution)/shard_map/ppermute | solution.py:335
  41.1 0.0 copy-done.2
  41.1 0.9 %forcing.1.frc_ref = f32[3,512,128]{2,1,0:T(8,128)S(1)} custom-call(s32[1]{0:T(128)} %bitcast.mine_ref, s32[20,192]{1,0:T(8,128)S(1)} %copy-done, s32[20,192]{1,0:T(8,128)S(1)} %copy-done.1, f32[20,192]{1,0:T(8,128)S(1)} %copy-done.2, f32[3,20,192]{2,1,0:T(8,128)S(1)} %get-tuple-element.31.pts_ref, f32[24,128]{1,0:T(8,128)S(1)} %slice_add_fusion.rot_ref), custom_call_target="tpu_custom_call" | custom-call | flops 1000000 | bytes 100000 | tf_op jit(solution)/shard_map/forcing/pallas_call | solution.py:339
  42.0 0.0 collective-permute-done.8.ya_ref
  42.1 0.5 %collective-permute-done.9.yb_ref = f32[3,8,128]{2,1,0:T(8,128)S(1)} collective-permute-done((f32[3,8,128]{2,1,0:T(8,128)S(1)}, f32[3,8,128]{2,1,0:T(8,128)S(1)}, u32[]{:S(2)}, u32[]{:S(2)}) %collective-permute-start.9) | collective-permute-done | bytes 12320 | tf_op jit(solution)/shard_map/ppermute | solution.py:335
  42.5 1.5 %stencil.1 = (f32[3,8,64,128]{3,2,1,0:T(8,128)}, f32[3,512,128]{2,1,0:T(8,128)}) custom-call(s32[1]{0:T(128)} %bitcast.mine_ref, f32[3,256,128]{2,1,0:T(8,128)S(1)} %get-tuple-element.29.outer_ref, f32[3,256,128]{2,1,0:T(8,128)S(1)} %get-tuple-element.30.inner_ref, f32[3,512,128]{2,1,0:T(8,128)S(1)} %forcing.1.frc_ref, ...), custom_call_target="tpu_custom_call" | custom-call | flops 1000000000 | bytes 100000 | tf_op jit(solution)/shard_map/stencil/pallas_call | solution.py:339
  (12 shorter events, 0.1 us)
Async XLA Ops:
  0.6 5.5 %copy-start = (s32[20,192]{1,0:T(8,128)S(1)}, s32[20,192]{1,0:T(8,128)}, u32[]{:S(2)}) copy-start(s32[20,192]{1,0:T(8,128)} %tile_ref.3) | copy-start | bytes 46084
  0.6 5.5 %copy-start.1 = (s32[20,192]{1,0:T(8,128)S(1)}, s32[20,192]{1,0:T(8,128)}, u32[]{:S(2)}) copy-start(s32[20,192]{1,0:T(8,128)} %cell_ref.3) | copy-start | bytes 46084
  7.2 12.4 %collective-permute-start.2 = (f32[24,128]{1,0:T(8,128)S(1)}, f32[24,128]{1,0:T(8,128)S(1)}, u32[]{:S(2)}, u32[]{:S(2)}) collective-permute-start(f32[24,128]{1,0:T(8,128)S(1)} %get-tuple-element.27), channel_id=1, source_target_pairs={{0,16},{4,20},{8,24},{12,28},{16,0},{20,4},{24,8},{28,12},{1,17},{... | collective-permute-start | bytes 36872 | tf_op jit(solution)/shard_map/ppermute | solution.py:330
  12.1 7.5 %collective-permute-start.1 = (f32[3,4,8,128]{3,2,1,0:T(8,128)S(1)}, f32[3,4,8,128]{3,2,1,0:T(8,128)S(1)}, u32[]{:S(2)}, u32[]{:S(2)}) collective-permute-start(f32[3,4,8,128]{3,2,1,0:T(8,128)S(1)} %get-tuple-element.42), channel_id=1, source_target_pairs={{0,28},{4,8},{8,4},{12,16},{16,12},{20,24},{24,20},{28,0},{1,29},{... | collective-permute-start | bytes 147464 | tf_op jit(solution)/shard_map/ppermute | solution.py:335
  15.0 4.6 %collective-permute-start = (f32[3,4,8,128]{3,2,1,0:T(8,128)S(1)}, f32[3,4,8,128]{3,2,1,0:T(8,128)S(1)}, u32[]{:S(2)}, u32[]{:S(2)}) collective-permute-start(f32[3,4,8,128]{3,2,1,0:T(8,128)S(1)} %get-tuple-element.43), channel_id=1, source_target_pairs={{0,4},{4,0},{8,12},{12,8},{16,20},{20,16},{24,28},{28,24},{1,5},{5... | collective-permute-start | bytes 147464 | tf_op jit(solution)/shard_map/ppermute | solution.py:330
  15.0 0.7 %copy-start.3 = (s32[1,1,9]{2,1,0:T(1,128)S(1)}, s32[1,1,9]{2,1,0:T(1,128)}, u32[]{:S(2)}) copy-start(s32[1,1,9]{2,1,0:T(1,128)} %cnt_ref.1) | copy-start | bytes 112
  19.6 1.3 %collective-permute-start.3 = (f32[120,128]{1,0:T(8,128)S(1)}, f32[120,128]{1,0:T(8,128)S(1)}, u32[]{:S(2)}, u32[]{:S(2)}) collective-permute-start(f32[120,128]{1,0:T(8,128)S(1)} %pad_maximum_fusion.1), channel_id=1, source_target_pairs={{0,1},{1,0},{2,3},{3,2},{4,5},{5,4},{6,7},{7,6},{8,9},{9,8},{10,11... | collective-permute-start | bytes 184328 | tf_op jit(solution)/shard_map/ppermute | solution.py:330
  21.0 5.4 %collective-permute-start.4 = (f32[120,128]{1,0:T(8,128)S(1)}, f32[120,128]{1,0:T(8,128)S(1)}, u32[]{:S(2)}, u32[]{:S(2)}) collective-permute-start(f32[120,128]{1,0:T(8,128)S(1)} %pad_maximum_fusion.2), channel_id=1, source_target_pairs={{0,3},{1,2},{2,1},{3,0},{4,7},{5,6},{6,5},{7,4},{8,11},{9,10},{10,... | collective-permute-start | bytes 184328 | tf_op jit(solution)/shard_map/ppermute | solution.py:335
  26.4 6.9 %collective-permute-start.5 = (f32[24,128]{1,0:T(8,128)S(1)}, f32[24,128]{1,0:T(8,128)S(1)}, u32[]{:S(2)}, u32[]{:S(2)}) collective-permute-start(f32[24,128]{1,0:T(8,128)S(1)} %slice_add_fusion.1), channel_id=1, source_target_pairs={{0,8},{4,12},{8,0},{12,4},{16,24},{20,28},{24,16},{28,20},{1,9},{5... | collective-permute-start | bytes 36872 | tf_op jit(solution)/shard_map/ppermute | solution.py:330
  30.1 8.6 %collective-permute-start.7 = (f32[192,128]{1,0:T(8,128)S(1)}, f32[192,128]{1,0:T(8,128)S(1)}, u32[]{:S(2)}, u32[]{:S(2)}) collective-permute-start(f32[192,128]{1,0:T(8,128)S(1)} %bitcast.21), channel_id=1, source_target_pairs={{0,28},{4,8},{8,4},{12,16},{16,12},{20,24},{24,20},{28,0},{1,29},{... | collective-permute-start | bytes 294920 | tf_op jit(solution)/shard_map/ppermute | solution.py:335
  33.3 5.3 %collective-permute-start.6 = (f32[216,128]{1,0:T(8,128)S(1)}, f32[216,128]{1,0:T(8,128)S(1)}, u32[]{:S(2)}, u32[]{:S(2)}) collective-permute-start(f32[216,128]{1,0:T(8,128)S(1)} %pad_maximum_fusion), channel_id=1, source_target_pairs={{0,4},{4,0},{8,12},{12,8},{16,20},{20,16},{24,28},{28,24},{1,5},{5... | collective-permute-start | bytes 331784 | tf_op jit(solution)/shard_map/ppermute | solution.py:330
  37.3 3.9 %copy-start.2 = (f32[20,192]{1,0:T(8,128)S(1)}, f32[20,192]{1,0:T(8,128)}, u32[]{:S(2)}) copy-start(f32[20,192]{1,0:T(8,128)} %coef_ref.1) | copy-start | bytes 46084
  38.6 3.4 %collective-permute-start.8 = (f32[3,8,128]{2,1,0:T(8,128)S(1)}, f32[3,8,128]{2,1,0:T(8,128)S(1)}, u32[]{:S(2)}, u32[]{:S(2)}) collective-permute-start(f32[3,8,128]{2,1,0:T(8,128)S(1)} %get-tuple-element.38), channel_id=1, source_target_pairs={{0,1},{1,0},{2,3},{3,2},{4,5},{5,4},{6,7},{7,6},{8,9},{9,8},{10,11... | collective-permute-start | bytes 36872 | tf_op jit(solution)/shard_map/ppermute | solution.py:330
  38.6 3.9 %collective-permute-start.9 = (f32[3,8,128]{2,1,0:T(8,128)S(1)}, f32[3,8,128]{2,1,0:T(8,128)S(1)}, u32[]{:S(2)}, u32[]{:S(2)}) collective-permute-start(f32[3,8,128]{2,1,0:T(8,128)S(1)} %get-tuple-element.39), channel_id=1, source_target_pairs={{0,3},{1,2},{2,1},{3,0},{4,7},{5,6},{6,5},{7,4},{8,11},{9,10},{10,... | collective-permute-start | bytes 36872 | tf_op jit(solution)/shard_map/ppermute | solution.py:335

commit v5 on v4

--- a/solution.py
+++ b/solution.py
@@ -57,21 +57,34 @@
 def list_blocks(lists, listed):
     total = jnp.int32(0)
     for used, tag in lists:
-
-        def put(j, n, tag=tag):
-            listed[n] = tag * 8 + j
-            return n + 1
-
-        total = lax.fori_loop(0, (used + 127) >> 7, put, total)
+        for j in range(8):
+            listed[total + j] = tag * 8 + j
+        total = total + ((used + 127) >> 7)
     return total
 
 
-def gather_lists(table, total, width, listed, direction, cnt_ref, src_ref, w_ref, out_ref):
-    for k in range(width - 1):
+def run_chunks(total, large, small, chunk):
+    many = (total + small - 1) // large
+
+    def big(i, carry):
+        chunk(i * large, large)
+        return carry
+
+    lax.fori_loop(0, many, big, 0)
+
+    def rest(i, carry):
+        chunk(many * large + i * small, small)
+        return carry
+
+    lax.fori_loop(0, jnp.maximum(total - many * large + small - 1, 0) // small, rest, 0)
+
+
+def gather_lists(table, total, large, small, listed, direction, cnt_ref, src_ref, w_ref, out_ref):
+    for k in range(large):
         listed[total + k] = listed[total - 1]
 
-    def step(i, carry):
-        blocks = [listed[width * i + k] for k in range(width)]
+    def chunk(first, width):
+        blocks = [listed[first + k] for k in range(width)]
         rows = [direction[b >> 3] * 8 + (b & 7) for b in blocks]
         cell = jnp.concatenate([src_ref[pl.ds(r, 1), :] for r in rows], axis=1)
         found = pick(table, cell)
@@ -83,12 +96,11 @@
             for c in range(3):
                 out_ref[b >> 3, c, pl.ds(j, 1), :] = found[c][:, k * 128 : (k + 1) * 128] * weight
             out_ref[b >> 3, 3, pl.ds(j, 1), :] = weight
-        return carry
-
-    lax.fori_loop(0, (total + width - 1) // width, step, 0)
-
-
-def make_far_gather(count_y, width):
+
+    run_chunks(total, large, small, chunk)
+
+
+def make_far_gather(count_y, large, small):
     def kernel(mine_ref, cnt_hbm, vel_hbm, src_hbm, w_hbm, dst_hbm, out_ref, table, vel_ref, src_ref, w_ref, dst_ref, sem, cnt_ref, listed, direction):
         half = vel_ref.shape[1] // 2
         pairs = [(cnt_hbm, cnt_ref), (src_hbm, src_ref)]
@@ -115,7 +127,7 @@
                 table[c, :, piece * 128 : (piece + 1) * 128] = high
                 table[c, :, 256 + piece * 128 : 256 + (piece + 1) * 128] = low
         copies[5].wait()
-        gather_lists(table, total, width, listed, direction, cnt_ref, src_ref, w_ref, out_ref)
+        gather_lists(table, total, large, small, listed, direction, cnt_ref, src_ref, w_ref, out_ref)
         copies[6].wait()
 
     return kernel
@@ -155,7 +167,7 @@
     rot_ref[0:turbines, :] = jnp.broadcast_to(sums, (turbines, 128))
 
 
-def make_near_gather(count_y, width):
+def make_near_gather(count_y, large, small):
     def kernel(mine_ref, cnt_ref, table, src_ref, w_ref, out_ref, listed, direction):
         out_ref[...] = jnp.zeros_like(out_ref)
         _, side_y = sides(mine_ref, count_y)
@@ -165,36 +177,34 @@
             direction[t] = d
             lists.append((cnt_ref[0, 0, d], t))
         total = list_blocks(lists, listed)
-        gather_lists(table, total, width, listed, direction, cnt_ref, src_ref, w_ref, out_ref)
-
-    return kernel
-
-
-def scatter_lists(val, n_lists, direction, dst_ref, listed, acc, extent, place, width=4):
+        gather_lists(table, total, large, small, listed, direction, cnt_ref, src_ref, w_ref, out_ref)
+
+    return kernel
+
+
+def scatter_lists(val, n_lists, direction, dst_ref, listed, acc, extent, place, large, small):
     lists = []
     for q in range(n_lists):
         used = jnp.sum(jnp.where(val[q, 3] != 0.0, 1.0, 0.0)).astype(jnp.int32)
         lists.append((used, q))
     total = list_blocks(lists, listed)
-    for k in range(width - 1):
+    for k in range(large):
         listed[total + k] = 0
 
-    def chunk(i, carry):
+    def chunk(first, width):
         cells, vals = [], [[], [], [], []]
         for k in range(width):
-            at = width * i + k
-            b = listed[at]
+            b = listed[first + k]
             q, j = b >> 3, b & 7
-            keep = jnp.where(at < total, 1.0, 0.0)
+            keep = jnp.where(first + k < total, 1.0, 0.0)
             cells.append(dst_ref[pl.ds(direction[q] * 8 + j, 1), :])
             for c in range(4):
                 vals[c].append(val[q, c, pl.ds(j, 1), :] * keep)
         cell = jnp.concatenate(cells, axis=1)
         vals = [jnp.concatenate(v, axis=1) for v in vals]
         acc[...] += spread(extent, place((cell >> 7) & 511), cell & 127, vals)
-        return carry
-
-    lax.fori_loop(0, (total + width - 1) // width, chunk, 0)
+
+    run_chunks(total, large, small, chunk)
 
 
 def make_first_scatter(count_y):
@@ -204,7 +214,7 @@
             val[q] = ref[1]
             direction[q] = 3 * (side_x * (q - 1) + 1) + 1
         acc[...] = jnp.zeros_like(acc)
-        scatter_lists(val, 3, direction, dst_ref, listed, acc, 512, lambda row: row)
+        scatter_lists(val, 3, direction, dst_ref, listed, acc, 512, lambda row: row, 12, 4)
 
     return kernel
 
@@ -230,7 +240,7 @@
         acc[0:128, :] = base_ref[0:128, :]
         acc[128:256, :] = base_ref[384:512, :]
         place = lambda row: jnp.where(row < 128, row, jnp.where(row >= 384, row - 256, 512))
-        scatter_lists(val, 6, direction, dst_ref, listed, acc, 256, place, 6)
+        scatter_lists(val, 6, direction, dst_ref, listed, acc, 256, place, 12, 4)
         side_x, _ = sides(mine_ref, count_y)
         for c in range(3):
             vel = jnp.concatenate([vel_ref[c, 0:128, :], vel_ref[c, 384:512, :]], axis=0)
@@ -246,7 +256,7 @@
     def kernel(mine_ref, base_ref, first_ref, second_ref, dst_ref, vel_ref, outer_ref, cor_ref, fa_ref, fb_ref, acc, val, listed, direction):
         load_later_lists(mine_ref, count_y, first_ref, second_ref, val, direction)
         acc[...] = base_ref[128:384, :]
-        scatter_lists(val, 6, direction, dst_ref, listed, acc, 256, lambda row: row - 128, 6)
+        scatter_lists(val, 6, direction, dst_ref, listed, acc, 256, lambda row: row - 128, 12, 4)
         _, side_y = sides(mine_ref, count_y)
         for c in range(3):
             cor_ref[c] = corrected(acc, vel_ref[c, 128:384, :], c)
@@ -361,12 +371,12 @@
 
     whole = ((72, 128), jnp.int32, VMEM)
     far, table, vel, src, weight, dst = call(
-        make_far_gather(count_y, 6),
+        make_far_gather(count_y, 12, 4),
         "far_gather",
         [((6, 4, 8, 128), F32, VMEM), ((3, 256, 512), BF16, VMEM), ((3, 512, 128), F32, VMEM), whole, ((72, 128), F32, VMEM), whole],
         [SMEM] + [HBM] * 5,
         (mine,) + tuple(pltpu.with_memory_space_constraint(v, pltpu.HBM) for v in (counts, vel, src, weight, dst)),
-        [pltpu.SemaphoreType.DMA((7,)), pltpu.SMEM((1, 1, 9), jnp.int32), ints(64), ints(8)],
+        [pltpu.SemaphoreType.DMA((7,)), pltpu.SMEM((1, 1, 9), jnp.int32), ints(72), ints(8)],
         flops=5 * 10**9,
     )
     low = swap(far[0:3], "gx", 1)
@@ -381,12 +391,12 @@
         flops=10**9,
     )
     (own,) = call(
-        make_near_gather(count_y, 4),
+        make_near_gather(count_y, 8, 4),
         "near_gather",
         [((3, 4, 8, 128), F32, VMEM)],
         [SMEM, SMEM] + [VMEM] * 3,
         (mine, counts, table, src, weight),
-        [ints(40), ints(8)],
+        [ints(48), ints(8)],
         flops=4 * 10**9,
     )
     for axis, count in (("gx", count_x), ("gy", count_y)):
@@ -408,12 +418,12 @@
         [((512, 512), F32, VMEM)],
         [SMEM] + [VMEM] * 4,
         (mine, low, own, high, dst),
-        [pltpu.VMEM((3, 4, 8, 128), F32), ints(40), ints(8)],
+        [pltpu.VMEM((3, 4, 8, 128), F32), ints(48), ints(8)],
         flops=4 * 10**9,
     )
     rotor = rotor + second[96:]
     rotor = rotor + swap(rotor, "gx", 2)
-    half_scratch = [pltpu.VMEM((256, 512), F32), pltpu.VMEM((6, 4, 8, 128), F32), ints(64), ints(8)]
+    half_scratch = [pltpu.VMEM((256, 512), F32), pltpu.VMEM((6, 4, 8, 128), F32), ints(72), ints(8)]
     outer, fa, fb = call(
         make_outer_scatter(count_y),
         "outer_scatter",

time: 43.9 us -> 42.1 us (0.959); the launches traced: 44.1 us -> 41.7 us
  waiting for transfers between devices: 3.08 us -> 10.2 us
  Pallas kernels: 24.7 us -> 19.2 us
  starting transfers between devices: 14.7 us -> 10.7 us
    pallas_call x8, Pallas kernels: 24.7 us -> 19.2 us  [call(): pl.pallas_call(kernel, out_shape=tuple((jax.ShapeDtypeStruct(shape, dtype...]
    ppermute x4, starting transfers between devices: 9.23 us -> 4.61 us  [swap_next(): lax.ppermute(value, axis, [(i, (i - 1 if i % 2 == 0 else i + 1) % count)...]
    ppermute x4, waiting for transfers between devices: 0.49 us -> 4.44 us  [swap_next(): lax.ppermute(value, axis, [(i, (i - 1 if i % 2 == 0 else i + 1) % count)...]
    ppermute x6, waiting for transfers between devices: 2.59 us -> 5.78 us  [swap(): return lax.ppermute(value, axis, [(i, i ^ step) for i in range(count)])]
    ppermute x6, starting transfers between devices: 5.45 us -> 6.12 us  [swap(): return lax.ppermute(value, axis, [(i, i ^ step) for i in range(count)])]
  transfers between devices with their start and end apart: 10 -> 10, of which waited for: 3 -> 7; matrix products, arithmetic and copies ran while one was open for 0% -> 0% of each run, Pallas kernels for 38% -> 25%
where the time goes in v5:
time: 42.1 us; the launch traced here: 41.7 us
  Pallas kernels  19.2 us (46%)
  starting transfers between devices  10.7 us (25%)
  waiting for transfers between devices  10.2 us (24%)
  between operations  0.77 us (2%)
  local copies, waits for them, and re-layouts  0.69 us (2%)
    pallas_call x8, Pallas kernels, call(): pl.pallas_call(kernel, out_shape=tuple((jax.ShapeDtypeStruct(shape, dtype...  19.2 us
    ppermute x6, starting transfers between devices, swap(): return lax.ppermute(value, axis, [(i, i ^ step) for i in range(count)])  6.12 us
    ppermute x6, waiting for transfers between devices, swap(): return lax.ppermute(value, axis, [(i, i ^ step) for i in range(count)])  5.78 us
    ppermute x4, starting transfers between devices, swap_next(): lax.ppermute(value, axis, [(i, (i - 1 if i % 2 == 0 else i + 1) % count)...  4.61 us
    ppermute x4, waiting for transfers between devices, swap_next(): lax.ppermute(value, axis, [(i, (i - 1 if i % 2 == 0 else i + 1) % count)...  4.44 us
  transfers between devices with their start and end apart: 10, of which 7 were waited for; matrix products, arithmetic and copies ran while one was open for 0% of the time, Pallas kernels for 25%

profile of v5, /device:TPU:0, one launch (start us, length us, event | category | flops | bytes accessed | tf_op | source)
XLA Modules:
  0.0 41.7 jit_solution(16346690319871673401)
XLA Ops:
  0.6 0.0 copy-start
  0.6 0.0 copy-start.1
  0.7 6.8 %far_gather.1 = (f32[6,4,8,128]{3,2,1,0:T(8,128)S(1)}, bf16[3,256,512]{2,1,0:T(8,128)(2,1)S(1)}, f32[3,512,128]{2,1,0:T(8,128)S(1)}, s32[72,128]{1,0:T(8,128)S(1...) custom-call(s32[1]{0:T(128)} %bitcast.mine_ref, s32[1,1,9]{2,1,0:T(1,128)} %cnt_ref.1, f32[3,512,128]{2,1,0:T(8,128)} %bitcast.22, ...), custom_call_target="tpu_custom_call" | custom-call | flops 5000000000 | bytes 100000 | tf_op jit(solution)/shard_map/far_gather/pallas_call | solution.py:349
  7.5 0.0 copy-done
  7.5 0.0 copy-done.1
  7.5 0.2 points.1
  7.7 3.2 %collective-permute-start.2 = (f32[24,128]{1,0:T(8,128)S(1)}, f32[24,128]{1,0:T(8,128)S(1)}, u32[]{:S(2)}, u32[]{:S(2)}) collective-permute-start(f32[24,128]{1,0:T(8,128)S(1)} %get-tuple-element.27), channel_id=1, source_target_pairs={{0,16},{4,20},{8,24},{12,28},{16,0},{20,4},{24,8},{28,12},{1,17},{... | collective-permute-start | bytes 36872 | tf_op jit(solution)/shard_map/ppermute | solution.py:340
  10.9 2.3 %collective-permute-start.1 = (f32[3,4,8,128]{3,2,1,0:T(8,128)S(1)}, f32[3,4,8,128]{3,2,1,0:T(8,128)S(1)}, u32[]{:S(2)}, u32[]{:S(2)}) collective-permute-start(f32[3,4,8,128]{3,2,1,0:T(8,128)S(1)} %get-tuple-element.42), channel_id=1, source_target_pairs={{0,28},{4,8},{8,4},{12,16},{16,12},{20,24},{24,20},{28,0},{1,29},{... | collective-permute-start | bytes 147464 | tf_op jit(solution)/shard_map/ppermute | solution.py:345
  13.2 0.3 collective-permute-start
  13.5 0.0 copy-start.3
  13.5 0.7 %copy-done.3 = s32[1,1,9]{2,1,0:T(1,128)S(1)} copy-done((s32[1,1,9]{2,1,0:T(1,128)S(1)}, s32[1,1,9]{2,1,0:T(1,128)}, u32[]{:S(2)}) %copy-start.3) | copy-done | bytes 60
  14.2 2.8 %near_gather.1.own_ref = f32[3,4,8,128]{3,2,1,0:T(8,128)S(1)} custom-call(s32[1]{0:T(128)} %bitcast.mine_ref, s32[1,1,9]{2,1,0:T(1,128)S(1)} %copy-done.3, bf16[3,256,512]{2,1,0:T(8,128)(2,1)S(1)} %get-tuple-element.23.table, s32[72,128]{1,0:T(8,128)S(1)} %get-tuple-element.24.src_ref, f32[72,128]{1,0:T(8,128)S(1)} %get-tuple-element.25.w_ref), custom_call_target="tpu_custom_call" | custom-call | flops 4000000000 | bytes 100000 | tf_op jit(solution)/shard_map/near_gather/pallas_call | solution.py:349
  17.0 0.0 collective-permute-done.2
  17.0 0.8 %collective-permute-done.1.high_ref = f32[3,4,8,128]{3,2,1,0:T(8,128)S(1)} collective-permute-done((f32[3,4,8,128]{3,2,1,0:T(8,128)S(1)}, f32[3,4,8,128]{3,2,1,0:T(8,128)S(1)}, u32[]{:S(2)}, u32[]{:S(2)}) %collective-permute-start.1) | collective-permute-done | bytes 49184 | tf_op jit(solution)/shard_map/ppermute | solution.py:345
  17.8 0.3 collective-permute-done.low_ref
  18.1 0.1 collective-permute-start.3
  18.2 1.2 %collective-permute-done.3.first_ref = f32[120,128]{1,0:T(8,128)S(1)} collective-permute-done((f32[120,128]{1,0:T(8,128)S(1)}, f32[120,128]{1,0:T(8,128)S(1)}, u32[]{:S(2)}, u32[]{:S(2)}) %collective-permute-start.3) | collective-permute-done | bytes 61472 | tf_op jit(solution)/shard_map/ppermute | solution.py:340
  19.5 0.4 %collective-permute-start.4 = (f32[120,128]{1,0:T(8,128)S(1)}, f32[120,128]{1,0:T(8,128)S(1)}, u32[]{:S(2)}, u32[]{:S(2)}) collective-permute-start(f32[120,128]{1,0:T(8,128)S(1)} %pad_maximum_fusion.2), channel_id=1, source_target_pairs={{0,3},{1,2},{2,1},{3,0},{4,7},{5,6},{6,5},{7,4},{8,11},{9,10},{10,... | collective-permute-start | bytes 184328 | tf_op jit(solution)/shard_map/ppermute | solution.py:345
  19.9 2.0 %first_scatter.1.base_ref = f32[512,512]{1,0:T(8,128)S(1)} custom-call(s32[1]{0:T(128)} %bitcast.mine_ref, f32[3,4,8,128]{3,2,1,0:T(8,128)S(1)} %collective-permute-done.low_ref, f32[3,4,8,128]{3,2,1,0:T(8,128)S(1)} %near_gather.1.own_ref, f32[3,4,8,128]{3,2,1,0:T(8,128)S(1)} %collective-permute-done.1.high_ref, s32[72,128]{1,0:T(8,128)S(1)} %get-tuple-element.26.dst_ref), custom_call_target="tpu_custom_call" | custom-call | flops 4000000000 | bytes 100000 | tf_op jit(solution)/shard_map/first_scatter/pallas_call | solution.py:349
  21.9 1.6 %collective-permute-done.4.second_ref = f32[120,128]{1,0:T(8,128)S(1)} collective-permute-done((f32[120,128]{1,0:T(8,128)S(1)}, f32[120,128]{1,0:T(8,128)S(1)}, u32[]{:S(2)}, u32[]{:S(2)}) %collective-permute-start.4) | collective-permute-done | bytes 61472 | tf_op jit(solution)/shard_map/ppermute | solution.py:345
  23.5 1.5 %collective-permute-start.5 = (f32[24,128]{1,0:T(8,128)S(1)}, f32[24,128]{1,0:T(8,128)S(1)}, u32[]{:S(2)}, u32[]{:S(2)}) collective-permute-start(f32[24,128]{1,0:T(8,128)S(1)} %slice_add_fusion.1), channel_id=1, source_target_pairs={{0,8},{4,12},{8,0},{12,4},{16,24},{20,28},{24,16},{28,20},{1,9},{5... | collective-permute-start | bytes 36872 | tf_op jit(solution)/shard_map/ppermute | solution.py:340
  25.0 2.8 %outer_scatter.1 = (f32[3,256,128]{2,1,0:T(8,128)S(1)}, f32[3,64,128]{2,1,0:T(8,128)S(1)}, f32[3,64,128]{2,1,0:T(8,128)S(1)}) custom-call(s32[1]{0:T(128)} %bitcast.mine_ref, f32[512,512]{1,0:T(8,128)S(1)} %first_scatter.1.base_ref, f32[120,128]{1,0:T(8,128)S(1)} %collective-permute-done.3.first_ref, f32[120,128]{1,0:T(8,128)S(1)} %collective-permute-done.4.second_ref, ...), custom_call_target="tpu_custom_call" | custom-call | flops 4000000000 | bytes 100000 | tf_op jit(solution)/shard_map/outer_scatter/pallas_call | solution.py:349
  27.9 1.1 %collective-permute-start.7 = (f32[192,128]{1,0:T(8,128)S(1)}, f32[192,128]{1,0:T(8,128)S(1)}, u32[]{:S(2)}, u32[]{:S(2)}) collective-permute-start(f32[192,128]{1,0:T(8,128)S(1)} %bitcast.21), channel_id=1, source_target_pairs={{0,28},{4,8},{8,4},{12,16},{16,12},{20,24},{24,20},{28,0},{1,29},{... | collective-permute-start | bytes 294920 | tf_op jit(solution)/shard_map/ppermute | solution.py:345
  29.0 0.0 collective-permute-done.5
  29.0 1.0 %collective-permute-start.6 = (f32[216,128]{1,0:T(8,128)S(1)}, f32[216,128]{1,0:T(8,128)S(1)}, u32[]{:S(2)}, u32[]{:S(2)}) collective-permute-start(f32[216,128]{1,0:T(8,128)S(1)} %pad_maximum_fusion), channel_id=1, source_target_pairs={{0,4},{4,0},{8,12},{12,8},{16,20},{20,16},{24,28},{28,24},{1,5},{5... | collective-permute-start | bytes 331784 | tf_op jit(solution)/shard_map/ppermute | solution.py:340
  30.0 2.9 %inner_scatter.1 = (f32[3,256,128]{2,1,0:T(8,128)S(1)}, f32[3,8,128]{2,1,0:T(8,128)S(1)}, f32[3,8,128]{2,1,0:T(8,128)S(1)}) custom-call(s32[1]{0:T(128)} %bitcast.mine_ref, f32[512,512]{1,0:T(8,128)S(1)} %first_scatter.1.base_ref, f32[120,128]{1,0:T(8,128)S(1)} %collective-permute-done.3.first_ref, f32[120,128]{1,0:T(8,128)S(1)} %collective-permute-done.4.second_ref, ...), custom_call_target="tpu_custom_call" | custom-call | flops 4000000000 | bytes 100000 | tf_op jit(solution)/shard_map/inner_scatter/pallas_call | solution.py:349
  32.8 0.0 copy-start.2
  32.8 4.1 %collective-permute-done.6.xa_ref = f32[216,128]{1,0:T(8,128)S(1)} collective-permute-done((f32[216,128]{1,0:T(8,128)S(1)}, f32[216,128]{1,0:T(8,128)S(1)}, u32[]{:S(2)}, u32[]{:S(2)}) %collective-permute-start.6) | collective-permute-done | bytes 110624 | tf_op jit(solution)/shard_map/ppermute | solution.py:340
  36.9 0.0 collective-permute-done.7.xb_ref
  36.9 0.1 collective-permute-start.8
  37.0 0.7 %collective-permute-start.9 = (f32[3,8,128]{2,1,0:T(8,128)S(1)}, f32[3,8,128]{2,1,0:T(8,128)S(1)}, u32[]{:S(2)}, u32[]{:S(2)}) collective-permute-start(f32[3,8,128]{2,1,0:T(8,128)S(1)} %get-tuple-element.39), channel_id=1, source_target_pairs={{0,3},{1,2},{2,1},{3,0},{4,7},{5,6},{6,5},{7,4},{8,11},{9,10},{10,... | collective-permute-start | bytes 36872 | tf_op jit(solution)/shard_map/ppermute | solution.py:345
  37.7 0.0 copy-done.2
  37.7 0.2 forcing.1.frc_ref
  37.9 0.2 collective-permute-done.8.ya_ref
  38.1 2.0 %collective-permute-done.9.yb_ref = f32[3,8,128]{2,1,0:T(8,128)S(1)} collective-permute-done((f32[3,8,128]{2,1,0:T(8,128)S(1)}, f32[3,8,128]{2,1,0:T(8,128)S(1)}, u32[]{:S(2)}, u32[]{:S(2)}) %collective-permute-start.9) | collective-permute-done | bytes 12320 | tf_op jit(solution)/shard_map/ppermute | solution.py:345
  40.1 1.5 %stencil.1 = (f32[3,8,64,128]{3,2,1,0:T(8,128)}, f32[3,512,128]{2,1,0:T(8,128)}) custom-call(s32[1]{0:T(128)} %bitcast.mine_ref, f32[3,256,128]{2,1,0:T(8,128)S(1)} %get-tuple-element.29.outer_ref, f32[3,256,128]{2,1,0:T(8,128)S(1)} %get-tuple-element.30.inner_ref, f32[3,512,128]{2,1,0:T(8,128)S(1)} %forcing.1.frc_ref, ...), custom_call_target="tpu_custom_call" | custom-call | flops 1000000000 | bytes 100000 | tf_op jit(solution)/shard_map/stencil/pallas_call | solution.py:349
  (12 shorter events, 0.1 us)
Async XLA Ops:
  0.6 6.8 %copy-start = (s32[20,192]{1,0:T(8,128)S(1)}, s32[20,192]{1,0:T(8,128)}, u32[]{:S(2)}) copy-start(s32[20,192]{1,0:T(8,128)} %tile_ref.3) | copy-start | bytes 46084
  0.6 6.8 %copy-start.1 = (s32[20,192]{1,0:T(8,128)S(1)}, s32[20,192]{1,0:T(8,128)}, u32[]{:S(2)}) copy-start(s32[20,192]{1,0:T(8,128)} %cell_ref.3) | copy-start | bytes 46084
  7.7 9.2 %collective-permute-start.2 = (f32[24,128]{1,0:T(8,128)S(1)}, f32[24,128]{1,0:T(8,128)S(1)}, u32[]{:S(2)}, u32[]{:S(2)}) collective-permute-start(f32[24,128]{1,0:T(8,128)S(1)} %get-tuple-element.27), channel_id=1, source_target_pairs={{0,16},{4,20},{8,24},{12,28},{16,0},{20,4},{24,8},{28,12},{1,17},{... | collective-permute-start | bytes 36872 | tf_op jit(solution)/shard_map/ppermute | solution.py:340
  10.9 6.9 %collective-permute-start.1 = (f32[3,4,8,128]{3,2,1,0:T(8,128)S(1)}, f32[3,4,8,128]{3,2,1,0:T(8,128)S(1)}, u32[]{:S(2)}, u32[]{:S(2)}) collective-permute-start(f32[3,4,8,128]{3,2,1,0:T(8,128)S(1)} %get-tuple-element.42), channel_id=1, source_target_pairs={{0,28},{4,8},{8,4},{12,16},{16,12},{20,24},{24,20},{28,0},{1,29},{... | collective-permute-start | bytes 147464 | tf_op jit(solution)/shard_map/ppermute | solution.py:345
  13.2 4.9 %collective-permute-start = (f32[3,4,8,128]{3,2,1,0:T(8,128)S(1)}, f32[3,4,8,128]{3,2,1,0:T(8,128)S(1)}, u32[]{:S(2)}, u32[]{:S(2)}) collective-permute-start(f32[3,4,8,128]{3,2,1,0:T(8,128)S(1)} %get-tuple-element.43), channel_id=1, source_target_pairs={{0,4},{4,0},{8,12},{12,8},{16,20},{20,16},{24,28},{28,24},{1,5},{5... | collective-permute-start | bytes 147464 | tf_op jit(solution)/shard_map/ppermute | solution.py:340
  13.5 0.7 %copy-start.3 = (s32[1,1,9]{2,1,0:T(1,128)S(1)}, s32[1,1,9]{2,1,0:T(1,128)}, u32[]{:S(2)}) copy-start(s32[1,1,9]{2,1,0:T(1,128)} %cnt_ref.1) | copy-start | bytes 112
  18.1 1.3 %collective-permute-start.3 = (f32[120,128]{1,0:T(8,128)S(1)}, f32[120,128]{1,0:T(8,128)S(1)}, u32[]{:S(2)}, u32[]{:S(2)}) collective-permute-start(f32[120,128]{1,0:T(8,128)S(1)} %pad_maximum_fusion.1), channel_id=1, source_target_pairs={{0,1},{1,0},{2,3},{3,2},{4,5},{5,4},{6,7},{7,6},{8,9},{9,8},{10,11... | collective-permute-start | bytes 184328 | tf_op jit(solution)/shard_map/ppermute | solution.py:340
  19.5 4.0 %collective-permute-start.4 = (f32[120,128]{1,0:T(8,128)S(1)}, f32[120,128]{1,0:T(8,128)S(1)}, u32[]{:S(2)}, u32[]{:S(2)}) collective-permute-start(f32[120,128]{1,0:T(8,128)S(1)} %pad_maximum_fusion.2), channel_id=1, source_target_pairs={{0,3},{1,2},{2,1},{3,0},{4,7},{5,6},{6,5},{7,4},{8,11},{9,10},{10,... | collective-permute-start | bytes 184328 | tf_op jit(solution)/shard_map/ppermute | solution.py:345
  23.5 5.5 %collective-permute-start.5 = (f32[24,128]{1,0:T(8,128)S(1)}, f32[24,128]{1,0:T(8,128)S(1)}, u32[]{:S(2)}, u32[]{:S(2)}) collective-permute-start(f32[24,128]{1,0:T(8,128)S(1)} %slice_add_fusion.1), channel_id=1, source_target_pairs={{0,8},{4,12},{8,0},{12,4},{16,24},{20,28},{24,16},{28,20},{1,9},{5... | collective-permute-start | bytes 36872 | tf_op jit(solution)/shard_map/ppermute | solution.py:340
  27.9 9.1 %collective-permute-start.7 = (f32[192,128]{1,0:T(8,128)S(1)}, f32[192,128]{1,0:T(8,128)S(1)}, u32[]{:S(2)}, u32[]{:S(2)}) collective-permute-start(f32[192,128]{1,0:T(8,128)S(1)} %bitcast.21), channel_id=1, source_target_pairs={{0,28},{4,8},{8,4},{12,16},{16,12},{20,24},{24,20},{28,0},{1,29},{... | collective-permute-start | bytes 294920 | tf_op jit(solution)/shard_map/ppermute | solution.py:345
  29.0 7.9 %collective-permute-start.6 = (f32[216,128]{1,0:T(8,128)S(1)}, f32[216,128]{1,0:T(8,128)S(1)}, u32[]{:S(2)}, u32[]{:S(2)}) collective-permute-start(f32[216,128]{1,0:T(8,128)S(1)} %pad_maximum_fusion), channel_id=1, source_target_pairs={{0,4},{4,0},{8,12},{12,8},{16,20},{20,16},{24,28},{28,24},{1,5},{5... | collective-permute-start | bytes 331784 | tf_op jit(solution)/shard_map/ppermute | solution.py:340
  32.8 4.9 %copy-start.2 = (f32[20,192]{1,0:T(8,128)S(1)}, f32[20,192]{1,0:T(8,128)}, u32[]{:S(2)}) copy-start(f32[20,192]{1,0:T(8,128)} %coef_ref.1) | copy-start | bytes 46084
  36.9 1.2 %collective-permute-start.8 = (f32[3,8,128]{2,1,0:T(8,128)S(1)}, f32[3,8,128]{2,1,0:T(8,128)S(1)}, u32[]{:S(2)}, u32[]{:S(2)}) collective-permute-start(f32[3,8,128]{2,1,0:T(8,128)S(1)} %get-tuple-element.38), channel_id=1, source_target_pairs={{0,1},{1,0},{2,3},{3,2},{4,5},{5,4},{6,7},{7,6},{8,9},{9,8},{10,11... | collective-permute-start | bytes 36872 | tf_op jit(solution)/shard_map/ppermute | solution.py:340
  37.0 3.1 %collective-permute-start.9 = (f32[3,8,128]{2,1,0:T(8,128)S(1)}, f32[3,8,128]{2,1,0:T(8,128)S(1)}, u32[]{:S(2)}, u32[]{:S(2)}) collective-permute-start(f32[3,8,128]{2,1,0:T(8,128)S(1)} %get-tuple-element.39), channel_id=1, source_target_pairs={{0,3},{1,2},{2,1},{3,0},{4,7},{5,6},{6,5},{7,4},{8,11},{9,10},{10,... | collective-permute-start | bytes 36872 | tf_op jit(solution)/shard_map/ppermute | solution.py:345

commit v6 on v5

--- a/solution.py
+++ b/solution.py
@@ -79,7 +79,7 @@
     lax.fori_loop(0, jnp.maximum(total - many * large + small - 1, 0) // small, rest, 0)
 
 
-def gather_lists(table, total, large, small, listed, direction, cnt_ref, src_ref, w_ref, out_ref):
+def gather_lists(table, total, large, small, listed, direction, src_ref, w_ref, out_ref):
     for k in range(large):
         listed[total + k] = listed[total - 1]
 
@@ -88,11 +88,9 @@
         rows = [direction[b >> 3] * 8 + (b & 7) for b in blocks]
         cell = jnp.concatenate([src_ref[pl.ds(r, 1), :] for r in rows], axis=1)
         found = pick(table, cell)
-        lane = lax.broadcasted_iota(jnp.int32, (1, 128), 1)
         for k, (b, r) in enumerate(zip(blocks, rows)):
-            used = cnt_ref[0, 0, r >> 3]
             j = b & 7
-            weight = jnp.where(lane + j * 128 < used, w_ref[pl.ds(r, 1), :], 0.0)
+            weight = w_ref[pl.ds(r, 1), :]
             for c in range(3):
                 out_ref[b >> 3, c, pl.ds(j, 1), :] = found[c][:, k * 128 : (k + 1) * 128] * weight
             out_ref[b >> 3, 3, pl.ds(j, 1), :] = weight
@@ -101,16 +99,27 @@
 
 
 def make_far_gather(count_y, large, small):
-    def kernel(mine_ref, cnt_hbm, vel_hbm, src_hbm, w_hbm, dst_hbm, out_ref, table, vel_ref, src_ref, w_ref, dst_ref, sem, cnt_ref, listed, direction):
+    def kernel(
+        mine_ref, cnt_hbm, vel_hbm, src_hbm, w_hbm, dst_hbm, tile_hbm, cell_hbm,
+        out_ref, table, vel_ref, src_ref, w_ref, dst_ref, tile_ref, cell_ref, pts_ref, rot_ref,
+        sem, cnt_ref, listed, direction, tlist,
+    ):
         half = vel_ref.shape[1] // 2
-        pairs = [(cnt_hbm, cnt_ref), (src_hbm, src_ref)]
+        pairs = [(cnt_hbm, cnt_ref), (src_hbm, src_ref), (w_hbm, w_ref)]
         pairs += [(vel_hbm.at[c], vel_ref.at[c]) for c in range(3)]
-        pairs += [(w_hbm, w_ref), (dst_hbm, dst_ref)]
+        pairs += [(tile_hbm, tile_ref), (cell_hbm, cell_ref), (dst_hbm, dst_ref)]
         copies = [pltpu.make_async_copy(a, b, sem.at[k]) for k, (a, b) in enumerate(pairs)]
         for copy in copies:
             copy.start()
         out_ref[...] = jnp.zeros_like(out_ref)
-        copies[0].wait()
+        pts_ref[...] = jnp.zeros_like(pts_ref)
+        rot_ref[...] = jnp.zeros_like(rot_ref)
+        for copy in copies[:3]:
+            copy.wait()
+        slot = lax.broadcasted_iota(jnp.int32, (8, 128), 0) * 128 + lax.broadcasted_iota(jnp.int32, (8, 128), 1)
+        for d in range(9):
+            part = slice(d * 8, d * 8 + 8)
+            w_ref[part, :] = jnp.where(slot < cnt_ref[0, 0, d], w_ref[part, :], 0.0)
         side_x, side_y = sides(mine_ref, count_y)
         lists = []
         for s in range(2):
@@ -119,16 +128,16 @@
                 direction[3 * s + t] = d
                 lists.append((cnt_ref[0, 0, d], 3 * s + t))
         total = list_blocks(lists, listed)
-        copies[1].wait()
         for c in range(3):
-            copies[2 + c].wait()
+            copies[3 + c].wait()
             for piece in range(2):
                 high, low = halves(vel_ref[c, piece * half : (piece + 1) * half, :])
                 table[c, :, piece * 128 : (piece + 1) * 128] = high
                 table[c, :, 256 + piece * 128 : 256 + (piece + 1) * 128] = low
-        copies[5].wait()
-        gather_lists(table, total, large, small, listed, direction, cnt_ref, src_ref, w_ref, out_ref)
-        copies[6].wait()
+        for copy in copies[6:]:
+            copy.wait()
+        gather_lists(table, total, large, small, listed, direction, src_ref, w_ref, out_ref)
+        gather_points(mine_ref[0], table, tile_ref, cell_ref, pts_ref, rot_ref, tlist)
 
     return kernel
 
@@ -145,10 +154,8 @@
     return total
 
 
-def points_kernel(mine_ref, table, tile_ref, cell_ref, pts_ref, rot_ref, tlist):
+def gather_points(mine, table, tile_ref, cell_ref, pts_ref, rot_ref, tlist):
     turbines, points = tile_ref.shape
-    pts_ref[...] = jnp.zeros_like(pts_ref)
-    mine = mine_ref[0]
     n_turb = active_turbines(tile_ref, mine, tlist)
 
     def turbine(i, carry):
@@ -162,22 +169,25 @@
         return carry
 
     lax.fori_loop(0, (n_turb + 1) >> 1, turbine, 0)
-    rot_ref[...] = jnp.zeros_like(rot_ref)
     sums = jnp.sum(pts_ref[0], axis=1, keepdims=True)
     rot_ref[0:turbines, :] = jnp.broadcast_to(sums, (turbines, 128))
 
 
+def used_slots(weight):
+    return jnp.sum(jnp.where(weight != 0.0, 1.0, 0.0)).astype(jnp.int32)
+
+
 def make_near_gather(count_y, large, small):
-    def kernel(mine_ref, cnt_ref, table, src_ref, w_ref, out_ref, listed, direction):
+    def kernel(mine_ref, table, src_ref, w_ref, out_ref, listed, direction):
         out_ref[...] = jnp.zeros_like(out_ref)
         _, side_y = sides(mine_ref, count_y)
-        lists = []
+        used = [used_slots(w_ref[d * 8 : d * 8 + 8, :]) for d in (3, 4, 5)]
+        last = jnp.where(side_y > 0, used[0], used[2])
+        lists = [(jnp.where(side_y > 0, used[2], used[0]), 0), (used[1], 1), (last, 2)]
         for t in range(3):
-            d = 3 + side_y * (1 - t) + 1
-            direction[t] = d
-            lists.append((cnt_ref[0, 0, d], t))
+            direction[t] = 3 + side_y * (1 - t) + 1
         total = list_blocks(lists, listed)
-        gather_lists(table, total, large, small, listed, direction, cnt_ref, src_ref, w_ref, out_ref)
+        gather_lists(table, total, large, small, listed, direction, src_ref, w_ref, out_ref)
 
     return kernel
 
@@ -185,8 +195,7 @@
 def scatter_lists(val, n_lists, direction, dst_ref, listed, acc, extent, place, large, small):
     lists = []
     for q in range(n_lists):
-        used = jnp.sum(jnp.where(val[q, 3] != 0.0, 1.0, 0.0)).astype(jnp.int32)
-        lists.append((used, q))
+        lists.append((used_slots(val[q, 3]), q))
     total = list_blocks(lists, listed)
     for k in range(large):
         listed[total + k] = 0
@@ -211,7 +220,8 @@
     def kernel(mine_ref, low_ref, own_ref, high_ref, dst_ref, acc, val, listed, direction):
         side_x, _ = sides(mine_ref, count_y)
         for q, ref in enumerate((low_ref, own_ref, high_ref)):
-            val[q] = ref[1]
+            for c in range(4):
+                val[q, c] = ref[32 + c * 8 : 40 + c * 8, :]
             direction[q] = 3 * (side_x * (q - 1) + 1) + 1
         acc[...] = jnp.zeros_like(acc)
         scatter_lists(val, 3, direction, dst_ref, listed, acc, 512, lambda row: row, 12, 4)
@@ -234,45 +244,56 @@
     return (1.0 - acc[:, 384:512]) * vel - acc[:, c * 128 : (c + 1) * 128]
 
 
-def make_outer_scatter(count_y):
-    def kernel(mine_ref, base_ref, first_ref, second_ref, dst_ref, vel_ref, cor_ref, fa_ref, fb_ref, acc, val, listed, direction):
+def edge_rows(ref, c, columns):
+    at = (lambda r: ref[r, columns]) if c is None else (lambda r: ref[c, r, columns])
+    spare = [at(slice(0, 2))]
+    low = [at(slice(x * 64, x * 64 + 1)) for x in range(1, 7)]
+    high = [at(slice(x * 64 + 63, x * 64 + 64)) for x in range(1, 7)]
+    return jnp.concatenate([at(slice(0, 64)), at(slice(448, 512))] + low + spare + high + spare, axis=0)
+
+
+def edge_place(row):
+    x, y = row >> 6, row & 63
+    inside = jnp.where(y == 0, 127 + x, jnp.where(y == 63, 135 + x, 1024))
+    return jnp.where(x == 0, y, jnp.where(x == 7, 64 + y, inside))
+
+
+def make_edge_scatter(count_y):
+    def kernel(
+        mine_ref, base_ref, first_ref, second_ref, dst_ref, vel_ref,
+        cor_ref, xa_ref, xb_ref, ya_ref, yb_ref, acc, val, listed, direction,
+    ):
         load_later_lists(mine_ref, count_y, first_ref, second_ref, val, direction)
-        acc[0:128, :] = base_ref[0:128, :]
-        acc[128:256, :] = base_ref[384:512, :]
-        place = lambda row: jnp.where(row < 128, row, jnp.where(row >= 384, row - 256, 512))
-        scatter_lists(val, 6, direction, dst_ref, listed, acc, 256, place, 12, 4)
-        side_x, _ = sides(mine_ref, count_y)
+        acc[...] = edge_rows(base_ref, None, slice(None))
+        scatter_lists(val, 6, direction, dst_ref, listed, acc, 144, edge_place, 12, 4)
+        side_x, side_y = sides(mine_ref, count_y)
         for c in range(3):
-            vel = jnp.concatenate([vel_ref[c, 0:128, :], vel_ref[c, 384:512, :]], axis=0)
-            cor = corrected(acc, vel, c)
-            cor_ref[c] = cor
-            fa_ref[c] = jnp.where(side_x > 0, cor[192:256], cor[0:64])
-            fb_ref[c] = jnp.where(side_x > 0, cor[0:64], cor[192:256])
+            cor = corrected(acc, edge_rows(vel_ref, c, slice(None)), c)
+            cor_ref[c] = cor[0:128]
+            xa_ref[c] = jnp.where(side_x > 0, cor[64:128], cor[0:64])
+            xb_ref[c] = jnp.where(side_x > 0, cor[0:64], cor[64:128])
+            low = jnp.concatenate([cor[0:1], cor[128:134], cor[64:65]], axis=0)
+            high = jnp.concatenate([cor[63:64], cor[136:142], cor[127:128]], axis=0)
+            ya_ref[c] = jnp.where(side_y > 0, high, low)
+            yb_ref[c] = jnp.where(side_y > 0, low, high)
 
     return kernel
 
 
 def make_inner_scatter(count_y):
-    def kernel(mine_ref, base_ref, first_ref, second_ref, dst_ref, vel_ref, outer_ref, cor_ref, fa_ref, fb_ref, acc, val, listed, direction):
+    def kernel(mine_ref, base_ref, first_ref, second_ref, dst_ref, vel_ref, cor_ref, acc, val, listed, direction):
         load_later_lists(mine_ref, count_y, first_ref, second_ref, val, direction)
-        acc[...] = base_ref[128:384, :]
-        scatter_lists(val, 6, direction, dst_ref, listed, acc, 256, lambda row: row - 128, 12, 4)
-        _, side_y = sides(mine_ref, count_y)
+        acc[...] = base_ref[64:448, :]
+        scatter_lists(val, 6, direction, dst_ref, listed, acc, 384, lambda row: row - 64, 12, 4)
         for c in range(3):
-            cor_ref[c] = corrected(acc, vel_ref[c, 128:384, :], c)
-            for x in range(8):
-                ref, at = (cor_ref, x - 2) if 2 <= x < 6 else (outer_ref, x if x < 2 else x - 4)
-                low = ref[c, at * 64 : at * 64 + 1, :]
-                high = ref[c, at * 64 + 63 : at * 64 + 64, :]
-                fa_ref[c, x : x + 1, :] = jnp.where(side_y > 0, high, low)
-                fb_ref[c, x : x + 1, :] = jnp.where(side_y > 0, low, high)
-
-    return kernel
-
-
-def forcing_kernel(mine_ref, tile_ref, cell_ref, coef_ref, pts_ref, rot_ref, out_ref, tlist):
+            cor_ref[c] = corrected(acc, vel_ref[c, 64:448, :], c)
+
+    return kernel
+
+
+def add_forces(mine, tile_ref, cell_ref, coef_ref, pts_ref, rot_ref, out_ref, tlist):
     out_ref[...] = jnp.zeros_like(out_ref)
-    n_turb = active_turbines(tile_ref, mine_ref[0], tlist)
+    n_turb = active_turbines(tile_ref, mine, tlist)
     points = tile_ref.shape[1]
 
     def turbine(i, carry):
@@ -294,10 +315,14 @@
 
 
 def make_stencil(count_y):
-    def kernel(mine_ref, outer_ref, inner_ref, frc_ref, xa_ref, xb_ref, ya_ref, yb_ref, out_hbm, frc_hbm, out_ref, sem):
-        side_x, side_y = sides(mine_ref, count_y)
+    def kernel(
+        mine_ref, edge_ref, inner_ref, tile_ref, cell_ref, coef_ref, pts_ref, rot_ref, xa_ref, xb_ref, ya_ref, yb_ref,
+        out_hbm, frc_hbm, out_ref, frc_ref, sem, tlist,
+    ):
+        add_forces(mine_ref[0], tile_ref, cell_ref, coef_ref, pts_ref, rot_ref, frc_ref, tlist)
         given = pltpu.make_async_copy(frc_ref, frc_hbm, sem.at[8])
         given.start()
+        side_x, side_y = sides(mine_ref, count_y)
         lane = lax.broadcasted_iota(jnp.int32, (64, 128), 1)
 
         def slab(c, x):
@@ -305,7 +330,7 @@
                 return jnp.where(side_x > 0, xb_ref[c * 64 : c * 64 + 64, :], xa_ref[c * 64 : c * 64 + 64, :])
             if x > 7:
                 return jnp.where(side_x > 0, xa_ref[c * 64 : c * 64 + 64, :], xb_ref[c * 64 : c * 64 + 64, :])
-            ref, at = (inner_ref, x - 2) if 2 <= x < 6 else (outer_ref, x if x < 2 else x - 4)
+            ref, at = (inner_ref, x - 1) if 1 <= x < 7 else (edge_ref, 0 if x == 0 else 1)
             return ref[c, at * 64 : at * 64 + 64, :]
 
         copies = []
@@ -370,44 +395,35 @@
     ints = lambda n: pltpu.SMEM((n,), jnp.int32)
 
     whole = ((72, 128), jnp.int32, VMEM)
-    far, table, vel, src, weight, dst = call(
+    ints_t = (blade_tile.shape, jnp.int32, VMEM)
+    given = (counts, vel, src, weight, dst, blade_tile, blade_cell)
+    far, table, vel, src, weight, dst, tile, cell, pts, rotor = call(
         make_far_gather(count_y, 12, 4),
         "far_gather",
-        [((6, 4, 8, 128), F32, VMEM), ((3, 256, 512), BF16, VMEM), ((3, 512, 128), F32, VMEM), whole, ((72, 128), F32, VMEM), whole],
-        [SMEM] + [HBM] * 5,
-        (mine,) + tuple(pltpu.with_memory_space_constraint(v, pltpu.HBM) for v in (counts, vel, src, weight, dst)),
-        [pltpu.SemaphoreType.DMA((7,)), pltpu.SMEM((1, 1, 9), jnp.int32), ints(72), ints(8)],
+        [((6, 4, 8, 128), F32, VMEM), ((3, 256, 512), BF16, VMEM), ((3, 512, 128), F32, VMEM), whole]
+        + [((72, 128), F32, VMEM), whole, ints_t, ints_t]
+        + [((3, turbines, points), F32, VMEM), ((rows_t, 128), F32, VMEM)],
+        [SMEM] + [HBM] * 7,
+        (mine,) + tuple(pltpu.with_memory_space_constraint(v, pltpu.HBM) for v in given),
+        [pltpu.SemaphoreType.DMA((9,)), pltpu.SMEM((1, 1, 9), jnp.int32), ints(72), ints(8), ints(32)],
         flops=5 * 10**9,
     )
-    low = swap(far[0:3], "gx", 1)
-    high = swap_next(far[3:6], "gx")
-    pts, rotor = call(
-        points_kernel,
-        "points",
-        [((3, turbines, points), F32, VMEM), ((rows_t, 128), F32, VMEM)],
-        [SMEM] + [VMEM] * 3,
-        (mine, table, blade_tile, blade_cell),
-        [ints(32)],
-        flops=10**9,
-    )
+    low = swap(jnp.concatenate([far[0:3].reshape(96, 128), rotor], axis=0), "gx", 1)
+    high = swap_next(far[3:6].reshape(96, 128), "gx")
     (own,) = call(
         make_near_gather(count_y, 8, 4),
         "near_gather",
         [((3, 4, 8, 128), F32, VMEM)],
-        [SMEM, SMEM] + [VMEM] * 3,
-        (mine, counts, table, src, weight),
+        [SMEM] + [VMEM] * 3,
+        (mine, table, src, weight),
         [ints(48), ints(8)],
         flops=4 * 10**9,
     )
-    for axis, count in (("gx", count_x), ("gy", count_y)):
-        step = 4
-        while step < count:
-            rotor = rotor + swap(rotor, axis, step)
-            step *= 2
+    rotor = rotor + low[96:]
+    own = own.reshape(96, 128)
 
     def y_payload(t):
-        parts = [part[t].reshape(32, 128) for part in (low, own, high)]
-        return jnp.concatenate(parts + [rotor], axis=0)
+        return jnp.concatenate([part[t * 32 : t * 32 + 32] for part in (low, own, high)] + [rotor], axis=0)
 
     first = swap(y_payload(0), "gy", 1)
     rotor = rotor + first[96:]
@@ -422,47 +438,43 @@
         flops=4 * 10**9,
     )
     rotor = rotor + second[96:]
-    rotor = rotor + swap(rotor, "gx", 2)
-    half_scratch = [pltpu.VMEM((256, 512), F32), pltpu.VMEM((6, 4, 8, 128), F32), ints(72), ints(8)]
-    outer, fa, fb = call(
-        make_outer_scatter(count_y),
-        "outer_scatter",
-        [((3, 256, 128), F32, VMEM), ((3, 64, 128), F32, VMEM), ((3, 64, 128), F32, VMEM)],
+    for axis, count in (("gx", count_x), ("gy", count_y)):
+        step = 4
+        while step < count:
+            rotor = rotor + swap(rotor, axis, step)
+            step *= 2
+    lists = pltpu.VMEM((6, 4, 8, 128), F32)
+    face_x, face_y = ((3, 64, 128), F32, VMEM), ((3, 8, 128), F32, VMEM)
+    edge, xa, xb, ya, yb = call(
+        make_edge_scatter(count_y),
+        "edge_scatter",
+        [((3, 128, 128), F32, VMEM), face_x, face_x, face_y, face_y],
         [SMEM] + [VMEM] * 5,
         (mine, acc, first, second, dst, vel),
-        half_scratch,
+        [pltpu.VMEM((144, 512), F32), lists, ints(72), ints(8)],
         flops=4 * 10**9,
     )
-    xa = swap(jnp.concatenate([fa.reshape(192, 128), rotor], axis=0), "gx", 1)
-    xb = swap_next(fb.reshape(192, 128), "gx")
-    inner, fa, fb = call(
+    xb = swap_next(jnp.concatenate([xb.reshape(192, 128), rotor], axis=0), "gx")
+    xa = swap(xa.reshape(192, 128), "gx", 1)
+    ya = swap(ya, "gy", 1)
+    yb = swap_next(yb, "gy")
+    (inner,) = call(
         make_inner_scatter(count_y),
         "inner_scatter",
-        [((3, 256, 128), F32, VMEM), ((3, 8, 128), F32, VMEM), ((3, 8, 128), F32, VMEM)],
-        [SMEM] + [VMEM] * 6,
-        (mine, acc, first, second, dst, vel, outer),
-        half_scratch,
-        flops=4 * 10**9,
-    )
-    rotor, xb, fa, fb = lax.optimization_barrier((rotor + xa[192:], xb, fa, fb))
-    ya = swap(fa, "gy", 1)
-    yb = swap_next(fb, "gy")
-    (force,) = call(
-        forcing_kernel,
-        "forcing",
-        [((3, 512, 128), F32, VMEM)],
+        [((3, 384, 128), F32, VMEM)],
         [SMEM] + [VMEM] * 5,
-        (mine, blade_tile, blade_cell, blade_coef, pts, rotor),
-        [ints(32)],
-        flops=10**6,
-    )
+        (mine, acc, first, second, dst, vel),
+        [pltpu.VMEM((384, 512), F32), lists, ints(72), ints(8)],
+        flops=6 * 10**9,
+    )
+    rotor = rotor + xb[192:]
     updated, forcing = call(
         make_stencil(count_y),
         "stencil",
         [((3, 8, 64, 128), F32, HBM), ((3, 512, 128), F32, HBM)],
-        [SMEM] + [VMEM] * 7,
-        (mine, outer, inner, force, xa, xb, ya, yb),
-        [pltpu.VMEM((3, 8, 64, 128), F32), pltpu.SemaphoreType.DMA((9,))],
+        [SMEM] + [VMEM] * 11,
+        (mine, edge, inner, tile, cell, blade_coef, pts, rotor, xa, xb, ya, yb),
+        [pltpu.VMEM((3, 8, 64, 128), F32), pltpu.VMEM((3, 512, 128), F32), pltpu.SemaphoreType.DMA((9,)), ints(32)],
     )
     return updated, forcing.reshape(velocity.shape)
 

time: 42.1 us -> 40.7 us (0.967)
  waiting for transfers between devices: 10.2 us -> 6.7 us
  Pallas kernels: 19.2 us -> 21.5 us
  local copies, waits for them, and re-layouts: 0.69 us -> 0.03 us
    ppermute x4, starting transfers between devices: 4.61 us -> 8.99 us  [swap_next(): lax.ppermute(value, axis, [(i, (i - 1 if i % 2 == 0 else i + 1) % count)...]
    ppermute x6 -> x5, starting transfers between devices: 6.12 us -> 1.99 us  [swap(): return lax.ppermute(value, axis, [(i, i ^ step) for i in range(count)])]
    ppermute x6 -> x5, waiting for transfers between devices: 5.78 us -> 3.05 us  [swap(): return lax.ppermute(value, axis, [(i, i ^ step) for i in range(count)])]
    pallas_call x8 -> x6, Pallas kernels: 19.2 us -> 21.5 us  [call(): pl.pallas_call(kernel, out_shape=tuple((jax.ShapeDtypeStruct(shape, dtype...]
    ppermute x4, waiting for transfers between devices: 4.44 us -> 3.65 us  [swap_next(): lax.ppermute(value, axis, [(i, (i - 1 if i % 2 == 0 else i + 1) % count)...]
    unnamed x8 -> x2, local copies, waits for them, and re-layouts: 0.67 us -> 0.01 us
  transfers between devices with their start and end apart: 10 -> 9, of which waited for: 7 -> 4; matrix products, arithmetic and copies ran while one was open for 0% -> 0% of each run, Pallas kernels for 25% -> 30%
where the time goes in v6:
time: 40.7 us; the launch traced here: 40.1 us
  Pallas kernels  21.5 us (53%)
  starting transfers between devices  11 us (27%)
  waiting for transfers between devices  6.7 us (16%)
  between operations  0.77 us (2%)
    pallas_call x6, Pallas kernels, call(): pl.pallas_call(kernel, out_shape=tuple((jax.ShapeDtypeStruct(shape, dtype...  21.5 us
    ppermute x4, starting transfers between devices, swap_next(): lax.ppermute(value, axis, [(i, (i - 1 if i % 2 == 0 else i + 1) % count)...  8.99 us
    ppermute x4, waiting for transfers between devices, swap_next(): lax.ppermute(value, axis, [(i, (i - 1 if i % 2 == 0 else i + 1) % count)...  3.65 us
    ppermute x5, waiting for transfers between devices, swap(): return lax.ppermute(value, axis, [(i, i ^ step) for i in range(count)])  3.05 us
    ppermute x5, starting transfers between devices, swap(): return lax.ppermute(value, axis, [(i, i ^ step) for i in range(count)])  1.99 us
  transfers between devices with their start and end apart: 9, of which 4 were waited for; matrix products, arithmetic and copies ran while one was open for 0% of the time, Pallas kernels for 30%

profile of v6, /device:TPU:0, one launch (start us, length us, event | category | flops | bytes accessed | tf_op | source)
XLA Modules:
  0.0 40.1 jit_solution(4785073875328916641)
XLA Ops:
  0.6 7.2 %far_gather.1 = (f32[6,4,8,128]{3,2,1,0:T(8,128)S(1)}, bf16[3,256,512]{2,1,0:T(8,128)(2,1)S(1)}, f32[3,512,128]{2,1,0:T(8,128)S(1)}, s32[72,128]{1,0:T(8,128)S(1...) custom-call(s32[1]{0:T(128)} %bitcast.mine_ref, ...), custom_call_target="tpu_custom_call" | custom-call | flops 5000000000 | bytes 100000 | tf_op jit(solution)/shard_map/far_gather/pallas_call | solution.py:374
  7.8 5.7 %collective-permute-start.1 = (f32[96,128]{1,0:T(8,128)S(1)}, f32[96,128]{1,0:T(8,128)S(1)}, u32[]{:S(2)}, u32[]{:S(2)}) collective-permute-start(f32[96,128]{1,0:T(8,128)S(1)} %bitcast.19), channel_id=1, source_target_pairs={{0,28},{4,8},{8,4},{12,16},{16,12},{20,24},{24,20},{28,0},{1,29},{... | collective-permute-start | bytes 147464 | tf_op jit(solution)/shard_map/ppermute | solution.py:370
  13.6 0.0 collective-permute-start
  13.6 2.4 %near_gather.1 = f32[3,4,8,128]{3,2,1,0:T(8,128)S(1)} custom-call(s32[1]{0:T(128)} %bitcast.mine_ref, bf16[3,256,512]{2,1,0:T(8,128)(2,1)S(1)} %get-tuple-element.21.table, s32[72,128]{1,0:T(8,128)S(1)} %get-tuple-element.22.src_ref, f32[72,128]{1,0:T(8,128)S(1)} %get-tuple-element.23.w_ref), custom_call_target="tpu_custom_call" | custom-call | flops 4000000000 | bytes 100000 | tf_op jit(solution)/shard_map/near_gather/pallas_call | solution.py:374
  15.9 0.0 collective-permute-done.1.high_ref
  16.0 1.8 %collective-permute-done.low_ref = f32[120,128]{1,0:T(8,128)S(1)} collective-permute-done((f32[120,128]{1,0:T(8,128)S(1)}, f32[120,128]{1,0:T(8,128)S(1)}, u32[]{:S(2)}, u32[]{:S(2)}) %collective-permute-start) | collective-permute-done | bytes 61472 | tf_op jit(solution)/shard_map/ppermute | solution.py:365
  17.8 0.1 collective-permute-start.2
  17.9 1.2 %collective-permute-done.2.first_ref = f32[120,128]{1,0:T(8,128)S(1)} collective-permute-done((f32[120,128]{1,0:T(8,128)S(1)}, f32[120,128]{1,0:T(8,128)S(1)}, u32[]{:S(2)}, u32[]{:S(2)}) %collective-permute-start.2) | collective-permute-done | bytes 61472 | tf_op jit(solution)/shard_map/ppermute | solution.py:365
  19.1 0.3 collective-permute-start.3
  19.4 2.7 %first_scatter.1.base_ref = f32[512,512]{1,0:T(8,128)S(1)} custom-call(s32[1]{0:T(128)} %bitcast.mine_ref, f32[120,128]{1,0:T(8,128)S(1)} %collective-permute-done.low_ref, f32[96,128]{1,0:T(8,128)S(1)} %bitcast.16, f32[96,128]{1,0:T(8,128)S(1)} %collective-permute-done.1.high_ref, s32[72,128]{1,0:T(8,128)S(1)} %get-tuple-element.24.dst_ref), custom_call_target="tpu_custom_call" | custom-call | flops 4000000000 | bytes 100000 | tf_op jit(solution)/shard_map/first_scatter/pallas_call | solution.py:374
  22.2 1.0 %collective-permute-done.3.second_ref = f32[120,128]{1,0:T(8,128)S(1)} collective-permute-done((f32[120,128]{1,0:T(8,128)S(1)}, f32[120,128]{1,0:T(8,128)S(1)}, u32[]{:S(2)}, u32[]{:S(2)}) %collective-permute-start.3) | collective-permute-done | bytes 61472 | tf_op jit(solution)/shard_map/ppermute | solution.py:370
  23.2 0.6 %collective-permute-start.4 = (f32[24,128]{1,0:T(8,128)S(1)}, f32[24,128]{1,0:T(8,128)S(1)}, u32[]{:S(2)}, u32[]{:S(2)}) collective-permute-start(f32[24,128]{1,0:T(8,128)S(1)} %slice_add_fusion.1), channel_id=1, source_target_pairs={{0,16},{4,20},{8,24},{12,28},{16,0},{20,4},{24,8},{28,12},{1,17},{... | collective-permute-start | bytes 36872 | tf_op jit(solution)/shard_map/ppermute | solution.py:365
  23.7 3.1 %edge_scatter.1 = (f32[3,128,128]{2,1,0:T(8,128)S(1)}, f32[3,64,128]{2,1,0:T(8,128)S(1)}, f32[3,64,128]{2,1,0:T(8,128)S(1)}, f32[3,8,128]{2,1,0:T(8,128)S(1)}, f32[3,8,128]{2,1,0:T(8,128)S(1)}) custom-call(s32[1]{0:T(128)} %bitcast.mine_ref, f32[512,512]{1,0:T(8,128)S(1)} %first_scatter.1.base_ref, f32[120,128]{1,0:T(8,128)S(1)} %collective-permute-done.2.first_ref, ...), custom_call_target="tpu_custom_call" | custom-call | flops 4000000000 | bytes 100000 | tf_op jit(solution)/shard_map/edge_scatter/pallas_call | solution.py:374
  26.8 0.1 collective-permute-start.7
  26.9 1.5 %collective-permute-start.8 = (f32[3,8,128]{2,1,0:T(8,128)S(1)}, f32[3,8,128]{2,1,0:T(8,128)S(1)}, u32[]{:S(2)}, u32[]{:S(2)}) collective-permute-start(f32[3,8,128]{2,1,0:T(8,128)S(1)} %get-tuple-element.33), channel_id=1, source_target_pairs={{0,3},{1,2},{2,1},{3,0},{4,7},{5,6},{6,5},{7,4},{8,11},{9,10},{10,... | collective-permute-start | bytes 36872 | tf_op jit(solution)/shard_map/ppermute | solution.py:370
  28.4 1.3 %collective-permute-start.6 = (f32[192,128]{1,0:T(8,128)S(1)}, f32[192,128]{1,0:T(8,128)S(1)}, u32[]{:S(2)}, u32[]{:S(2)}) collective-permute-start(f32[192,128]{1,0:T(8,128)S(1)} %bitcast.17), channel_id=1, source_target_pairs={{0,4},{4,0},{8,12},{12,8},{16,20},{20,16},{24,28},{28,24},{1,5},{5... | collective-permute-start | bytes 294920 | tf_op jit(solution)/shard_map/ppermute | solution.py:365
  29.7 0.0 collective-permute-done.4
  29.7 1.4 %collective-permute-start.5 = (f32[216,128]{1,0:T(8,128)S(1)}, f32[216,128]{1,0:T(8,128)S(1)}, u32[]{:S(2)}, u32[]{:S(2)}) collective-permute-start(f32[216,128]{1,0:T(8,128)S(1)} %pad_maximum_fusion), channel_id=1, source_target_pairs={{0,28},{4,8},{8,4},{12,16},{16,12},{20,24},{24,20},{28,0},{1,29},{... | collective-permute-start | bytes 331784 | tf_op jit(solution)/shard_map/ppermute | solution.py:370
  31.1 3.7 %inner_scatter.1.inner_ref = f32[3,384,128]{2,1,0:T(8,128)S(1)} custom-call(s32[1]{0:T(128)} %bitcast.mine_ref, f32[512,512]{1,0:T(8,128)S(1)} %first_scatter.1.base_ref, f32[120,128]{1,0:T(8,128)S(1)} %collective-permute-done.2.first_ref, f32[120,128]{1,0:T(8,128)S(1)} %collective-permute-done.3.second_ref, s32[72,128]{1,0:T(8,128)S(1)} %get-tuple-element.24.dst_ref, ...), custom_call_target="tpu_custom_call" | custom-call | flops 6000000000 | bytes 100000 | tf_op jit(solution)/shard_map/inner_scatter/pallas_call | solution.py:374
  34.9 0.0 copy-start
  34.9 2.7 %collective-permute-done.5.xb_ref = f32[216,128]{1,0:T(8,128)S(1)} collective-permute-done((f32[216,128]{1,0:T(8,128)S(1)}, f32[216,128]{1,0:T(8,128)S(1)}, u32[]{:S(2)}, u32[]{:S(2)}) %collective-permute-start.5) | collective-permute-done | bytes 110624 | tf_op jit(solution)/shard_map/ppermute | solution.py:370
  37.6 0.0 collective-permute-done.7.ya_ref
  37.6 0.0 collective-permute-done.8.yb_ref
  37.6 0.0 collective-permute-done.6.xa_ref
  37.6 0.0 copy-done
  37.6 2.5 %stencil.1 = (f32[3,8,64,128]{3,2,1,0:T(8,128)}, f32[3,512,128]{2,1,0:T(8,128)}) custom-call(s32[1]{0:T(128)} %bitcast.mine_ref, f32[3,128,128]{2,1,0:T(8,128)S(1)} %get-tuple-element.26.edge_ref, f32[3,384,128]{2,1,0:T(8,128)S(1)} %inner_scatter.1.inner_ref, s32[20,192]{1,0:T(8,128)S(1)} %get-tuple-element.27.tile_ref, ...), custom_call_target="tpu_custom_call" | custom-call | flops 1000000000 | bytes 100000 | tf_op jit(solution)/shard_map/stencil/pallas_call | solution.py:374
  (13 shorter events, 0.1 us)
Async XLA Ops:
  7.8 8.1 %collective-permute-start.1 = (f32[96,128]{1,0:T(8,128)S(1)}, f32[96,128]{1,0:T(8,128)S(1)}, u32[]{:S(2)}, u32[]{:S(2)}) collective-permute-start(f32[96,128]{1,0:T(8,128)S(1)} %bitcast.19), channel_id=1, source_target_pairs={{0,28},{4,8},{8,4},{12,16},{16,12},{20,24},{24,20},{28,0},{1,29},{... | collective-permute-start | bytes 147464 | tf_op jit(solution)/shard_map/ppermute | solution.py:370
  13.6 4.2 %collective-permute-start = (f32[120,128]{1,0:T(8,128)S(1)}, f32[120,128]{1,0:T(8,128)S(1)}, u32[]{:S(2)}, u32[]{:S(2)}) collective-permute-start(f32[120,128]{1,0:T(8,128)S(1)} %pad_maximum_fusion.1), channel_id=1, source_target_pairs={{0,4},{4,0},{8,12},{12,8},{16,20},{20,16},{24,28},{28,24},{1,5},{5... | collective-permute-start | bytes 184328 | tf_op jit(solution)/shard_map/ppermute | solution.py:365
  17.8 1.3 %collective-permute-start.2 = (f32[120,128]{1,0:T(8,128)S(1)}, f32[120,128]{1,0:T(8,128)S(1)}, u32[]{:S(2)}, u32[]{:S(2)}) collective-permute-start(f32[120,128]{1,0:T(8,128)S(1)} %pad_maximum_fusion.2), channel_id=1, source_target_pairs={{0,1},{1,0},{2,3},{3,2},{4,5},{5,4},{6,7},{7,6},{8,9},{9,8},{10,11... | collective-permute-start | bytes 184328 | tf_op jit(solution)/shard_map/ppermute | solution.py:365
  19.1 4.0 %collective-permute-start.3 = (f32[120,128]{1,0:T(8,128)S(1)}, f32[120,128]{1,0:T(8,128)S(1)}, u32[]{:S(2)}, u32[]{:S(2)}) collective-permute-start(f32[120,128]{1,0:T(8,128)S(1)} %pad_maximum_fusion.3), channel_id=1, source_target_pairs={{0,3},{1,2},{2,1},{3,0},{4,7},{5,6},{6,5},{7,4},{8,11},{9,10},{10,... | collective-permute-start | bytes 184328 | tf_op jit(solution)/shard_map/ppermute | solution.py:370
  23.2 6.5 %collective-permute-start.4 = (f32[24,128]{1,0:T(8,128)S(1)}, f32[24,128]{1,0:T(8,128)S(1)}, u32[]{:S(2)}, u32[]{:S(2)}) collective-permute-start(f32[24,128]{1,0:T(8,128)S(1)} %slice_add_fusion.1), channel_id=1, source_target_pairs={{0,16},{4,20},{8,24},{12,28},{16,0},{20,4},{24,8},{28,12},{1,17},{... | collective-permute-start | bytes 36872 | tf_op jit(solution)/shard_map/ppermute | solution.py:365
  26.8 10.8 %collective-permute-start.7 = (f32[3,8,128]{2,1,0:T(8,128)S(1)}, f32[3,8,128]{2,1,0:T(8,128)S(1)}, u32[]{:S(2)}, u32[]{:S(2)}) collective-permute-start(f32[3,8,128]{2,1,0:T(8,128)S(1)} %get-tuple-element.32), channel_id=1, source_target_pairs={{0,1},{1,0},{2,3},{3,2},{4,5},{5,4},{6,7},{7,6},{8,9},{9,8},{10,11... | collective-permute-start | bytes 36872 | tf_op jit(solution)/shard_map/ppermute | solution.py:365
  26.9 10.7 %collective-permute-start.8 = (f32[3,8,128]{2,1,0:T(8,128)S(1)}, f32[3,8,128]{2,1,0:T(8,128)S(1)}, u32[]{:S(2)}, u32[]{:S(2)}) collective-permute-start(f32[3,8,128]{2,1,0:T(8,128)S(1)} %get-tuple-element.33), channel_id=1, source_target_pairs={{0,3},{1,2},{2,1},{3,0},{4,7},{5,6},{6,5},{7,4},{8,11},{9,10},{10,... | collective-permute-start | bytes 36872 | tf_op jit(solution)/shard_map/ppermute | solution.py:370
  28.4 9.2 %collective-permute-start.6 = (f32[192,128]{1,0:T(8,128)S(1)}, f32[192,128]{1,0:T(8,128)S(1)}, u32[]{:S(2)}, u32[]{:S(2)}) collective-permute-start(f32[192,128]{1,0:T(8,128)S(1)} %bitcast.17), channel_id=1, source_target_pairs={{0,4},{4,0},{8,12},{12,8},{16,20},{20,16},{24,28},{28,24},{1,5},{5... | collective-permute-start | bytes 294920 | tf_op jit(solution)/shard_map/ppermute | solution.py:365
  29.7 7.9 %collective-permute-start.5 = (f32[216,128]{1,0:T(8,128)S(1)}, f32[216,128]{1,0:T(8,128)S(1)}, u32[]{:S(2)}, u32[]{:S(2)}) collective-permute-start(f32[216,128]{1,0:T(8,128)S(1)} %pad_maximum_fusion), channel_id=1, source_target_pairs={{0,28},{4,8},{8,4},{12,16},{16,12},{20,24},{24,20},{28,0},{1,29},{... | collective-permute-start | bytes 331784 | tf_op jit(solution)/shard_map/ppermute | solution.py:370
  34.9 2.7 %copy-start = (f32[20,192]{1,0:T(8,128)S(1)}, f32[20,192]{1,0:T(8,128)}, u32[]{:S(2)}) copy-start(f32[20,192]{1,0:T(8,128)} %coef_ref.1) | copy-start | bytes 46084

commit v7 on v6

--- a/solution.py
+++ b/solution.py
@@ -100,14 +100,14 @@
 
 def make_far_gather(count_y, large, small):
     def kernel(
-        mine_ref, cnt_hbm, vel_hbm, src_hbm, w_hbm, dst_hbm, tile_hbm, cell_hbm,
-        out_ref, table, vel_ref, src_ref, w_ref, dst_ref, tile_ref, cell_ref, pts_ref, rot_ref,
+        mine_ref, cnt_hbm, vel_hbm, src_hbm, w_hbm, dst_hbm, tile_hbm, cell_hbm, coef_hbm,
+        out_ref, table, vel_ref, src_ref, w_ref, dst_ref, tile_ref, cell_ref, coef_ref, pts_ref, rot_ref,
         sem, cnt_ref, listed, direction, tlist,
     ):
         half = vel_ref.shape[1] // 2
         pairs = [(cnt_hbm, cnt_ref), (src_hbm, src_ref), (w_hbm, w_ref)]
         pairs += [(vel_hbm.at[c], vel_ref.at[c]) for c in range(3)]
-        pairs += [(tile_hbm, tile_ref), (cell_hbm, cell_ref), (dst_hbm, dst_ref)]
+        pairs += [(tile_hbm, tile_ref), (cell_hbm, cell_ref), (coef_hbm, coef_ref), (dst_hbm, dst_ref)]
         copies = [pltpu.make_async_copy(a, b, sem.at[k]) for k, (a, b) in enumerate(pairs)]
         for copy in copies:
             copy.start()
@@ -396,16 +396,16 @@
 
     whole = ((72, 128), jnp.int32, VMEM)
     ints_t = (blade_tile.shape, jnp.int32, VMEM)
-    given = (counts, vel, src, weight, dst, blade_tile, blade_cell)
-    far, table, vel, src, weight, dst, tile, cell, pts, rotor = call(
+    given = (counts, vel, src, weight, dst, blade_tile, blade_cell, blade_coef)
+    far, table, vel, src, weight, dst, tile, cell, coef, pts, rotor = call(
         make_far_gather(count_y, 12, 4),
         "far_gather",
         [((6, 4, 8, 128), F32, VMEM), ((3, 256, 512), BF16, VMEM), ((3, 512, 128), F32, VMEM), whole]
-        + [((72, 128), F32, VMEM), whole, ints_t, ints_t]
+        + [((72, 128), F32, VMEM), whole, ints_t, ints_t, (blade_tile.shape, F32, VMEM)]
         + [((3, turbines, points), F32, VMEM), ((rows_t, 128), F32, VMEM)],
-        [SMEM] + [HBM] * 7,
+        [SMEM] + [HBM] * 8,
         (mine,) + tuple(pltpu.with_memory_space_constraint(v, pltpu.HBM) for v in given),
-        [pltpu.SemaphoreType.DMA((9,)), pltpu.SMEM((1, 1, 9), jnp.int32), ints(72), ints(8), ints(32)],
+        [pltpu.SemaphoreType.DMA((10,)), pltpu.SMEM((1, 1, 9), jnp.int32), ints(72), ints(8), ints(32)],
         flops=5 * 10**9,
     )
     low = swap(jnp.concatenate([far[0:3].reshape(96, 128), rotor], axis=0), "gx", 1)
@@ -454,6 +454,7 @@
         [pltpu.VMEM((144, 512), F32), lists, ints(72), ints(8)],
         flops=4 * 10**9,
     )
+    rotor, xa, ya, yb = lax.optimization_barrier((rotor, xa, ya, yb))
     xb = swap_next(jnp.concatenate([xb.reshape(192, 128), rotor], axis=0), "gx")
     xa = swap(xa.reshape(192, 128), "gx", 1)
     ya = swap(ya, "gy", 1)
@@ -473,7 +474,7 @@
         "stencil",
         [((3, 8, 64, 128), F32, HBM), ((3, 512, 128), F32, HBM)],
         [SMEM] + [VMEM] * 11,
-        (mine, edge, inner, tile, cell, blade_coef, pts, rotor, xa, xb, ya, yb),
+        (mine, edge, inner, tile, cell, coef, pts, rotor, xa, xb, ya, yb),
         [pltpu.VMEM((3, 8, 64, 128), F32), pltpu.VMEM((3, 512, 128), F32), pltpu.SemaphoreType.DMA((9,)), ints(32)],
     )
     return updated, forcing.reshape(velocity.shape)

time: 40.7 us -> 43.3 us (1.064)
  waiting for transfers between devices: 6.7 us -> 9.42 us
  starting transfers between devices: 11 us -> 9.81 us
  Pallas kernels: 21.5 us -> 22.5 us
    ppermute x5, waiting for transfers between devices: 3.05 us -> 6.63 us  [swap(): return lax.ppermute(value, axis, [(i, i ^ step) for i in range(count)])]
    ppermute x5, starting transfers between devices: 1.99 us -> 0.35 us  [swap(): return lax.ppermute(value, axis, [(i, i ^ step) for i in range(count)])]
    pallas_call x6, Pallas kernels: 21.5 us -> 22.5 us  [call(): pl.pallas_call(kernel, out_shape=tuple((jax.ShapeDtypeStruct(shape, dtype...]
    ppermute x4, waiting for transfers between devices: 3.65 us -> 2.79 us  [swap_next(): lax.ppermute(value, axis, [(i, (i - 1 if i % 2 == 0 else i + 1) % count)...]
    ppermute x4, starting transfers between devices: 8.99 us -> 9.46 us  [swap_next(): lax.ppermute(value, axis, [(i, (i - 1 if i % 2 == 0 else i + 1) % count)...]
  transfers between devices with their start and end apart: 9 -> 9, of which waited for: 4 -> 8; matrix products, arithmetic and copies ran while one was open for 0% -> 0% of each run, Pallas kernels for 30% -> 27%
where the time goes in v7:
time: 43.3 us; the launch traced here: 42.6 us
  Pallas kernels  22.5 us (52%)
  starting transfers between devices  9.81 us (23%)
  waiting for transfers between devices  9.42 us (22%)
  between operations  0.74 us (2%)
    pallas_call x6, Pallas kernels, call(): pl.pallas_call(kernel, out_shape=tuple((jax.ShapeDtypeStruct(shape, dtype...  22.5 us
    ppermute x4, starting transfers between devices, swap_next(): lax.ppermute(value, axis, [(i, (i - 1 if i % 2 == 0 else i + 1) % count)...  9.46 us
    ppermute x5, waiting for transfers between devices, swap(): return lax.ppermute(value, axis, [(i, i ^ step) for i in range(count)])  6.63 us
    ppermute x4, waiting for transfers between devices, swap_next(): lax.ppermute(value, axis, [(i, (i - 1 if i % 2 == 0 else i + 1) % count)...  2.79 us
  transfers between devices with their start and end apart: 9, of which 8 were waited for; matrix products, arithmetic and copies ran while one was open for 0% of the time, Pallas kernels for 27%

profile of v7, /device:TPU:0, one launch (start us, length us, event | category | flops | bytes accessed | tf_op | source)
XLA Modules:
  0.0 42.6 jit_solution(6279133404139760474)
XLA Ops:
  0.6 7.9 %far_gather.1 = (f32[6,4,8,128]{3,2,1,0:T(8,128)S(1)}, bf16[3,256,512]{2,1,0:T(8,128)(2,1)S(1)}, f32[3,512,128]{2,1,0:T(8,128)S(1)}, s32[72,128]{1,0:T(8,128)S(1...) custom-call(s32[1]{0:T(128)} %bitcast.mine_ref, ...), custom_call_target="tpu_custom_call" | custom-call | flops 5000000000 | bytes 100000 | tf_op jit(solution)/shard_map/far_gather/pallas_call | solution.py:374
  8.6 3.4 %collective-permute-start.1 = (f32[96,128]{1,0:T(8,128)S(1)}, f32[96,128]{1,0:T(8,128)S(1)}, u32[]{:S(2)}, u32[]{:S(2)}) collective-permute-start(f32[96,128]{1,0:T(8,128)S(1)} %bitcast.19), channel_id=1, source_target_pairs={{0,28},{4,8},{8,4},{12,16},{16,12},{20,24},{24,20},{28,0},{1,29},{... | collective-permute-start | bytes 147464 | tf_op jit(solution)/shard_map/ppermute | solution.py:370
  11.9 0.1 collective-permute-start
  12.1 3.0 %near_gather.1 = f32[3,4,8,128]{3,2,1,0:T(8,128)S(1)} custom-call(s32[1]{0:T(128)} %bitcast.mine_ref, bf16[3,256,512]{2,1,0:T(8,128)(2,1)S(1)} %get-tuple-element.26.table, s32[72,128]{1,0:T(8,128)S(1)} %get-tuple-element.27.src_ref, f32[72,128]{1,0:T(8,128)S(1)} %get-tuple-element.28.w_ref), custom_call_target="tpu_custom_call" | custom-call | flops 4000000000 | bytes 100000 | tf_op jit(solution)/shard_map/near_gather/pallas_call | solution.py:374
  15.1 0.3 collective-permute-done.1.high_ref
  15.4 0.8 %collective-permute-done.low_ref = f32[120,128]{1,0:T(8,128)S(1)} collective-permute-done((f32[120,128]{1,0:T(8,128)S(1)}, f32[120,128]{1,0:T(8,128)S(1)}, u32[]{:S(2)}, u32[]{:S(2)}) %collective-permute-start) | collective-permute-done | bytes 61472 | tf_op jit(solution)/shard_map/ppermute | solution.py:365
  16.2 0.1 collective-permute-start.2
  16.3 1.2 %collective-permute-done.2.first_ref = f32[120,128]{1,0:T(8,128)S(1)} collective-permute-done((f32[120,128]{1,0:T(8,128)S(1)}, f32[120,128]{1,0:T(8,128)S(1)}, u32[]{:S(2)}, u32[]{:S(2)}) %collective-permute-start.2) | collective-permute-done | bytes 61472 | tf_op jit(solution)/shard_map/ppermute | solution.py:365
  17.5 2.2 %collective-permute-start.3 = (f32[120,128]{1,0:T(8,128)S(1)}, f32[120,128]{1,0:T(8,128)S(1)}, u32[]{:S(2)}, u32[]{:S(2)}) collective-permute-start(f32[120,128]{1,0:T(8,128)S(1)} %pad_maximum_fusion.3), channel_id=1, source_target_pairs={{0,3},{1,2},{2,1},{3,0},{4,7},{5,6},{6,5},{7,4},{8,11},{9,10},{10,... | collective-permute-start | bytes 184328 | tf_op jit(solution)/shard_map/ppermute | solution.py:370
  19.7 2.7 %first_scatter.1.base_ref = f32[512,512]{1,0:T(8,128)S(1)} custom-call(s32[1]{0:T(128)} %bitcast.mine_ref, f32[120,128]{1,0:T(8,128)S(1)} %collective-permute-done.low_ref, f32[96,128]{1,0:T(8,128)S(1)} %bitcast.16, f32[96,128]{1,0:T(8,128)S(1)} %collective-permute-done.1.high_ref, s32[72,128]{1,0:T(8,128)S(1)} %get-tuple-element.29.dst_ref), custom_call_target="tpu_custom_call" | custom-call | flops 4000000000 | bytes 100000 | tf_op jit(solution)/shard_map/first_scatter/pallas_call | solution.py:374
  22.5 0.0 collective-permute-done.3.second_ref
  22.5 0.1 collective-permute-start.4
  22.6 2.6 %edge_scatter.1 = (f32[3,128,128]{2,1,0:T(8,128)S(1)}, f32[3,64,128]{2,1,0:T(8,128)S(1)}, f32[3,64,128]{2,1,0:T(8,128)S(1)}, f32[3,8,128]{2,1,0:T(8,128)S(1)}, f32[3,8,128]{2,1,0:T(8,128)S(1)}) custom-call(s32[1]{0:T(128)} %bitcast.mine_ref, f32[512,512]{1,0:T(8,128)S(1)} %first_scatter.1.base_ref, f32[120,128]{1,0:T(8,128)S(1)} %collective-permute-done.2.first_ref, ...), custom_call_target="tpu_custom_call" | custom-call | flops 4000000000 | bytes 100000 | tf_op jit(solution)/shard_map/edge_scatter/pallas_call | solution.py:374
  25.2 2.0 %collective-permute-done.4 = f32[24,128]{1,0:T(8,128)S(1)} collective-permute-done((f32[24,128]{1,0:T(8,128)S(1)}, f32[24,128]{1,0:T(8,128)S(1)}, u32[]{:S(2)}, u32[]{:S(2)}) %collective-permute-start.4) | collective-permute-done | bytes 12320 | tf_op jit(solution)/shard_map/ppermute | solution.py:365
  27.2 3.4 %collective-permute-start.5 = (f32[216,128]{1,0:T(8,128)S(1)}, f32[216,128]{1,0:T(8,128)S(1)}, u32[]{:S(2)}, u32[]{:S(2)}) collective-permute-start(f32[216,128]{1,0:T(8,128)S(1)} %pad_maximum_fusion), channel_id=1, source_target_pairs={{0,28},{4,8},{8,4},{12,16},{16,12},{20,24},{24,20},{28,0},{1,29},{... | collective-permute-start | bytes 331784 | tf_op jit(solution)/shard_map/ppermute | solution.py:370
  30.6 3.1 %inner_scatter.1.inner_ref = f32[3,384,128]{2,1,0:T(8,128)S(1)} custom-call(s32[1]{0:T(128)} %bitcast.mine_ref, f32[512,512]{1,0:T(8,128)S(1)} %first_scatter.1.base_ref, f32[120,128]{1,0:T(8,128)S(1)} %collective-permute-done.2.first_ref, f32[120,128]{1,0:T(8,128)S(1)} %collective-permute-done.3.second_ref, s32[72,128]{1,0:T(8,128)S(1)} %get-tuple-element.29.dst_ref, ...), custom_call_target="tpu_custom_call" | custom-call | flops 6000000000 | bytes 100000 | tf_op jit(solution)/shard_map/inner_scatter/pallas_call | solution.py:374
  33.7 0.1 collective-permute-start.7
  33.8 0.5 %collective-permute-start.8 = (f32[3,8,128]{2,1,0:T(8,128)S(1)}, f32[3,8,128]{2,1,0:T(8,128)S(1)}, u32[]{:S(2)}, u32[]{:S(2)}) collective-permute-start(f32[3,8,128]{2,1,0:T(8,128)S(1)} %get-tuple-element.43), channel_id=1, source_target_pairs={{0,3},{1,2},{2,1},{3,0},{4,7},{5,6},{6,5},{7,4},{8,11},{9,10},{10,... | collective-permute-start | bytes 36872 | tf_op jit(solution)/shard_map/ppermute | solution.py:370
  34.3 0.0 collective-permute-start.6
  34.3 0.5 %collective-permute-done.5.xb_ref = f32[216,128]{1,0:T(8,128)S(1)} collective-permute-done((f32[216,128]{1,0:T(8,128)S(1)}, f32[216,128]{1,0:T(8,128)S(1)}, u32[]{:S(2)}, u32[]{:S(2)}) %collective-permute-start.5) | collective-permute-done | bytes 110624 | tf_op jit(solution)/shard_map/ppermute | solution.py:370
  34.7 0.3 collective-permute-done.7.ya_ref
  35.0 2.0 %collective-permute-done.8.yb_ref = f32[3,8,128]{2,1,0:T(8,128)S(1)} collective-permute-done((f32[3,8,128]{2,1,0:T(8,128)S(1)}, f32[3,8,128]{2,1,0:T(8,128)S(1)}, u32[]{:S(2)}, u32[]{:S(2)}) %collective-permute-start.8) | collective-permute-done | bytes 12320 | tf_op jit(solution)/shard_map/ppermute | solution.py:370
  37.0 2.4 %collective-permute-done.6.xa_ref = f32[192,128]{1,0:T(8,128)S(1)} collective-permute-done((f32[192,128]{1,0:T(8,128)S(1)}, f32[192,128]{1,0:T(8,128)S(1)}, u32[]{:S(2)}, u32[]{:S(2)}) %collective-permute-start.6) | collective-permute-done | bytes 98336 | tf_op jit(solution)/shard_map/ppermute | solution.py:365
  39.4 3.2 %stencil.1 = (f32[3,8,64,128]{3,2,1,0:T(8,128)}, f32[3,512,128]{2,1,0:T(8,128)}) custom-call(s32[1]{0:T(128)} %bitcast.mine_ref, f32[3,128,128]{2,1,0:T(8,128)S(1)} %get-tuple-element.31.edge_ref, f32[3,384,128]{2,1,0:T(8,128)S(1)} %inner_scatter.1.inner_ref, s32[20,192]{1,0:T(8,128)S(1)} %get-tuple-element.32.tile_ref, ...), custom_call_target="tpu_custom_call" | custom-call | flops 1000000000 | bytes 100000 | tf_op jit(solution)/shard_map/stencil/pallas_call | solution.py:374
  (13 shorter events, 0.1 us)
Async XLA Ops:
  8.6 6.9 %collective-permute-start.1 = (f32[96,128]{1,0:T(8,128)S(1)}, f32[96,128]{1,0:T(8,128)S(1)}, u32[]{:S(2)}, u32[]{:S(2)}) collective-permute-start(f32[96,128]{1,0:T(8,128)S(1)} %bitcast.19), channel_id=1, source_target_pairs={{0,28},{4,8},{8,4},{12,16},{16,12},{20,24},{24,20},{28,0},{1,29},{... | collective-permute-start | bytes 147464 | tf_op jit(solution)/shard_map/ppermute | solution.py:370
  11.9 4.2 %collective-permute-start = (f32[120,128]{1,0:T(8,128)S(1)}, f32[120,128]{1,0:T(8,128)S(1)}, u32[]{:S(2)}, u32[]{:S(2)}) collective-permute-start(f32[120,128]{1,0:T(8,128)S(1)} %pad_maximum_fusion.1), channel_id=1, source_target_pairs={{0,4},{4,0},{8,12},{12,8},{16,20},{20,16},{24,28},{28,24},{1,5},{5... | collective-permute-start | bytes 184328 | tf_op jit(solution)/shard_map/ppermute | solution.py:365
  16.2 1.3 %collective-permute-start.2 = (f32[120,128]{1,0:T(8,128)S(1)}, f32[120,128]{1,0:T(8,128)S(1)}, u32[]{:S(2)}, u32[]{:S(2)}) collective-permute-start(f32[120,128]{1,0:T(8,128)S(1)} %pad_maximum_fusion.2), channel_id=1, source_target_pairs={{0,1},{1,0},{2,3},{3,2},{4,5},{5,4},{6,7},{7,6},{8,9},{9,8},{10,11... | collective-permute-start | bytes 184328 | tf_op jit(solution)/shard_map/ppermute | solution.py:365
  17.5 5.0 %collective-permute-start.3 = (f32[120,128]{1,0:T(8,128)S(1)}, f32[120,128]{1,0:T(8,128)S(1)}, u32[]{:S(2)}, u32[]{:S(2)}) collective-permute-start(f32[120,128]{1,0:T(8,128)S(1)} %pad_maximum_fusion.3), channel_id=1, source_target_pairs={{0,3},{1,2},{2,1},{3,0},{4,7},{5,6},{6,5},{7,4},{8,11},{9,10},{10,... | collective-permute-start | bytes 184328 | tf_op jit(solution)/shard_map/ppermute | solution.py:370
  22.5 4.7 %collective-permute-start.4 = (f32[24,128]{1,0:T(8,128)S(1)}, f32[24,128]{1,0:T(8,128)S(1)}, u32[]{:S(2)}, u32[]{:S(2)}) collective-permute-start(f32[24,128]{1,0:T(8,128)S(1)} %slice_add_fusion.1), channel_id=1, source_target_pairs={{0,16},{4,20},{8,24},{12,28},{16,0},{20,4},{24,8},{28,12},{1,17},{... | collective-permute-start | bytes 36872 | tf_op jit(solution)/shard_map/ppermute | solution.py:365
  27.2 7.5 %collective-permute-start.5 = (f32[216,128]{1,0:T(8,128)S(1)}, f32[216,128]{1,0:T(8,128)S(1)}, u32[]{:S(2)}, u32[]{:S(2)}) collective-permute-start(f32[216,128]{1,0:T(8,128)S(1)} %pad_maximum_fusion), channel_id=1, source_target_pairs={{0,28},{4,8},{8,4},{12,16},{16,12},{20,24},{24,20},{28,0},{1,29},{... | collective-permute-start | bytes 331784 | tf_op jit(solution)/shard_map/ppermute | solution.py:370
  33.7 1.2 %collective-permute-start.7 = (f32[3,8,128]{2,1,0:T(8,128)S(1)}, f32[3,8,128]{2,1,0:T(8,128)S(1)}, u32[]{:S(2)}, u32[]{:S(2)}) collective-permute-start(f32[3,8,128]{2,1,0:T(8,128)S(1)} %get-tuple-element.42), channel_id=1, source_target_pairs={{0,1},{1,0},{2,3},{3,2},{4,5},{5,4},{6,7},{7,6},{8,9},{9,8},{10,11... | collective-permute-start | bytes 36872 | tf_op jit(solution)/shard_map/ppermute | solution.py:365
  33.8 3.2 %collective-permute-start.8 = (f32[3,8,128]{2,1,0:T(8,128)S(1)}, f32[3,8,128]{2,1,0:T(8,128)S(1)}, u32[]{:S(2)}, u32[]{:S(2)}) collective-permute-start(f32[3,8,128]{2,1,0:T(8,128)S(1)} %get-tuple-element.43), channel_id=1, source_target_pairs={{0,3},{1,2},{2,1},{3,0},{4,7},{5,6},{6,5},{7,4},{8,11},{9,10},{10,... | collective-permute-start | bytes 36872 | tf_op jit(solution)/shard_map/ppermute | solution.py:370
  34.3 5.1 %collective-permute-start.6 = (f32[192,128]{1,0:T(8,128)S(1)}, f32[192,128]{1,0:T(8,128)S(1)}, u32[]{:S(2)}, u32[]{:S(2)}) collective-permute-start(f32[192,128]{1,0:T(8,128)S(1)} %bitcast.17), channel_id=1, source_target_pairs={{0,4},{4,0},{8,12},{12,8},{16,20},{20,16},{24,28},{28,24},{1,5},{5... | collective-permute-start | bytes 294920 | tf_op jit(solution)/shard_map/ppermute | solution.py:365

commit v8 on v7

--- a/solution.py
+++ b/solution.py
@@ -178,8 +178,9 @@
 
 
 def make_near_gather(count_y, large, small):
-    def kernel(mine_ref, table, src_ref, w_ref, out_ref, listed, direction):
+    def kernel(mine_ref, table, src_ref, w_ref, dst_ref, out_ref, acc, listed, direction):
         out_ref[...] = jnp.zeros_like(out_ref)
+        acc[...] = jnp.zeros_like(acc)
         _, side_y = sides(mine_ref, count_y)
         used = [used_slots(w_ref[d * 8 : d * 8 + 8, :]) for d in (3, 4, 5)]
         last = jnp.where(side_y > 0, used[0], used[2])
@@ -188,6 +189,8 @@
             direction[t] = 3 + side_y * (1 - t) + 1
         total = list_blocks(lists, listed)
         gather_lists(table, total, large, small, listed, direction, src_ref, w_ref, out_ref)
+        direction[0] = 4
+        scatter_lists(out_ref.at[1:2], 1, direction, dst_ref, listed, acc, 512, lambda row: row, 8, 4)
 
     return kernel
 
@@ -217,27 +220,27 @@
 
 
 def make_first_scatter(count_y):
-    def kernel(mine_ref, low_ref, own_ref, high_ref, dst_ref, acc, val, listed, direction):
-        side_x, _ = sides(mine_ref, count_y)
-        for q, ref in enumerate((low_ref, own_ref, high_ref)):
+    def kernel(mine_ref, base_ref, low_ref, high_ref, first_ref, dst_ref, acc, edge, val, later, listed, direction):
+        side_x, side_y = sides(mine_ref, count_y)
+        for q, ref in enumerate((low_ref, high_ref)):
             for c in range(4):
                 val[q, c] = ref[32 + c * 8 : 40 + c * 8, :]
-            direction[q] = 3 * (side_x * (q - 1) + 1) + 1
-        acc[...] = jnp.zeros_like(acc)
-        scatter_lists(val, 3, direction, dst_ref, listed, acc, 512, lambda row: row, 12, 4)
-
-    return kernel
-
-
-def load_later_lists(mine_ref, count_y, first_ref, second_ref, val, direction):
-    side_x, side_y = sides(mine_ref, count_y)
-    for t, ref in enumerate((first_ref, second_ref)):
-        for s in range(3):
-            q = 3 * t + s
-            for c in range(4):
-                at = (s * 4 + c) * 8
-                val[q, c] = ref[at : at + 8, :]
-            direction[q] = 3 * (side_x * (s - 1) + 1) + side_y * (2 * t - 1) + 1
+            direction[q] = 3 * (side_x * (2 * q - 1) + 1) + 1
+        acc[...] = base_ref[...]
+        scatter_lists(val, 2, direction, dst_ref, listed, acc, 512, lambda row: row, 12, 4)
+        edge[...] = edge_rows(acc, None, slice(None))
+        load_later_lists(side_x, -side_y, first_ref, 0, later, direction)
+        scatter_lists(later, 3, direction, dst_ref, listed, edge, 144, edge_place, 12, 4)
+
+    return kernel
+
+
+def load_later_lists(side_x, from_y, ref, start, val, direction):
+    for s in range(3):
+        for c in range(4):
+            at = (s * 4 + c) * 8
+            val[start + s, c] = ref[at : at + 8, :]
+        direction[start + s] = 3 * (side_x * (s - 1) + 1) + from_y + 1
 
 
 def corrected(acc, vel, c):
@@ -260,13 +263,13 @@
 
 def make_edge_scatter(count_y):
     def kernel(
-        mine_ref, base_ref, first_ref, second_ref, dst_ref, vel_ref,
+        mine_ref, base_ref, second_ref, dst_ref, vel_ref,
         cor_ref, xa_ref, xb_ref, ya_ref, yb_ref, acc, val, listed, direction,
     ):
-        load_later_lists(mine_ref, count_y, first_ref, second_ref, val, direction)
-        acc[...] = edge_rows(base_ref, None, slice(None))
-        scatter_lists(val, 6, direction, dst_ref, listed, acc, 144, edge_place, 12, 4)
         side_x, side_y = sides(mine_ref, count_y)
+        load_later_lists(side_x, side_y, second_ref, 0, val, direction)
+        acc[...] = base_ref[...]
+        scatter_lists(val, 3, direction, dst_ref, listed, acc, 144, edge_place, 12, 4)
         for c in range(3):
             cor = corrected(acc, edge_rows(vel_ref, c, slice(None)), c)
             cor_ref[c] = cor[0:128]
@@ -282,7 +285,9 @@
 
 def make_inner_scatter(count_y):
     def kernel(mine_ref, base_ref, first_ref, second_ref, dst_ref, vel_ref, cor_ref, acc, val, listed, direction):
-        load_later_lists(mine_ref, count_y, first_ref, second_ref, val, direction)
+        side_x, side_y = sides(mine_ref, count_y)
+        load_later_lists(side_x, -side_y, first_ref, 0, val, direction)
+        load_later_lists(side_x, side_y, second_ref, 3, val, direction)
         acc[...] = base_ref[64:448, :]
         scatter_lists(val, 6, direction, dst_ref, listed, acc, 384, lambda row: row - 64, 12, 4)
         for c in range(3):
@@ -336,21 +341,20 @@
         copies = []
         for x in range(8):
             now = [slab(c, x) for c in range(3)]
+            up = [0.03 - 0.1 * v for v in now]
+            down = [0.03 + 0.1 * v for v in now]
+            up[2] = jnp.where(lane == 127, 0.0, up[2])
+            down[2] = jnp.where(lane == 0, 0.0, down[2])
             for c in range(3):
                 u = now[c]
                 west, east = slab(c, x - 1), slab(c, x + 1)
                 ya, yb = ya_ref[c, x : x + 1, :], yb_ref[c, x : x + 1, :]
                 south = jnp.concatenate([jnp.where(side_y > 0, yb, ya), u[:-1]], axis=0)
                 north = jnp.concatenate([u[1:], jnp.where(side_y > 0, ya, yb)], axis=0)
-                upper = jnp.where(lane == 127, 0.0, pltpu.roll(u, 127, 1))
-                lower = jnp.where(lane == 0, 0.0, pltpu.roll(u, 1, 1))
-                laplace = east + west + north + south + upper + lower - 6.0 * u
-                advect = (
-                    now[0] * (east - west) * 0.5
-                    + now[1] * (north - south) * 0.5
-                    + now[2] * (upper - lower) * 0.5
-                )
-                out_ref[c, x] = u + 0.2 * (0.15 * laplace - advect + frc_ref[c, x * 64 : x * 64 + 64, :])
+                upper, lower = pltpu.roll(u, 127, 1), pltpu.roll(u, 1, 1)
+                moved = (up[0] * east + down[0] * west) + (up[1] * north + down[1] * south)
+                moved = moved + (up[2] * upper + down[2] * lower)
+                out_ref[c, x] = 0.82 * u + (moved + 0.2 * frc_ref[c, x * 64 : x * 64 + 64, :])
             copies.append(pltpu.make_async_copy(out_ref.at[:, x], out_hbm.at[:, x], sem.at[x]))
             copies[-1].start()
         for copy in copies:
@@ -410,12 +414,12 @@
     )
     low = swap(jnp.concatenate([far[0:3].reshape(96, 128), rotor], axis=0), "gx", 1)
     high = swap_next(far[3:6].reshape(96, 128), "gx")
-    (own,) = call(
+    own, acc = call(
         make_near_gather(count_y, 8, 4),
         "near_gather",
-        [((3, 4, 8, 128), F32, VMEM)],
-        [SMEM] + [VMEM] * 3,
-        (mine, table, src, weight),
+        [((3, 4, 8, 128), F32, VMEM), ((512, 512), F32, VMEM)],
+        [SMEM] + [VMEM] * 4,
+        (mine, table, src, weight, dst),
         [ints(48), ints(8)],
         flops=4 * 10**9,
     )
@@ -428,13 +432,14 @@
     first = swap(y_payload(0), "gy", 1)
     rotor = rotor + first[96:]
     second = swap_next(y_payload(2), "gy")
-    (acc,) = call(
+    three = pltpu.VMEM((3, 4, 8, 128), F32)
+    acc, edge = call(
         make_first_scatter(count_y),
         "first_scatter",
-        [((512, 512), F32, VMEM)],
-        [SMEM] + [VMEM] * 4,
-        (mine, low, own, high, dst),
-        [pltpu.VMEM((3, 4, 8, 128), F32), ints(48), ints(8)],
+        [((512, 512), F32, VMEM), ((144, 512), F32, VMEM)],
+        [SMEM] + [VMEM] * 5,
+        (mine, acc, low, high, first, dst),
+        [pltpu.VMEM((2, 4, 8, 128), F32), three, ints(48), ints(8)],
         flops=4 * 10**9,
     )
     rotor = rotor + second[96:]
@@ -449,12 +454,11 @@
         make_edge_scatter(count_y),
         "edge_scatter",
         [((3, 128, 128), F32, VMEM), face_x, face_x, face_y, face_y],
-        [SMEM] + [VMEM] * 5,
-        (mine, acc, first, second, dst, vel),
-        [pltpu.VMEM((144, 512), F32), lists, ints(72), ints(8)],
+        [SMEM] + [VMEM] * 4,
+        (mine, edge, second, dst, vel),
+        [pltpu.VMEM((144, 512), F32), three, ints(48), ints(8)],
         flops=4 * 10**9,
     )
-    rotor, xa, ya, yb = lax.optimization_barrier((rotor, xa, ya, yb))
     xb = swap_next(jnp.concatenate([xb.reshape(192, 128), rotor], axis=0), "gx")
     xa = swap(xa.reshape(192, 128), "gx", 1)
     ya = swap(ya, "gy", 1)

time: 43.3 us -> 40.6 us (0.938); the launches traced: 42.6 us -> 40.9 us
  starting transfers between devices: 9.81 us -> 17.8 us
  waiting for transfers between devices: 9.42 us -> 3.84 us
  Pallas kernels: 22.5 us -> 18.5 us
    ppermute x5, starting transfers between devices: 0.35 us -> 7.85 us  [swap(): return lax.ppermute(value, axis, [(i, i ^ step) for i in range(count)])]
    ppermute x5, waiting for transfers between devices: 6.63 us -> 0.91 us  [swap(): return lax.ppermute(value, axis, [(i, i ^ step) for i in range(count)])]
    pallas_call x6, Pallas kernels: 22.5 us -> 18.5 us  [call(): pl.pallas_call(kernel, out_shape=tuple((jax.ShapeDtypeStruct(shape, dtype...]
    ppermute x4, starting transfers between devices: 9.46 us -> 9.91 us  [swap_next(): lax.ppermute(value, axis, [(i, (i - 1 if i % 2 == 0 else i + 1) % count)...]
  transfers between devices with their start and end apart: 9 -> 9, of which waited for: 8 -> 3; matrix products, arithmetic and copies ran while one was open for 0% -> 0% of each run, Pallas kernels for 27% -> 25%
where the time goes in v8:
time: 40.6 us; the launch traced here: 40.9 us
  Pallas kernels  18.5 us (46%)
  starting transfers between devices  17.8 us (44%)
  waiting for transfers between devices  3.84 us (9%)
  between operations  0.77 us (2%)
    pallas_call x6, Pallas kernels, call(): pl.pallas_call(kernel, out_shape=tuple((jax.ShapeDtypeStruct(shape, dtype...  18.5 us
    ppermute x4, starting transfers between devices, swap_next(): lax.ppermute(value, axis, [(i, (i - 1 if i % 2 == 0 else i + 1) % count)...  9.91 us
    ppermute x5, starting transfers between devices, swap(): return lax.ppermute(value, axis, [(i, i ^ step) for i in range(count)])  7.85 us
    ppermute x4, waiting for transfers between devices, swap_next(): lax.ppermute(value, axis, [(i, (i - 1 if i % 2 == 0 else i + 1) % count)...  2.93 us
    ppermute x5, waiting for transfers between devices, swap(): return lax.ppermute(value, axis, [(i, i ^ step) for i in range(count)])  0.91 us
  transfers between devices with their start and end apart: 9, of which 3 were waited for; matrix products, arithmetic and copies ran while one was open for 0% of the time, Pallas kernels for 25%

profile of v8, /device:TPU:0, one launch (start us, length us, event | category | flops | bytes accessed | tf_op | source)
XLA Modules:
  0.0 40.9 jit_solution(13293837664027589686)
XLA Ops:
  0.6 5.7 %far_gather.1 = (f32[6,4,8,128]{3,2,1,0:T(8,128)S(1)}, bf16[3,256,512]{2,1,0:T(8,128)(2,1)S(1)}, f32[3,512,128]{2,1,0:T(8,128)S(1)}, s32[72,128]{1,0:T(8,128)S(1...) custom-call(s32[1]{0:T(128)} %bitcast.mine_ref, ...), custom_call_target="tpu_custom_call" | custom-call | flops 5000000000 | bytes 100000 | tf_op jit(solution)/shard_map/far_gather/pallas_call | solution.py:378
  6.4 3.7 %collective-permute-start = (f32[120,128]{1,0:T(8,128)S(1)}, f32[120,128]{1,0:T(8,128)S(1)}, u32[]{:S(2)}, u32[]{:S(2)}) collective-permute-start(f32[120,128]{1,0:T(8,128)S(1)} %pad_maximum_fusion.1), channel_id=1, source_target_pairs={{0,4},{4,0},{8,12},{12,8},{16,20},{20,16},{24,28},{28,24},{1,5},{5... | collective-permute-start | bytes 184328 | tf_op jit(solution)/shard_map/ppermute | solution.py:369
  10.1 3.7 %collective-permute-start.1 = (f32[96,128]{1,0:T(8,128)S(1)}, f32[96,128]{1,0:T(8,128)S(1)}, u32[]{:S(2)}, u32[]{:S(2)}) collective-permute-start(f32[96,128]{1,0:T(8,128)S(1)} %bitcast.17), channel_id=1, source_target_pairs={{0,28},{4,8},{8,4},{12,16},{16,12},{20,24},{24,20},{28,0},{1,29},{... | collective-permute-start | bytes 147464 | tf_op jit(solution)/shard_map/ppermute | solution.py:374
  13.8 1.7 %near_gather.1 = (f32[3,4,8,128]{3,2,1,0:T(8,128)S(1)}, f32[512,512]{1,0:T(8,128)S(1)}) custom-call(s32[1]{0:T(128)} %bitcast.mine_ref, bf16[3,256,512]{2,1,0:T(8,128)(2,1)S(1)} %get-tuple-element.24.table, s32[72,128]{1,0:T(8,128)S(1)} %get-tuple-element.25.src_ref, f32[72,128]{1,0:T(8,128)S(1)} %get-tuple-element.26.w_ref, ...), custom_call_target="tpu_custom_call" | custom-call | flops 4000000000 | bytes 100000 | tf_op jit(solution)/shard_map/near_gather/pallas_call | solution.py:378
  15.5 1.5 %collective-permute-done.1.high_ref = f32[96,128]{1,0:T(8,128)S(1)} collective-permute-done((f32[96,128]{1,0:T(8,128)S(1)}, f32[96,128]{1,0:T(8,128)S(1)}, u32[]{:S(2)}, u32[]{:S(2)}) %collective-permute-start.1) | collective-permute-done | bytes 49184 | tf_op jit(solution)/shard_map/ppermute | solution.py:374
  17.0 0.0 collective-permute-done.low_ref
  17.1 1.2 %collective-permute-start.2 = (f32[120,128]{1,0:T(8,128)S(1)}, f32[120,128]{1,0:T(8,128)S(1)}, u32[]{:S(2)}, u32[]{:S(2)}) collective-permute-start(f32[120,128]{1,0:T(8,128)S(1)} %pad_maximum_fusion.2), channel_id=1, source_target_pairs={{0,1},{1,0},{2,3},{3,2},{4,5},{5,4},{6,7},{7,6},{8,9},{9,8},{10,11... | collective-permute-start | bytes 184328 | tf_op jit(solution)/shard_map/ppermute | solution.py:369
  18.3 0.9 %collective-permute-done.2.first_ref = f32[120,128]{1,0:T(8,128)S(1)} collective-permute-done((f32[120,128]{1,0:T(8,128)S(1)}, f32[120,128]{1,0:T(8,128)S(1)}, u32[]{:S(2)}, u32[]{:S(2)}) %collective-permute-start.2) | collective-permute-done | bytes 61472 | tf_op jit(solution)/shard_map/ppermute | solution.py:369
  19.2 2.0 %collective-permute-start.3 = (f32[120,128]{1,0:T(8,128)S(1)}, f32[120,128]{1,0:T(8,128)S(1)}, u32[]{:S(2)}, u32[]{:S(2)}) collective-permute-start(f32[120,128]{1,0:T(8,128)S(1)} %pad_maximum_fusion.3), channel_id=1, source_target_pairs={{0,3},{1,2},{2,1},{3,0},{4,7},{5,6},{6,5},{7,4},{8,11},{9,10},{10,... | collective-permute-start | bytes 184328 | tf_op jit(solution)/shard_map/ppermute | solution.py:374
  21.2 3.5 %first_scatter.1 = (f32[512,512]{1,0:T(8,128)S(1)}, f32[144,512]{1,0:T(8,128)S(1)}) custom-call(s32[1]{0:T(128)} %bitcast.mine_ref, f32[512,512]{1,0:T(8,128)S(1)} %get-tuple-element.28.base_ref, f32[120,128]{1,0:T(8,128)S(1)} %collective-permute-done.low_ref, f32[96,128]{1,0:T(8,128)S(1)} %collective-permute-done.1.high_ref, ...), custom_call_target="tpu_custom_call" | custom-call | flops 4000000000 | bytes 100000 | tf_op jit(solution)/shard_map/first_scatter/pallas_call | solution.py:378
  24.7 0.0 collective-permute-done.3.second_ref
  24.7 0.1 collective-permute-start.4
  24.8 1.4 %edge_scatter.1 = (f32[3,128,128]{2,1,0:T(8,128)S(1)}, f32[3,64,128]{2,1,0:T(8,128)S(1)}, f32[3,64,128]{2,1,0:T(8,128)S(1)}, f32[3,8,128]{2,1,0:T(8,128)S(1)}, f32[3,8,128]{2,1,0:T(8,128)S(1)}) custom-call(s32[1]{0:T(128)} %bitcast.mine_ref, f32[144,512]{1,0:T(8,128)S(1)} %get-tuple-element.32.base_ref, f32[120,128]{1,0:T(8,128)S(1)} %collective-permute-done.3.second_ref, ...), custom_call_target="tpu_custom_call" | custom-call | flops 4000000000 | bytes 100000 | tf_op jit(solution)/shard_map/edge_scatter/pallas_call | solution.py:378
  26.2 2.8 %collective-permute-start.6 = (f32[192,128]{1,0:T(8,128)S(1)}, f32[192,128]{1,0:T(8,128)S(1)}, u32[]{:S(2)}, u32[]{:S(2)}) collective-permute-start(f32[192,128]{1,0:T(8,128)S(1)} %bitcast.15), channel_id=1, source_target_pairs={{0,4},{4,0},{8,12},{12,8},{16,20},{20,16},{24,28},{28,24},{1,5},{5... | collective-permute-start | bytes 294920 | tf_op jit(solution)/shard_map/ppermute | solution.py:369
  29.0 0.0 collective-permute-start.7
  29.0 1.3 %collective-permute-start.8 = (f32[3,8,128]{2,1,0:T(8,128)S(1)}, f32[3,8,128]{2,1,0:T(8,128)S(1)}, u32[]{:S(2)}, u32[]{:S(2)}) collective-permute-start(f32[3,8,128]{2,1,0:T(8,128)S(1)} %get-tuple-element.43), channel_id=1, source_target_pairs={{0,3},{1,2},{2,1},{3,0},{4,7},{5,6},{6,5},{7,4},{8,11},{9,10},{10,... | collective-permute-start | bytes 36872 | tf_op jit(solution)/shard_map/ppermute | solution.py:374
  30.3 0.0 collective-permute-done.4
  30.3 3.0 %collective-permute-start.5 = (f32[216,128]{1,0:T(8,128)S(1)}, f32[216,128]{1,0:T(8,128)S(1)}, u32[]{:S(2)}, u32[]{:S(2)}) collective-permute-start(f32[216,128]{1,0:T(8,128)S(1)} %pad_maximum_fusion), channel_id=1, source_target_pairs={{0,28},{4,8},{8,4},{12,16},{16,12},{20,24},{24,20},{28,0},{1,29},{... | collective-permute-start | bytes 331784 | tf_op jit(solution)/shard_map/ppermute | solution.py:374
  33.3 3.8 %inner_scatter.1.inner_ref = f32[3,384,128]{2,1,0:T(8,128)S(1)} custom-call(s32[1]{0:T(128)} %bitcast.mine_ref, f32[512,512]{1,0:T(8,128)S(1)} %get-tuple-element.35.base_ref, f32[120,128]{1,0:T(8,128)S(1)} %collective-permute-done.2.first_ref, f32[120,128]{1,0:T(8,128)S(1)} %collective-permute-done.3.second_ref, s32[72,128]{1,0:T(8,128)S(1)} %get-tuple-element.27.dst_ref, ...), custom_call_target="tpu_custom_call" | custom-call | flops 6000000000 | bytes 100000 | tf_op jit(solution)/shard_map/inner_scatter/pallas_call | solution.py:378
  37.1 1.4 %collective-permute-done.5.xb_ref = f32[216,128]{1,0:T(8,128)S(1)} collective-permute-done((f32[216,128]{1,0:T(8,128)S(1)}, f32[216,128]{1,0:T(8,128)S(1)}, u32[]{:S(2)}, u32[]{:S(2)}) %collective-permute-start.5) | collective-permute-done | bytes 110624 | tf_op jit(solution)/shard_map/ppermute | solution.py:374
  38.5 0.0 collective-permute-done.7.ya_ref
  38.5 0.0 collective-permute-done.8.yb_ref
  38.5 0.0 collective-permute-done.6.xa_ref
  38.5 2.4 %stencil.1 = (f32[3,8,64,128]{3,2,1,0:T(8,128)}, f32[3,512,128]{2,1,0:T(8,128)}) custom-call(s32[1]{0:T(128)} %bitcast.mine_ref, f32[3,128,128]{2,1,0:T(8,128)S(1)} %get-tuple-element.34.edge_ref, f32[3,384,128]{2,1,0:T(8,128)S(1)} %inner_scatter.1.inner_ref, s32[20,192]{1,0:T(8,128)S(1)} %get-tuple-element.36.tile_ref, ...), custom_call_target="tpu_custom_call" | custom-call | flops 1000000000 | bytes 100000 | tf_op jit(solution)/shard_map/stencil/pallas_call | solution.py:378
  (13 shorter events, 0.1 us)
Async XLA Ops:
  6.4 10.7 %collective-permute-start = (f32[120,128]{1,0:T(8,128)S(1)}, f32[120,128]{1,0:T(8,128)S(1)}, u32[]{:S(2)}, u32[]{:S(2)}) collective-permute-start(f32[120,128]{1,0:T(8,128)S(1)} %pad_maximum_fusion.1), channel_id=1, source_target_pairs={{0,4},{4,0},{8,12},{12,8},{16,20},{20,16},{24,28},{28,24},{1,5},{5... | collective-permute-start | bytes 184328 | tf_op jit(solution)/shard_map/ppermute | solution.py:369
  10.1 6.9 %collective-permute-start.1 = (f32[96,128]{1,0:T(8,128)S(1)}, f32[96,128]{1,0:T(8,128)S(1)}, u32[]{:S(2)}, u32[]{:S(2)}) collective-permute-start(f32[96,128]{1,0:T(8,128)S(1)} %bitcast.17), channel_id=1, source_target_pairs={{0,28},{4,8},{8,4},{12,16},{16,12},{20,24},{24,20},{28,0},{1,29},{... | collective-permute-start | bytes 147464 | tf_op jit(solution)/shard_map/ppermute | solution.py:374
  17.1 2.1 %collective-permute-start.2 = (f32[120,128]{1,0:T(8,128)S(1)}, f32[120,128]{1,0:T(8,128)S(1)}, u32[]{:S(2)}, u32[]{:S(2)}) collective-permute-start(f32[120,128]{1,0:T(8,128)S(1)} %pad_maximum_fusion.2), channel_id=1, source_target_pairs={{0,1},{1,0},{2,3},{3,2},{4,5},{5,4},{6,7},{7,6},{8,9},{9,8},{10,11... | collective-permute-start | bytes 184328 | tf_op jit(solution)/shard_map/ppermute | solution.py:369
  19.2 5.5 %collective-permute-start.3 = (f32[120,128]{1,0:T(8,128)S(1)}, f32[120,128]{1,0:T(8,128)S(1)}, u32[]{:S(2)}, u32[]{:S(2)}) collective-permute-start(f32[120,128]{1,0:T(8,128)S(1)} %pad_maximum_fusion.3), channel_id=1, source_target_pairs={{0,3},{1,2},{2,1},{3,0},{4,7},{5,6},{6,5},{7,4},{8,11},{9,10},{10,... | collective-permute-start | bytes 184328 | tf_op jit(solution)/shard_map/ppermute | solution.py:374
  24.7 5.5 %collective-permute-start.4 = (f32[24,128]{1,0:T(8,128)S(1)}, f32[24,128]{1,0:T(8,128)S(1)}, u32[]{:S(2)}, u32[]{:S(2)}) collective-permute-start(f32[24,128]{1,0:T(8,128)S(1)} %slice_add_fusion.1), channel_id=1, source_target_pairs={{0,16},{4,20},{8,24},{12,28},{16,0},{20,4},{24,8},{28,12},{1,17},{... | collective-permute-start | bytes 36872 | tf_op jit(solution)/shard_map/ppermute | solution.py:369
  26.2 12.3 %collective-permute-start.6 = (f32[192,128]{1,0:T(8,128)S(1)}, f32[192,128]{1,0:T(8,128)S(1)}, u32[]{:S(2)}, u32[]{:S(2)}) collective-permute-start(f32[192,128]{1,0:T(8,128)S(1)} %bitcast.15), channel_id=1, source_target_pairs={{0,4},{4,0},{8,12},{12,8},{16,20},{20,16},{24,28},{28,24},{1,5},{5... | collective-permute-start | bytes 294920 | tf_op jit(solution)/shard_map/ppermute | solution.py:369
  29.0 9.5 %collective-permute-start.7 = (f32[3,8,128]{2,1,0:T(8,128)S(1)}, f32[3,8,128]{2,1,0:T(8,128)S(1)}, u32[]{:S(2)}, u32[]{:S(2)}) collective-permute-start(f32[3,8,128]{2,1,0:T(8,128)S(1)} %get-tuple-element.42), channel_id=1, source_target_pairs={{0,1},{1,0},{2,3},{3,2},{4,5},{5,4},{6,7},{7,6},{8,9},{9,8},{10,11... | collective-permute-start | bytes 36872 | tf_op jit(solution)/shard_map/ppermute | solution.py:369
  29.0 9.5 %collective-permute-start.8 = (f32[3,8,128]{2,1,0:T(8,128)S(1)}, f32[3,8,128]{2,1,0:T(8,128)S(1)}, u32[]{:S(2)}, u32[]{:S(2)}) collective-permute-start(f32[3,8,128]{2,1,0:T(8,128)S(1)} %get-tuple-element.43), channel_id=1, source_target_pairs={{0,3},{1,2},{2,1},{3,0},{4,7},{5,6},{6,5},{7,4},{8,11},{9,10},{10,... | collective-permute-start | bytes 36872 | tf_op jit(solution)/shard_map/ppermute | solution.py:374
  30.3 8.2 %collective-permute-start.5 = (f32[216,128]{1,0:T(8,128)S(1)}, f32[216,128]{1,0:T(8,128)S(1)}, u32[]{:S(2)}, u32[]{:S(2)}) collective-permute-start(f32[216,128]{1,0:T(8,128)S(1)} %pad_maximum_fusion), channel_id=1, source_target_pairs={{0,28},{4,8},{8,4},{12,16},{16,12},{20,24},{24,20},{28,0},{1,29},{... | collective-permute-start | bytes 331784 | tf_op jit(solution)/shard_map/ppermute | solution.py:374
